TPU v7x, 32 devices: a whole 2x2x4 slice. The times are simulated.
32 devices in a mesh: shard: 2 (over x), ctx: 4 (over z), tp: 4 (over y, core).
Axes of the slice: x: 2, y: 2, z: 4, core: 2. Of those that a mesh axis runs over, the one named last changes fastest.
Arguments:
- hidden_in: bfloat16 [8, 1024, 768], P('shard', 'ctx'), may hold values from -6 to 6
- token_type: int32 [8, 1024], P('shard', 'ctx'), may hold values 0 or 1
- segment: int32 [8, 1024], P('shard', 'ctx'), may hold values from 0 to 17, as said below
- query_weight: bfloat16 [4, 768, 768], P(None, 'shard', 'tp'), may hold values from -0.21875 to 0.21875
- key_value_weight: bfloat16 [2, 768, 768], P(None, 'shard', 'tp'), may hold values from -0.21875 to 0.21875
- query_bias: float32 [4, 768], P(None, 'tp'), may hold values from -1.75 to 1.75
- value_bias: float32 [768], P('tp'), may hold values from -1.75 to 1.75
- out_weight: bfloat16 [768, 768], P('tp', 'shard'), may hold values from -1.75 to 1.75
- out_bias: float32 [768], replicated, may hold values from -1.75 to 1.75
- norm1_gain: float32 [768], replicated, may hold values from 0.5 to 1.5
- norm1_bias: float32 [768], replicated, may hold values from -1.75 to 1.75
- up_weight: bfloat16 [768, 3072], P('shard', 'tp'), may hold values from -0.21875 to 0.21875
- up_bias: float32 [3072], P('tp'), may hold values from -1.75 to 1.75
- down_weight: bfloat16 [3072, 768], P('tp', 'shard'), may hold values from -0.109375 to 0.109375
- down_bias: float32 [768], replicated, may hold values from -1.75 to 1.75
- norm2_gain: float32 [768], replicated, may hold values from 0.5 to 1.5
- norm2_bias: float32 [768], replicated, may hold values from -1.75 to 1.75
- out_grad: bfloat16 [8, 1024, 768], P('shard', 'ctx'), may hold values from -6 to 6
Outputs:
- hidden_out: bfloat16 [8, 1024, 768], P('shard', 'ctx')
- in_grad: float32 [8, 1024, 768], P('shard', 'ctx')
- query_weight_grad: float32 [4, 768, 768], P(None, 'shard', 'tp')
- key_value_weight_grad: float32 [2, 768, 768], P(None, 'shard', 'tp')
- query_bias_grad: float32 [4, 768], P(None, 'tp')
- value_bias_grad: float32 [768], P('tp')
- out_weight_grad: float32 [768, 768], P('tp', 'shard')
- out_bias_grad: float32 [768], replicated
- norm1_gain_grad: float32 [768], replicated
- norm1_bias_grad: float32 [768], replicated
- up_weight_grad: float32 [768, 3072], P('shard', 'tp')
- up_bias_grad: float32 [3072], P('tp')
- down_weight_grad: float32 [3072, 768], P('tp', 'shard')
- down_bias_grad: float32 [768], replicated
- norm2_gain_grad: float32 [768], replicated
- norm2_bias_grad: float32 [768], replicated
Inputs may be any that keep to these rules, and one draw needn't show every extreme that they name: `token_type`: 0 marks a word, 1 an entity. `segment`: within each sequence the documents are numbered 1, 2, 3 in order, each holds 60 to 800 consecutive positions, and the positions after the last document are 0.
All inputs are finite; a program needn't handle non-finite values. No bound on the sum of `token_type` on one device may be relied on, other than what follows from the above.
Results may differ from a plain program's by a relative error of at most 0.02.
Values may be sent and summed in bfloat16 or wider, within the bound.
A program may use at most 128 MiB of HBM per device.

v0:
```python
import jax
import jax.numpy as jnp
from jax import lax
from jax.sharding import PartitionSpec as P

HEAD = 64
FF = 3072


eps_norm = 1e-05
big_neg = -1e30
root_half = 0.7071067811865476
inv_root_two_pi = 0.3989422804014327


def norm_forward(values, gain_vec, bias_vec):
    average = jnp.mean(values, axis=-1, keepdims=True)
    centred = values - average
    variance = jnp.mean(centred * centred, axis=-1, keepdims=True)
    inv_spread = lax.rsqrt(variance + eps_norm)
    normed = centred * inv_spread
    return (normed * gain_vec + bias_vec, normed, inv_spread)


def norm_backward(upstream, normed, inv_spread, gain_vec):
    scaled = upstream * gain_vec
    mean_first = jnp.mean(scaled, axis=-1, keepdims=True)
    second = jnp.mean(scaled * normed, axis=-1, keepdims=True)
    return inv_spread * (scaled - mean_first - normed * second)


def head_scores(queries, key_block, key_word):
    toward_word = jnp.einsum(
        "sqc,skc->sqk", queries[0], key_block, preferred_element_type=jnp.float32
    )
    toward_entity = jnp.einsum(
        "sqc,skc->sqk", queries[1], key_block, preferred_element_type=jnp.float32
    )
    return jnp.where(key_word, toward_word, toward_entity) * HEAD ** (-0.5)


def widen_cols(vector, full_width, offset):
    blank = jnp.zeros(vector.shape[:-1] + (full_width,), jnp.float32)
    return lax.dynamic_update_slice_in_dim(blank, vector, offset, vector.ndim - 1)


def per_device(
    hidden_in,
    token_type,
    segment,
    query_weight,
    key_value_weight,
    query_bias,
    value_bias,
    out_weight,
    out_bias,
    norm1_gain,
    norm1_bias,
    up_weight,
    up_bias,
    down_weight,
    down_bias,
    norm2_gain,
    norm2_bias,
    out_grad,
):
    seq_count, local_len, model_width = hidden_in.shape
    row_count = seq_count * local_len
    tensor_count = lax.axis_size("tp")
    tensor_rank = lax.axis_index("tp")
    share_rows = row_count // tensor_count
    share_start = tensor_rank * share_rows

    def own_rows(values):
        return lax.dynamic_slice_in_dim(values, share_start, share_rows, 0)

    weights_query, weights_keyval, weights_out, weights_up, weights_down = (
        lax.all_gather(query_weight, "shard", axis=1, tiled=True),
        lax.all_gather(key_value_weight, "shard", axis=1, tiled=True),
        lax.all_gather(out_weight, "shard", axis=1, tiled=True),
        lax.all_gather(up_weight, "shard", axis=0, tiled=True),
        lax.all_gather(down_weight, "shard", axis=1, tiled=True),
    )
    part_width = weights_query.shape[2]
    feed_width = weights_up.shape[1]
    heads_here = part_width // HEAD
    row_data = hidden_in.reshape(row_count, model_width)
    is_word = (token_type.reshape(row_count) == 0)[:, None]
    query_four = (
        jnp.einsum("rd,kde->kre", row_data, weights_query, preferred_element_type=jnp.float32)
        + query_bias[:, None, :]
    )
    chosen = jnp.stack(
        [
            jnp.where(is_word, query_four[0], query_four[2]),
            jnp.where(is_word, query_four[1], query_four[3]),
        ]
    ).astype(jnp.bfloat16)
    key_values = jnp.einsum(
        "rd,kde->kre", row_data, weights_keyval, preferred_element_type=jnp.float32
    )
    key_values = (
        key_values + jnp.stack([jnp.zeros_like(value_bias), value_bias])[:, None, :]
    ).astype(jnp.bfloat16)

    def by_head(values):
        return values.reshape(2, seq_count, local_len, heads_here, HEAD).transpose(3, 0, 1, 2, 4)

    def by_rows(values):
        return values.transpose(1, 2, 3, 0, 4).reshape(2, row_count, part_width)

    query_heads = by_head(chosen)
    keys_all = lax.all_gather(by_head(key_values), "ctx", axis=3, tiled=True)
    types_all, segments_all = (
        lax.all_gather(token_type, "ctx", axis=1, tiled=True),
        lax.all_gather(segment, "ctx", axis=1, tiled=True),
    )
    key_word = (types_all == 0)[:, None, :]
    allowed = (segment[:, :, None] == segments_all[:, None, :]) & (segments_all[:, None, :] > 0)

    def attend_head(pieces):
        queries, key_value = pieces
        scores = head_scores(queries, key_value[0], key_word)
        row_max = jnp.max(jnp.where(allowed, scores, big_neg), axis=-1, keepdims=True)
        exponent = jnp.exp(jnp.where(allowed, scores - row_max, big_neg))
        denominator = jnp.maximum(jnp.sum(exponent, axis=-1, keepdims=True), 1.0)
        probability = (exponent / denominator).astype(jnp.bfloat16)
        context = jnp.einsum(
            "sqk,skc->sqc", probability, key_value[1], preferred_element_type=jnp.float32
        )
        return (context.astype(jnp.bfloat16), row_max, denominator)

    context_heads, row_maxima, denominators = lax.map(attend_head, (query_heads, keys_all))
    context = context_heads.transpose(1, 2, 0, 3).reshape(row_count, part_width)
    attn_terms = jnp.dot(context, weights_out, preferred_element_type=jnp.float32)
    grad_output = out_grad.reshape(row_count, model_width).astype(jnp.float32)
    attention = lax.psum(attn_terms.astype(jnp.bfloat16), "tp").astype(jnp.float32) + out_bias
    first_out, first_hat, first_inv = norm_forward(
        row_data.astype(jnp.float32) + attention, norm1_gain, norm1_bias
    )
    first_low = first_out.astype(jnp.bfloat16)
    up_value = jnp.dot(first_low, weights_up, preferred_element_type=jnp.float32) + up_bias
    normal_cdf = 0.5 * (1.0 + lax.erf(up_value * root_half))
    active = jax.nn.gelu(up_value, approximate=False).astype(jnp.bfloat16)
    up_value, normal_cdf, active, down_terms = (
        up_value,
        normal_cdf,
        active,
        jnp.dot(active, weights_down, preferred_element_type=jnp.float32),
    )
    feed_out = lax.psum(down_terms.astype(jnp.bfloat16), "tp").astype(jnp.float32) + down_bias
    final_out, second_hat, second_inv = norm_forward(first_out + feed_out, norm2_gain, norm2_bias)
    hidden_out = final_out.astype(jnp.bfloat16).reshape(seq_count, local_len, model_width)
    grad_second = norm_backward(grad_output, second_hat, second_inv, norm2_gain)
    grad_feed = grad_second.astype(jnp.bfloat16)
    grad_down = jnp.dot(active.T, grad_feed, preferred_element_type=jnp.float32)
    grad_active = jnp.dot(grad_feed, weights_down.T, preferred_element_type=jnp.float32)
    gelu_slope = normal_cdf + up_value * jnp.exp(-0.5 * up_value * up_value) * inv_root_two_pi
    grad_up = (grad_active * gelu_slope).astype(jnp.bfloat16)
    grad_upw = jnp.dot(first_low.T, grad_up, preferred_element_type=jnp.float32)
    up_terms = jnp.dot(grad_up, weights_up.T, preferred_element_type=jnp.float32)
    grad_down, grad_up, grad_upw, up_terms = (grad_down, grad_up, grad_upw, up_terms)
    grad_first = grad_second + lax.psum(up_terms.astype(jnp.bfloat16), "tp").astype(jnp.float32)
    grad_first_in = norm_backward(grad_first, first_hat, first_inv, norm1_gain)
    grad_attention = grad_first_in.astype(jnp.bfloat16)
    first_hat_own, grad_first_own = (own_rows(first_hat), own_rows(grad_first))
    second_hat_own, grad_output_own = (own_rows(second_hat), own_rows(grad_output))
    grad_attn_own, grad_feed_own = (own_rows(grad_attention), own_rows(grad_feed))
    grad_outw = jnp.dot(context.T, grad_attention, preferred_element_type=jnp.float32)
    grad_context = jnp.dot(
        grad_attention, weights_out.T, preferred_element_type=jnp.float32
    ).astype(jnp.bfloat16)
    grad_context_heads = grad_context.reshape(seq_count, local_len, heads_here, HEAD).transpose(
        2, 0, 1, 3
    )

    def attend_back(pieces):
        queries, key_value, grad_ctx_head, row_max, denominator = pieces
        scores = head_scores(queries, key_value[0], key_word)
        probability = jnp.exp(jnp.where(allowed, scores - row_max, big_neg)) / denominator
        grad_weights = jnp.einsum(
            "sqc,skc->sqk", grad_ctx_head, key_value[1], preferred_element_type=jnp.float32
        )
        row_dot = jnp.sum(probability * grad_weights, axis=-1, keepdims=True)
        grad_scores = (probability * (grad_weights - row_dot)).astype(jnp.bfloat16) * jnp.bfloat16(
            HEAD ** (-0.5)
        )
        zero_block = jnp.zeros_like(grad_scores)
        grad_word = jnp.where(key_word, grad_scores, zero_block)
        grad_entity = jnp.where(key_word, zero_block, grad_scores)
        grad_queries = jnp.stack(
            [
                jnp.einsum(
                    "sqk,skc->sqc", grad_word, key_value[0], preferred_element_type=jnp.float32
                ),
                jnp.einsum(
                    "sqk,skc->sqc", grad_entity, key_value[0], preferred_element_type=jnp.float32
                ),
            ]
        )
        grad_keys = jnp.einsum(
            "sqk,sqc->skc", grad_word, queries[0], preferred_element_type=jnp.float32
        )
        grad_keys = grad_keys + jnp.einsum(
            "sqk,sqc->skc", grad_entity, queries[1], preferred_element_type=jnp.float32
        )
        grad_values = jnp.einsum(
            "sqk,sqc->skc",
            probability.astype(jnp.bfloat16),
            grad_ctx_head,
            preferred_element_type=jnp.float32,
        )
        return (grad_queries, jnp.stack([grad_keys, grad_values]))

    grad_query_heads, grad_kv_heads = lax.map(
        attend_back, (query_heads, keys_all, grad_context_heads, row_maxima, denominators)
    )
    grad_kv_mine = lax.psum_scatter(
        grad_kv_heads.astype(jnp.bfloat16), "ctx", scatter_dimension=3, tiled=True
    ).astype(jnp.float32)
    grad_keyval = by_rows(grad_kv_mine).astype(jnp.bfloat16)
    grad_chosen = by_rows(grad_query_heads).astype(jnp.bfloat16)
    zero_rows = jnp.zeros_like(grad_chosen[0])
    grad_query_four = jnp.stack(
        [
            jnp.where(is_word, grad_chosen[0], zero_rows),
            jnp.where(is_word, grad_chosen[1], zero_rows),
            jnp.where(is_word, zero_rows, grad_chosen[0]),
            jnp.where(is_word, zero_rows, grad_chosen[1]),
        ]
    )
    grad_queryw = jnp.einsum(
        "rd,kre->kde", row_data, grad_query_four, preferred_element_type=jnp.float32
    )
    grad_keyvalw = jnp.einsum(
        "rd,kre->kde", row_data, grad_keyval, preferred_element_type=jnp.float32
    )
    back_input = jnp.einsum(
        "kre,kde->rd", grad_query_four, weights_query, preferred_element_type=jnp.float32
    )
    back_input = back_input + jnp.einsum(
        "kre,kde->rd", grad_keyval, weights_keyval, preferred_element_type=jnp.float32
    )
    in_grad = (
        grad_first_in + lax.psum(back_input.astype(jnp.bfloat16), "tp").astype(jnp.float32)
    ).reshape(seq_count, local_len, model_width)
    column_at = tensor_rank * part_width
    feed_at = tensor_rank * feed_width
    small_grads = lax.psum(
        (
            jnp.sum(grad_first_own * first_hat_own, axis=0),
            jnp.sum(grad_first_own, axis=0),
            jnp.sum(grad_output_own * second_hat_own, axis=0),
            jnp.sum(grad_output_own, axis=0),
            jnp.sum(grad_attn_own, axis=0, dtype=jnp.float32),
            jnp.sum(grad_feed_own, axis=0, dtype=jnp.float32),
            widen_cols(jnp.sum(grad_query_four, axis=1, dtype=jnp.float32), model_width, column_at),
            widen_cols(jnp.sum(grad_keyval[1], axis=0, dtype=jnp.float32), model_width, column_at),
            widen_cols(jnp.sum(grad_up, axis=0, dtype=jnp.float32), FF, feed_at),
        ),
        ("shard", "ctx", "tp"),
    )
    (
        gain_one_grad,
        shift_one_grad,
        gain_two_grad,
        shift_two_grad,
        out_shift_grad,
        down_shift_grad,
        query_full,
        value_full,
        up_full,
    ) = small_grads
    query_shift_grad = lax.dynamic_slice_in_dim(query_full, column_at, part_width, 1)
    value_shift_grad = lax.dynamic_slice_in_dim(value_full, column_at, part_width, 0)
    up_shift_grad = lax.dynamic_slice_in_dim(up_full, feed_at, feed_width, 0)
    weight_grads = (grad_queryw, grad_keyvalw, grad_outw, grad_upw, grad_down)
    summed = (
        lax.psum(weight_grads[0].astype(jnp.bfloat16), "ctx").astype(jnp.float32),
        lax.psum(weight_grads[1].astype(jnp.bfloat16), "ctx").astype(jnp.float32),
        lax.psum(weight_grads[2].astype(jnp.bfloat16), "ctx").astype(jnp.float32),
        lax.psum(weight_grads[3].astype(jnp.bfloat16), "ctx").astype(jnp.float32),
        lax.psum(weight_grads[4].astype(jnp.bfloat16), "ctx").astype(jnp.float32),
    )
    my_grads = (
        lax.psum_scatter(
            summed[0].astype(jnp.bfloat16), "shard", scatter_dimension=1, tiled=True
        ).astype(jnp.float32),
        lax.psum_scatter(
            summed[1].astype(jnp.bfloat16), "shard", scatter_dimension=1, tiled=True
        ).astype(jnp.float32),
        lax.psum_scatter(
            summed[2].astype(jnp.bfloat16), "shard", scatter_dimension=1, tiled=True
        ).astype(jnp.float32),
        lax.psum_scatter(
            summed[3].astype(jnp.bfloat16), "shard", scatter_dimension=0, tiled=True
        ).astype(jnp.float32),
        lax.psum_scatter(
            summed[4].astype(jnp.bfloat16), "shard", scatter_dimension=1, tiled=True
        ).astype(jnp.float32),
    )
    return (
        hidden_out,
        in_grad,
        my_grads[0],
        my_grads[1],
        query_shift_grad,
        value_shift_grad,
        my_grads[2],
        out_shift_grad,
        gain_one_grad,
        shift_one_grad,
        my_grads[3],
        up_shift_grad,
        my_grads[4],
        down_shift_grad,
        gain_two_grad,
        shift_two_grad,
    )


def solution(mesh):
    in_specs = (
        P("shard", "ctx", None),
        P("shard", "ctx"),
        P("shard", "ctx"),
        P(None, "shard", "tp"),
        P(None, "shard", "tp"),
        P(None, "tp"),
        P("tp"),
        P("tp", "shard"),
        P(),
        P(),
        P(),
        P("shard", "tp"),
        P("tp"),
        P("tp", "shard"),
        P(),
        P(),
        P(),
        P("shard", "ctx", None),
    )
    out_specs = (
        P("shard", "ctx", None),
        P("shard", "ctx", None),
        P(None, "shard", "tp"),
        P(None, "shard", "tp"),
        P(None, "tp"),
        P("tp"),
        P("tp", "shard"),
        P(),
        P(),
        P(),
        P("shard", "tp"),
        P("tp"),
        P("tp", "shard"),
        P(),
        P(),
        P(),
    )
    return jax.shard_map(
        per_device, mesh=mesh, in_specs=in_specs, out_specs=out_specs, check_vma=False
    )
```

profile of v0, /device:TPU:0, one launch (start us, length us, event | category | flops | bytes accessed | tf_op | source)
XLA Modules:
  0.0 815.7 jit_solution(1495779303078105990)
XLA Ops:
  8.6 10.9 %all_gather.26 = bf16[2,768,192]{1,2,0:T(8,128)(2,1)S(1)} all-gather(bf16[2,384,192]{1,2,0:T(8,128)(2,1)} %param.26), channel_id=1, replica_groups=mesh['shard'=2,'ctx'=4,'tp'=4] {'shard'}, dimensions={1}, use_global_device_ids=true | all-gather | bytes 884736 | tf_op jit(solution)/shard_map/all_gather | solution.py:79
  24.4 13.6 %all_gather.24 = s32[4,1024]{1,0:T(4,128)S(1)} all-gather(s32[4,256]{1,0:T(4,128)S(1)} %copy-done.43), channel_id=1, replica_groups=mesh['shard'=2,'ctx'=4,'tp'=4] {'ctx'}, dimensions={1}, use_global_device_ids=true | all-gather | bytes 20480 | tf_op jit(solution)/shard_map/all_gather | solution.py:115
  38.1 13.3 %all_gather.28 = s32[4,1024]{1,0:T(4,128)S(1)} all-gather(s32[4,256]{1,0:T(4,128)S(1)} %copy-done.22), channel_id=1, replica_groups=mesh['shard'=2,'ctx'=4,'tp'=4] {'ctx'}, dimensions={1}, use_global_device_ids=true | all-gather | bytes 20480 | tf_op jit(solution)/shard_map/all_gather | solution.py:116
  51.3 5.9 all_gather.29
  58.4 2.7 add_bitcast_fusion
  64.9 35.8 %all-gather.7.cloned.1.call-done = bf16[3,2,4,1024,64]{3,4,2,1,0:T(8,128)(2,1)} async-done(((bf16[3,2,4,256,64]{3,4,2,1,0:T(8,128)(2,1)}), bf16[3,2,4,1024,64]{3,4,2,1,0:T(8,128)(2,1)}) %all-gather.7.cloned.1.call-update) | async-done | bytes 3145744 | tf_op jit(solution)/shard_map/all_gather | solution.py:113
  100.7 30.9 %while.28 = (s32[]{:T(128)}, bf16[3,4,256,64]{2,3,1,0:T(8,128)(2,1)}, f32[3,4,256,1]{2,1,3,0:T(4,128)}, f32[3,4,256,1]{2,1,3,0:T(4,128)}, pred[4,1,1024]{2,0,1:T...) while((s32[]{:T(128)}, ...), condition=%wide.region_3.4_spmd.clone, body=%wide.region_0.3_spmd.clone.sunk | while | flops 420544512 | bytes 23113960 | solution.py:133
  102.5 2.8 select_reduce_fusion.2
  107.1 3.3 fusion.170
  112.8 2.8 select_reduce_fusion.2
  117.4 3.3 fusion.170
  123.1 2.8 select_reduce_fusion.2
  127.6 3.3 fusion.170
  136.7 39.5 %all-reduce.9.cloned.1.call-done = bf16[1024,768]{1,0:T(8,128)(2,1)} async-done(((bf16[1024,768]{1,0:T(8,128)(2,1)}), bf16[1024,768]{1,0:T(8,128)(2,1)}) %all-reduce.9.cloned.1.call-update) | async-done | bytes 1572880 | tf_op jit(solution)/shard_map/psum | solution.py:137
  181.4 19.1 %all-gather.9.cloned.1.call-done = bf16[768,768]{1,0:T(8,128)(2,1)} async-done(((bf16[384,768]{1,0:T(8,128)(2,1)}), bf16[768,768]{1,0:T(8,128)(2,1)}) %all-gather.9.cloned.1.call-update) | async-done | bytes 1179664 | tf_op jit(solution)/shard_map/all_gather | solution.py:81
  200.5 10.3 %fusion.93 = (bf16[1024,768]{1,0:T(8,128)(2,1)}, f32[1024,768]{1,0:T(8,128)}) fusion(f32[768]{0:T(1024)S(1)} %copy-done.50, bf16[768,768]{1,0:T(8,128)(2,1)} %all-gather.9.cloned.1.call-done, f32[1024,768]{1,0:T(8,128)S(1)} %subtract_multiply_fusion.3, f32[768]{0:T(1024)S(1)} %copy-done.36, f32[768]{0:T(1024)S(1)} %copy-done.29), kind=kOutput, calls=%fused_computation.90 | convolution fusion | flops 1262223360 | bytes 9053184 | tf_op jit(solution)/shard_map/dot_general | solution.py:142
  210.7 13.9 %all-gather.11.cloned.1.call-done = bf16[768,768]{1,0:T(8,128)(2,1)} async-done(((bf16[768,384]{1,0:T(8,128)(2,1)}), bf16[768,768]{1,0:T(8,128)(2,1)}) %all-gather.11.cloned.1.call-update) | async-done | bytes 1179664 | tf_op jit(solution)/shard_map/all_gather | solution.py:82
  224.6 4.3 convolution_convert_fusion.1
  230.8 41.2 %all-reduce.11.cloned.1.call-done = bf16[1024,768]{1,0:T(8,128)(2,1)} async-done(((bf16[1024,768]{1,0:T(8,128)(2,1)}), bf16[1024,768]{1,0:T(8,128)(2,1)}) %all-reduce.11.cloned.1.call-update) | async-done | bytes 1572880 | tf_op jit(solution)/shard_map/psum | solution.py:151
  281.3 3.4 convert_reduce_fusion
  288.7 42.8 %all-reduce.13.cloned.1.call-done = bf16[1024,768]{1,0:T(8,128)(2,1)} async-done(((bf16[1024,768]{1,0:T(8,128)(2,1)}), bf16[1024,768]{1,0:T(8,128)(2,1)}) %all-reduce.13.cloned.1.call-update) | async-done | bytes 1572880 | tf_op jit(solution)/shard_map/psum | solution.py:163
  331.6 4.8 multiply_reduce_fusion.6
  343.8 150.3 %while.29 = (s32[]{:T(128)}, bf16[3,2,4,256,64]{3,4,2,1,0:T(8,128)(2,1)}, bf16[3,2,4,1024,64]{3,4,2,1,0:T(8,128)(2,1)}, pred[4,1,1024]{2,0,1:T(4,128)(4,1)}, bf1...) while((s32[]{:T(128)}, ...), condition=%wide.region_17.18_spmd.clone, body=%wide.region_15.17_spmd.clone.sunk | while | flops 1123033088 | bytes 97640736 | solution.py:215
  344.5 3.8 fusion.179
  350.2 5.1 exponential_divide_fusion.2
  355.2 7.7 fusion.181
  362.9 7.7 fusion.180
  372.3 3.5 fusion.183
  375.8 7.9 fusion.184
  383.7 8.0 fusion.185
  394.6 3.8 fusion.179
  400.3 5.0 exponential_divide_fusion.2
  405.3 7.7 fusion.181
  413.0 7.7 fusion.180
  422.4 3.5 fusion.183
  425.9 7.9 fusion.184
  433.8 8.0 fusion.185
  444.7 3.8 fusion.179
  450.4 5.0 exponential_divide_fusion.2
  455.4 7.7 fusion.181
  463.1 7.7 fusion.180
  472.5 3.5 fusion.183
  476.0 7.9 fusion.184
  483.9 8.0 fusion.185
  499.8 4.7 convolution_convert_fusion.3
  514.8 3.8 fusion.110
  518.6 3.6 copy.56
  522.2 4.0 reshape.227
  526.3 28.4 %reduce-scatter.15.cloned.1.call-done = bf16[3,2,4,256,64]{3,4,2,1,0:T(8,128)(2,1)} async-done(((bf16[3,2,4,1024,64]{3,4,2,1,0:T(8,128)(2,1)}), bf16[3,2,4,256,64]{3,4,2,1,0:T(8,128)(2,1)}) %reduce-scatter.15.cloned.1.call-update) | async-done | bytes 786448 | tf_op jit(solution)/shard_map/reduce_scatter | solution.py:218
  554.7 2.6 copy.55
  559.9 3.3 fusion.112
  563.1 3.0 copy.58
  566.1 3.0 reshape.229
  569.2 3.9 convolution_convert_fusion.4
  573.5 3.2 fusion.120
  580.7 13.9 %reduce-scatter.25.cloned.1.call-done = bf16[384,768]{1,0:T(8,128)(2,1)} async-done(((bf16[768,768]{1,0:T(8,128)(2,1)}), bf16[384,768]{1,0:T(8,128)(2,1)}) %reduce-scatter.25.cloned.1.call-update) | async-done | bytes 589840
  596.7 22.6 %reduce-scatter.19.cloned.1.call-done = bf16[384,768]{1,0:T(8,128)(2,1)} async-done(((bf16[768,768]{1,0:T(8,128)(2,1)}), bf16[384,768]{1,0:T(8,128)(2,1)}) %reduce-scatter.19.cloned.1.call-update) | async-done | bytes 589840
  619.3 2.9 reshape.228
  624.4 12.5 %reduce-scatter.21.cloned.1.call-done = bf16[384,384]{1,0:T(8,128)(2,1)} async-done(((bf16[768,384]{1,0:T(8,128)(2,1)}), bf16[384,384]{1,0:T(8,128)(2,1)}) %reduce-scatter.21.cloned.1.call-update) | async-done | bytes 294928
  639.3 22.2 %reduce-scatter.17.cloned.1.call-done = bf16[384,768]{1,0:T(8,128)(2,1)} async-done(((bf16[768,768]{1,0:T(8,128)(2,1)}), bf16[384,768]{1,0:T(8,128)(2,1)}) %reduce-scatter.17.cloned.1.call-update) | async-done | bytes 589840 | tf_op jit(solution)/shard_map/reduce_scatter | solution.py:295
  661.6 3.4 bitcast_convert_fusion
  675.9 41.3 %all-reduce.1 = (f32[4,768]{1,0:T(4,128)S(1)}, f32[768]{0:T(1024)S(1)}, f32[768]{0:T(1024)}, f32[768]{0:T(1024)}, f32[768]{0:T(1024)}, /*index=5*/f32[3072]{0:T(...) all-reduce(f32[4,768]{1,0:T(4,128)S(1)} %dynamic_update_slice.28, ...), channel_id=1, replica_groups=mesh['shard'=2,'ctx'=4,'tp'=4] {'shard','ctx','tp'}, use_global_device_ids=true, to_apply=%region_25.26 | all-reduce | flops 11520 | bytes 92160 | tf_op jit(solution)/shard_map/psum | solution.py:249
  719.1 4.1 convert_add_fusion
  723.2 77.6 %all-reduce.17.cloned.1.call-done = (bf16[4,384,192]{1,2,0:T(8,128)(2,1)}, bf16[2,384,192]{1,2,0:T(8,128)(2,1)}, bf16[192,384]{1,0:T(8,128)(2,1)}, bf16[384,768]{1,0:T(8,128)(2,1)}, bf16[768,384]{1,0:T(8,128)(2,1)}) async-done(((bf16[4,384,192]{1,2,0:T(8,128)(2,1)}, bf16[2,384,192]{1,2,0:T(8,128)(2,1)}, bf16[192,384]{1,0:T(8,128)(2,1)}, bf16[384,768]{1,0:T(8,128)(2,1)}, bf16[768,384]{1,0:T(8,128)(2,1)}), ...) | async-done | bytes 2211856 | tf_op jit(solution)/shard_map/psum | solution.py:279
  (266 shorter events, 126.2 us)
Async XLA Ops:
  7.2 51.3 %all-gather.5.cloned.1.call-start = ((), (), s32[]{:S(2)}) async-start(), calls=%async_computation.6 | async-start | bytes 1769472 | tf_op jit(solution)/shard_map/all_gather | solution.py:78
  7.9 92.7 %all-gather.7.cloned.1.call-start = ((), (), s32[]{:S(2)}) async-start(), calls=%async_computation.7 | async-start | bytes 3932160 | tf_op jit(solution)/shard_map/all_gather | solution.py:113
  20.4 4.0 copy-start.43
  20.4 17.7 %copy-start.22 = (s32[4,256]{1,0:T(4,128)S(1)}, s32[4,256]{1,0:T(4,128)}, u32[]{:S(2)}) copy-start(s32[4,256]{1,0:T(4,128)} %param.24) | copy-start | bytes 12292
  20.4 31.0 %copy-start.31 = (bf16[192,384]{1,0:T(8,128)(2,1)S(1)}, bf16[192,384]{1,0:T(8,128)(2,1)}, u32[]{:S(2)}) copy-start(bf16[192,384]{1,0:T(8,128)(2,1)} %param.29) | copy-start | bytes 442372
  22.7 35.8 %copy-start.3 = (bf16[4,256,768]{2,1,0:T(8,128)(2,1)S(1)}, bf16[4,256,768]{2,1,0:T(8,128)(2,1)}, u32[]{:S(2)}) copy-start(bf16[4,256,768]{2,1,0:T(8,128)(2,1)} %param.22) | copy-start | bytes 4718596
  22.7 35.8 %copy-start.49 = (f32[4,192]{1,0:T(4,128)S(1)}, f32[4,192]{1,0:T(4,128)}, u32[]{:S(2)}) copy-start(f32[4,192]{1,0:T(4,128)} %param.27) | copy-start | bytes 9220
  24.3 151.9 %all-reduce.9.cloned.1.call-start = ((), (), s32[]{:S(2)}) async-start(), calls=%async_computation.8 | async-start | bytes 3145728 | tf_op jit(solution)/shard_map/psum | solution.py:137
  24.4 36.7 %copy-start.44 = (pred[1024]{0:T(1024)(128)(4,1)}, pred[1024]{0:T(1024)(128)(4,1)S(1)}, u32[]{:S(2)}) copy-start(pred[1024]{0:T(1024)(128)(4,1)S(1)} %eq.36) | copy-start | bytes 3076
  100.7 32.6 %copy-start.19 = (bf16[192,768]{1,0:T(8,128)(2,1)S(1)}, bf16[192,768]{1,0:T(8,128)(2,1)}, u32[]{:S(2)}) copy-start(bf16[192,768]{1,0:T(8,128)(2,1)} %all_gather.29) | copy-start | bytes 884740
  100.7 1.8 copy-start.23
  100.7 1.9 copy-start.25
  100.7 1.9 copy-start.27
  111.0 1.8 copy-start.27
  121.3 1.9 copy-start.27
  131.5 4.7 copy-start.6
  131.5 44.7 %copy-start.42 = (f32[768]{0:T(1024)S(1)}, f32[768]{0:T(1024)}, u32[]{:S(2)}) copy-start(f32[768]{0:T(1024)} %param.30) | copy-start | bytes 9220
  133.2 45.1 %copy-start.8 = (bf16[24,8,4,256]{3,1,2,0:T(8,128)(2,1)}, bf16[24,8,4,256]{3,1,2,0:T(8,128)(2,1)S(1)}, u32[]{:S(2)}) copy-start(bf16[24,8,4,256]{3,1,2,0:T(8,128)(2,1)S(1)} %copy.64) | copy-start | bytes 1179652
  135.0 65.4 %all-gather.9.cloned.1.call-start = ((), (), s32[]{:S(2)}) async-start(), calls=%async_computation.9 | async-start | bytes 1769472 | tf_op jit(solution)/shard_map/all_gather | solution.py:81
  135.6 89.0 %all-gather.11.cloned.1.call-start = ((), (), s32[]{:S(2)}) async-start(), calls=%async_computation.10 | async-start | bytes 1769472 | tf_op jit(solution)/shard_map/all_gather | solution.py:82
  136.2 135.8 %all-reduce.11.cloned.1.call-start = ((), (), s32[]{:S(2)}) async-start(), calls=%async_computation.11 | async-start | bytes 3145728 | tf_op jit(solution)/shard_map/psum | solution.py:151
  176.2 2.1 copy-start.4
  179.3 157.1 %copy-start.33 = (f32[1024]{0:T(1024)}, f32[1024]{0:T(1024)S(1)}, u32[]{:S(2)}) copy-start(f32[1024]{0:T(1024)S(1)} %add_rsqrt_fusion.1) | copy-start | bytes 12292
  179.3 21.2 %copy-start.29 = (f32[768]{0:T(1024)S(1)}, f32[768]{0:T(1024)}, u32[]{:S(2)}) copy-start(f32[768]{0:T(1024)} %param.31) | copy-start | bytes 9220
  179.3 21.2 %copy-start.36 = (f32[768]{0:T(1024)S(1)}, f32[768]{0:T(1024)}, u32[]{:S(2)}) copy-start(f32[768]{0:T(1024)} %param.32) | copy-start | bytes 9220
  179.3 21.2 %copy-start.50 = (f32[768]{0:T(1024)S(1)}, f32[768]{0:T(1024)}, u32[]{:S(2)}) copy-start(f32[768]{0:T(1024)} %param.34) | copy-start | bytes 9220
  224.6 4.4 copy-start.32
  228.9 43.1 %copy-start.35 = (f32[768]{0:T(1024)S(1)}, f32[768]{0:T(1024)}, u32[]{:S(2)}) copy-start(f32[768]{0:T(1024)} %param.36) | copy-start | bytes 9220
  229.0 102.6 %all-reduce.13.cloned.1.call-start = ((), (), s32[]{:S(2)}) async-start(), calls=%async_computation.12 | async-start | bytes 3145728 | tf_op jit(solution)/shard_map/psum | solution.py:163
  272.0 2.2 copy-start.5
  277.4 2.2 copy-start.48
  277.4 3.9 copy-start.52
  279.1 5.7 copy-start.11
  281.3 4.6 copy-start.47
  285.9 45.7 %copy-start.46 = (f32[768]{0:T(1024)S(1)}, f32[768]{0:T(1024)}, u32[]{:S(2)}) copy-start(f32[768]{0:T(1024)} %param.38) | copy-start | bytes 9220
  288.5 266.2 %reduce-scatter.15.cloned.1.call-start = ((), (), s32[]{:S(2)}) async-start(), calls=%async_computation.13 | async-start | bytes 3932160 | tf_op jit(solution)/shard_map/reduce_scatter | solution.py:218
  348.2 1.9 copy-start.24
  348.3 1.9 copy-start.26
  348.3 1.9 copy-start.28
  398.3 1.9 copy-start.24
  398.3 1.9 copy-start.26
  398.4 1.9 copy-start.28
  448.4 1.9 copy-start.24
  448.4 1.9 copy-start.26
  448.4 1.9 copy-start.28
  494.1 84.9 %reduce-scatter.23.cloned.1.call-start = ((), (), s32[]{:S(2)}) async-start(), calls=%async_computation.18 | async-start | bytes 589824
  499.6 95.0 %reduce-scatter.25.cloned.1.call-start = ((), (), s32[]{:S(2)}) async-start(), calls=%async_computation.19 | async-start | bytes 1769472
  506.9 5.7 copy-start.45
  506.9 112.4 %reduce-scatter.19.cloned.1.call-start = ((), (), s32[]{:S(2)}) async-start(), calls=%async_computation.16 | async-start | bytes 1769472
  513.8 59.6 %copy-start.14 = (bf16[1,1024,192]{1,2,0:T(8,128)(2,1)}, bf16[1,1024,192]{1,2,0:T(8,128)(2,1)S(1)}, u32[]{:S(2)}) copy-start(bf16[1,1024,192]{1,2,0:T(8,128)(2,1)S(1)} %get-tuple-element.250) | copy-start | bytes 1179652
  526.3 110.6 %reduce-scatter.21.cloned.1.call-start = ((), (), s32[]{:S(2)}) async-start(), calls=%async_computation.17 | async-start | bytes 884736
  559.9 9.4 %copy-start.30 = (f32[768]{0:T(1024)S(1)}, f32[768]{0:T(1024)}, u32[]{:S(2)}) copy-start(f32[768]{0:T(1024)} %param.31) | copy-start | bytes 9220
  559.9 9.4 %copy-start.37 = (f32[768]{0:T(1024)S(1)}, f32[768]{0:T(1024)}, u32[]{:S(2)}) copy-start(f32[768]{0:T(1024)} %param.32) | copy-start | bytes 9220
  569.2 92.3 %reduce-scatter.17.cloned.1.call-start = ((), (), s32[]{:S(2)}) async-start(), calls=%async_computation.15 | async-start | bytes 1769472 | tf_op jit(solution)/shard_map/reduce_scatter | solution.py:295
  573.2 146.0 %all-reduce.15.cloned.1.call-start = ((), (), s32[]{:S(2)}) async-start(), calls=%async_computation.14 | async-start | bytes 3145728 | tf_op jit(solution)/shard_map/psum | solution.py:245
  573.5 3.2 copy-start.10
  573.5 3.2 copy-start.13
  578.9 221.9 %all-reduce.17.cloned.1.call-start = ((), (), s32[]{:S(2)}) async-start(), calls=%async_computation.20 | async-start | bytes 4423680 | tf_op jit(solution)/shard_map/psum | solution.py:279
  661.5 7.6 copy-start.15
  664.9 54.2 %copy-start.34 = (f32[1024]{0:T(1024)S(1)}, f32[1024]{0:T(1024)}, u32[]{:S(2)}) copy-start(f32[1024]{0:T(1024)} %copy-done.33) | copy-start | bytes 12292
  664.9 54.2 %copy-start.39 = (f32[1024]{0:T(1024)S(1)}, f32[1024]{0:T(1024)}, u32[]{:S(2)}) copy-start(f32[1024]{0:T(1024)} %copy-done.38) | copy-start | bytes 12292
  664.9 54.2 %copy-start.41 = (f32[1024]{0:T(1024)S(1)}, f32[1024]{0:T(1024)}, u32[]{:S(2)}) copy-start(f32[1024]{0:T(1024)} %copy-done.40) | copy-start | bytes 12292
  800.9 5.7 copy-start.21
  800.9 6.8 copy-start.20
  (16 other events, 22.4 us)
Sparse Core Ops, SparseCore 0:
  9.5 25.4 all-gather.4
  37.2 63.4 all-gather.6
  135.1 41.0 all-reduce.8
  177.6 22.7 all-gather.8
  201.8 22.7 all-gather.10
  229.1 42.8 all-reduce.10
  288.6 42.8 all-reduce.12
  494.2 60.4 reduce-scatter.14
  557.0 13.0 reduce-scatter.22
  572.8 21.8 reduce-scatter.24
  597.4 21.8 reduce-scatter.18
  621.4 15.3 reduce-scatter.20
  639.7 21.8 reduce-scatter.16
  663.7 43.4 all-reduce.14
  710.5 90.3 all-reduce.16
where the time goes:
time: 825 us; the launch traced here: 816 us
  waiting for transfers between devices  371 us (45%)
  matrix products  212 us (26%)
  blocking collectives  85 us (10%)
  local copies, waits for them, and re-layouts  66 us (8%)
  other arithmetic  64.1 us (8%)
  between operations  15 us (2%)
    psum x1, waiting for transfers between devices, per_device(): lax.psum(weight_grads[0].astype(jnp.bfloat16), 'ctx').astype(jnp.float32)  77.6 us
    unnamed x19, waiting for transfers between devices  50.9 us
    psum x1, waiting for transfers between devices, per_device(): lax.psum(up_terms.astype(jnp.bfloat16), 'tp').astype(jnp.float32)  42.8 us
    psum x1, blocking collectives, per_device(): lax.psum((jnp.sum(grad_first_own * first_hat_own, axis=0), jnp.sum(grad_f...  41.3 us
    psum x1, waiting for transfers between devices, per_device(): lax.psum(down_terms.astype(jnp.bfloat16), 'tp').astype(jnp.float32)  41.2 us
    psum x1, waiting for transfers between devices, per_device(): lax.psum(attn_terms.astype(jnp.bfloat16), 'tp').astype(jnp.float32)  39.5 us
    unnamed x108, local copies, waits for them, and re-layouts  38.4 us
    all_gather x1, waiting for transfers between devices, per_device(): keys_all = lax.all_gather(by_head(key_values), 'ctx', axis=3, tiled=True)  35.8 us
  transfers between devices with their start and end apart: 15, of which 12 were waited for; matrix products, arithmetic and copies ran while one was open for 14% of the time, Pallas kernels for 0%

commit v1 on v0

v1 whole, which is shorter than its diff:
```python
import functools

import jax
import jax.numpy as jnp
from jax import lax
from jax.experimental import pallas as pl
from jax.experimental.pallas import tpu as pltpu
from jax.sharding import PartitionSpec as P

BF = jnp.bfloat16
F32 = jnp.float32
HEAD = 64
EPS = 1e-05
MASKED = -1e30
ROOT_HALF = 0.7071067811865476
INV_ROOT_TWO_PI = 0.3989422804014327
VMEM_LIMIT = 66 * 1024 * 1000
MESH = pl.DeviceIdType.MESH
DMA = pltpu.SemaphoreType.DMA


def nn(left, right):
    return lax.dot_general(left, right, (((1,), (0,)), ((), ())), preferred_element_type=F32)


def nt(left, right):
    return lax.dot_general(left, right, (((1,), (1,)), ((), ())), preferred_element_type=F32)


def tn(left, right):
    return lax.dot_general(left, right, (((0,), (0,)), ((), ())), preferred_element_type=F32)


def remote(src, dst, send_sem, recv_sem, peer):
    return pltpu.make_async_remote_copy(
        src_ref=src,
        dst_ref=dst,
        send_sem=send_sem,
        recv_sem=recv_sem,
        device_id=peer,
        device_id_type=MESH,
    )


def greet(peers):
    barrier = pltpu.get_barrier_semaphore()
    for peer in peers:
        pl.semaphore_signal(barrier, inc=1, device_id=peer, device_id_type=MESH)
    pl.semaphore_wait(barrier, len(peers))


class Place:
    def __init__(self, ns, nc):
        self.s = lax.axis_index("shard")
        self.c = lax.axis_index("ctx")
        self.t = lax.axis_index("tp")
        self.core = lax.rem(self.t, 2)
        self.y = self.t // 2
        self.mate_t = self.t + 1 - 2 * self.core
        self.ymate_t = lax.rem(self.t + 2, 4)
        self.mate = {"tp": self.mate_t}
        self.ymate = {"tp": self.ymate_t}
        self.zpeers = [{"ctx": lax.rem(self.c + k, nc)} for k in range(1, nc)]
        self.xpeers = [{"shard": lax.rem(self.s + r, ns)} for r in range(1, ns)]


class TpGather:
    def __init__(self, place, buf, sems):
        self.p, self.buf = place, buf
        self.ys, self.yr, self.ks, self.kr, self.fs, self.fr = sems

    def _y(self, b, i, src):
        p = self.p
        return remote(src, self.buf.at[b, p.t], self.ys.at[i], self.yr.at[i], p.ymate)

    def _k(self, b, i, src):
        p = self.p
        return remote(src, self.buf.at[b, p.t], self.ks.at[i], self.kr.at[i], p.mate)

    def _f(self, b, i):
        p = self.p
        piece = self.buf.at[b, p.ymate_t]
        return remote(piece, piece, self.fs.at[i], self.fr.at[i], p.mate)

    def send(self, b, i, src=None):
        src = self.buf.at[b, self.p.t] if src is None else src
        self._y(b, i, src).start()
        self._k(b, i, src).start()

    def forward(self, b, i):
        p = self.p
        piece = self.buf.at[b, p.ymate_t]
        remote(piece, piece, self.ys.at[i], self.yr.at[i], p.ymate).wait_recv()
        self._f(b, i).start()

    def arrive(self, b, i):
        p = self.p
        piece = self.buf.at[b, p.mate_t]
        remote(piece, piece, self.ks.at[i], self.kr.at[i], p.mate).wait_recv()
        piece = self.buf.at[b, lax.rem(p.mate_t + 2, 4)]
        remote(piece, piece, self.fs.at[i], self.fr.at[i], p.mate).wait_recv()

    def drain(self, b, i, src=None):
        src = self.buf.at[b, self.p.t] if src is None else src
        self._y(b, i, src).wait_send()
        self._k(b, i, src).wait_send()
        self._f(b, i).wait_send()


class TpReduce:
    def __init__(self, place, terms, from_mate, staged, from_y, sems):
        self.p, self.terms, self.from_mate, self.staged, self.from_y = (
            place,
            terms,
            from_mate,
            staged,
            from_y,
        )
        self.ks, self.kr, self.ys, self.yr = sems

    def _k(self, b):
        p = self.p
        return remote(
            self.terms.at[b, :, 1 - p.core],
            self.from_mate.at[b],
            self.ks.at[b],
            self.kr.at[b],
            p.mate,
        )

    def _y(self, b):
        return remote(
            self.staged.at[b], self.from_y.at[b], self.ys.at[b], self.yr.at[b], self.p.ymate
        )

    def send(self, b):
        self._k(b).start()

    def across(self, b):
        p = self.p
        self._k(b).wait_recv()
        other = 1 - p.y
        self.staged[b] = (
            self.terms[b, other, p.core].astype(F32) + self.from_mate[b, other].astype(F32)
        ).astype(BF)
        self._y(b).start()

    def result(self, b):
        p = self.p
        self._y(b).wait_recv()
        return (
            self.terms[b, p.y, p.core].astype(F32)
            + self.from_mate[b, p.y].astype(F32)
            + self.from_y[b].astype(F32)
        )

    def drain(self, b):
        self._k(b).wait_send()
        self._y(b).wait_send()


def column(row, width=128):
    return jnp.broadcast_to(row, (width, row.shape[-1])).T


def project_kernel(
    ns, nc, x_ref, code_ref, w_ref, bias_ref,
    xf_ref, q_ref, kv_ref, codef_ref, wf_ref,
    local, zs, zr, ds, dr, ws, wr, *tp_sems,
):
    p = Place(ns, nc)
    piece = x_ref.shape[1] // 4
    greet([p.mate, p.ymate] + p.zpeers + p.xpeers)
    heads = w_ref.shape[0] - 1

    def weight(h, r):
        return remote(
            w_ref.at[h], wf_ref.at[h, p.s], ws.at[h, r], wr.at[h, r], p.xpeers[r]
        )

    for h in range(heads + 1):
        for r in range(ns - 1):
            weight(h, r).start()
    mine = pl.ds(p.t * piece, piece)

    def x_send(k):
        peer = p.zpeers[k]
        return remote(
            x_ref.at[peer["ctx"], mine], xf_ref.at[p.c, p.t], zs.at[k], zr.at[k], peer
        )

    def code_send(k):
        peer = p.zpeers[k]
        return remote(code_ref.at[peer["ctx"]], codef_ref.at[p.c], ds.at[k], dr.at[k], peer)

    for k in range(nc - 1):
        x_send(k).start()
    for k in range(nc - 1):
        code_send(k).start()
    own = x_ref.at[p.c, mine]
    copies = [
        pltpu.make_async_copy(own, xf_ref.at[p.c, p.t], local.at[0]),
        pltpu.make_async_copy(code_ref.at[p.c], codef_ref.at[p.c], local.at[1]),
        pltpu.make_async_copy(w_ref, wf_ref.at[:, p.s], local.at[2]),
    ]
    for copy in copies:
        copy.start()
    gather = TpGather(p, xf_ref, tp_sems)
    gather.send(p.c, 0, own)
    blocks = [lax.rem(p.c + nc - k, nc) for k in range(nc)]
    for k in range(1, nc):
        landed = xf_ref.at[blocks[k], p.t]
        remote(landed, landed, zs.at[k - 1], zr.at[k - 1], p.zpeers[k - 1]).wait_recv()
        gather.send(blocks[k], k)
        gather.forward(blocks[k - 1], k - 1)
    gather.forward(blocks[nc - 1], nc - 1)
    for k in range(nc):
        gather.arrive(blocks[k], k)
    for k in range(nc - 1):
        landed = codef_ref.at[blocks[k + 1]]
        remote(landed, landed, ds.at[k], dr.at[k], p.zpeers[k]).wait_recv()
    for copy in copies:
        copy.wait()
    width = xf_ref.shape[-1]
    rows = 4 * piece
    for h in range(heads):
        for r in range(ns - 1):
            landed = wf_ref.at[h, lax.rem(p.s + ns - 1 - r, ns)]
            remote(landed, landed, ws.at[h, r], wr.at[h, r], p.xpeers[r]).wait_recv()

        def project(b, carry):
            x = xf_ref[b].reshape(rows, width)
            out = nn(x, wf_ref[h].reshape(width, 384)) + bias_ref[h]
            entity = column(codef_ref[b]) < 0.0
            at = pl.ds(pl.multiple_of(b * rows, rows), rows)
            chosen = jnp.where(entity, out[:, 128:256], out[:, 0:128])
            q_ref[h, at] = (chosen * HEAD ** (-0.5)).astype(BF)
            kv_ref[h, at] = out[:, 256:384].astype(BF)
            return carry

        lax.fori_loop(0, nc, project, 0)
    for r in range(ns - 1):
        landed = wf_ref.at[heads, lax.rem(p.s + ns - 1 - r, ns)]
        remote(landed, landed, ws.at[heads, r], wr.at[heads, r], p.xpeers[r]).wait_recv()
    for h in range(heads + 1):
        for r in range(ns - 1):
            weight(h, r).wait_send()
    for k in range(nc - 1):
        x_send(k).wait_send()
        code_send(k).wait_send()
    gather.drain(p.c, 0, own)
    for k in range(1, nc):
        gather.drain(blocks[k], k)


def attend_kernel(q_ref, kv_ref, code_ref, e_ref, ctx_ref, inv_ref, kcat, vt, segcol):
    h, b = pl.program_id(0), pl.program_id(1)
    length = kv_ref.shape[1]
    nblk, rows = code_ref.shape[0], code_ref.shape[2]

    @pl.when((h == 0) & (b == 0))
    def _():
        for j in range(nblk):
            col = jnp.abs(column(code_ref[j]))
            segcol[j * rows : (j + 1) * rows] = jnp.where(col == 0.0, -1.0, col)

    @pl.when(b == 0)
    def _():
        low_half = lax.broadcasted_iota(jnp.int32, (rows, 128), 1) < HEAD
        for j in range(nblk):
            at = slice(j * rows, (j + 1) * rows)
            entity = column(code_ref[j]) < 0.0
            kv = kv_ref[0, at].astype(F32)
            turned = pltpu.roll(kv, HEAD, 1)
            keep = jnp.where(low_half, kv, turned)
            kcat[at] = jnp.where(low_half == entity, 0.0, keep).astype(BF)
            vt[:, at] = jnp.where(low_half, 0.0, kv).T.astype(BF)

    scores = nt(kcat[...], q_ref[0])
    segment = jnp.abs(code_ref[b])
    col = segcol[...]
    allowed = jnp.concatenate([col] * (rows // 128), axis=1) == segment
    scores = jnp.where(allowed, scores, MASKED)
    top = jnp.max(scores, axis=0, keepdims=True)
    top = jnp.where(top == MASKED, 0.0, top)
    exponent = jnp.exp(scores - top)
    inverse = 1.0 / jnp.maximum(jnp.sum(exponent, axis=0, keepdims=True), 1.0)
    exponent = exponent.astype(BF)
    e_ref[0] = exponent
    inv_ref[0, 0] = inverse
    ctx_ref[...] = (nn(vt[...], exponent) * inverse).T.astype(BF)


def spread(values):
    average = jnp.mean(values, axis=-1, keepdims=True)
    centred = values - average
    inverse = lax.rsqrt(jnp.mean(centred * centred, axis=-1, keepdims=True) + EPS)
    return centred * inverse, inverse


def unspread(upstream, normed, inverse, gain):
    scaled = upstream * gain
    first = jnp.mean(scaled, axis=-1, keepdims=True)
    second = jnp.mean(scaled * normed, axis=-1, keepdims=True)
    return inverse * (scaled - first - normed * second)


def total(values):
    return jnp.sum(values, axis=0, keepdims=True)


SKEWS_C = (0, 1, 3, 4, 5, 6, 8, 9, 10, 11, 13, 14, 15)


def feed_kernel(
    ns, nc, ctx_ref, wo_ref, xf_ref, og_ref, wu_ref, wd_ref, vec_ref,
    ga_ref, hid_ref, gfi_ref, dff_ref, small_ref,
    wuf, wdf, ogo, hsend,
    t0, m0, s0, y0, t1, m1, s1, y1, t2, m2, s2, y2,
    low, gf, active, slope, gup, fo, fh, fi, gs, dst, xr,
    local, ws, wr, os, orr, hs, hr, xs, xrs, *tp_sems,
):
    p = Place(ns, nc)
    piece, width = xf_ref.shape[2:]
    rows = 4 * piece
    greet([p.mate, p.ymate] + p.zpeers + p.xpeers)
    weights = ((wu_ref, wuf), (wd_ref, wdf))

    def weight(a, r):
        src, dst = weights[a]
        return remote(src, dst.at[p.s], ws.at[a, r], wr.at[a, r], p.xpeers[r])

    for a in range(2):
        for r in range(ns - 1):
            weight(a, r).start()
    mine = pl.ds(p.t * piece, piece)

    def og_send(k):
        peer = p.zpeers[k]
        return remote(og_ref.at[peer["ctx"], mine], ogo.at[p.c], os.at[k], orr.at[k], peer)

    for k in range(nc - 1):
        og_send(k).start()
    copies = [
        pltpu.make_async_copy(og_ref.at[p.c, mine], ogo.at[p.c], local.at[0]),
        pltpu.make_async_copy(wu_ref, wuf.at[p.s], local.at[1]),
        pltpu.make_async_copy(wd_ref, wdf.at[p.s], local.at[2]),
    ]
    for copy in copies:
        copy.start()
    small_ref[...] = jnp.zeros_like(small_ref)

    sums = [
        TpReduce(p, *bufs, [tp_sems[j].at[i] for j in range(4)])
        for i, bufs in enumerate(((t0, m0, s0, y0), (t1, m1, s1, y1), (t2, m2, s2, y2)))
    ]
    shares = [
        TpGather(p, buf, [tp_sems[4 + j].at[i] for j in range(6)])
        for i, buf in enumerate((low, gf, ga_ref))
    ]
    out_bias, gain1, bias1, up_bias, down_bias, gain2, bias2 = (
        vec_ref[i : i + 1] for i in range(7)
    )

    def put(terms, b, values):
        terms[b] = values.astype(BF).reshape(2, 2, piece, width)

    def add_small(row, values):
        small_ref[row : row + 1] += total(values)

    def out_project(b):
        put(t0, b, nt(ctx_ref[b], wo_ref[...]))
        sums[0].send(b)

    def norm_one(b):
        h = xf_ref[b, p.t].astype(F32) + (sums[0].result(b) + out_bias)
        normed, inverse = spread(h)
        first = normed * gain1 + bias1
        fo[b] = first
        fh[b] = normed
        fi[b] = inverse
        low[b, p.t] = first.astype(BF)
        shares[0].send(b, b)

    def feed_forward(b):
        @pl.when(b == 0)
        def _():
            for a in range(2):
                for r in range(ns - 1):
                    landed = weights[a][1].at[lax.rem(p.s + ns - 1 - r, ns)]
                    remote(landed, landed, ws.at[a, r], wr.at[a, r], p.xpeers[r]).wait_recv()
            for copy in copies[1:]:
                copy.wait()

        shares[0].arrive(b, b)
        up = nn(low[b].reshape(rows, width), wuf[...].reshape(width, -1)) + up_bias
        cdf = 0.5 * (1.0 + lax.erf(up * ROOT_HALF))
        act = (up * cdf).astype(BF)
        active[b] = act
        slope[b] = cdf + up * (jnp.exp(-0.5 * up * up) * INV_ROOT_TWO_PI)
        put(t1, b, nt(act, wdf[...].reshape(width, -1)))
        sums[1].send(b)

    def hid_send(b):
        return remote(hsend.at[b], hid_ref.at[p.c], hs.at[b], hr.at[p.c], {"ctx": b})

    def norm_two(b):
        @pl.when(b == 0)
        def _():
            for k in range(nc - 1):
                landed = ogo.at[lax.rem(p.c + nc - 1 - k, nc)]
                remote(landed, landed, os.at[k], orr.at[k], p.zpeers[k]).wait_recv()
            copies[0].wait()

        normed, inverse = spread(fo[b] + (sums[1].result(b) + down_bias))
        hsend[b] = (normed * gain2 + bias2).astype(BF)

        upstream = ogo[b].astype(F32)
        add_small(2, upstream * normed)
        add_small(3, upstream)
        grad = unspread(upstream, normed, inverse, gain2)
        gs[b] = grad
        grad = grad.astype(BF)
        gf[b, p.t] = grad
        add_small(5, grad.astype(F32))
        shares[1].send(b, b)

        @pl.when(b != p.c)
        def _():
            hid_send(b).start()

        @pl.when(b == p.c)
        def _():
            pltpu.make_async_copy(hsend.at[b], hid_ref.at[p.c], local.at[3]).start()

    def feed_back(b):
        shares[1].arrive(b, b)
        grad = nn(gf[b].reshape(rows, width), wdf[...].reshape(width, -1))
        grad = (grad.astype(BF).astype(F32) * slope[b]).astype(BF)
        gup[b] = grad
        add_small(6, grad.astype(F32))
        put(t2, b, nt(grad, wuf[...].reshape(width, -1)))
        sums[2].send(b)

    def norm_back(b):
        grad = gs[b] + sums[2].result(b)
        add_small(0, grad * fh[b])
        add_small(1, grad)
        grad = unspread(grad, fh[b], fi[b], gain1)
        gfi_ref[b] = grad
        grad = grad.astype(BF)
        ga_ref[b, p.t] = grad
        add_small(4, grad.astype(F32))
        shares[2].send(b, b)

    stages = (
        out_project,
        sums[0].across,
        norm_one,
        lambda b: shares[0].forward(b, b),
        feed_forward,
        sums[1].across,
        norm_two,
        lambda b: shares[1].forward(b, b),
        feed_back,
        sums[2].across,
        norm_back,
        lambda b: shares[2].forward(b, b),
        lambda b: shares[2].arrive(b, b),
    )

    def grad_send(a, r):
        return remote(
            dst.at[a, p.xpeers[r]["shard"]], xr.at[a, r], xs.at[a, r], xrs.at[a, r], p.xpeers[r]
        )

    def weight_grad(a):
        left = (low, gf)[a][...].reshape(nc * rows, width)
        right = (gup, active)[a][...].reshape(nc * rows, -1)
        dst[a] = tn(left, right).astype(BF).reshape(dst.shape[1:])
        for r in range(ns - 1):
            grad_send(a, r).start()

    def slot(step, carry):
        for skew, stage in zip(SKEWS_C, stages):
            b = step - skew

            @pl.when((b >= 0) & (b < nc))
            def _(stage=stage, b=b):
                stage(b)

        for a in range(2):

            @pl.when(step == SKEWS_C[8] + nc - 1 + a)
            def _(a=a):
                weight_grad(1 - a)

        return carry

    lax.fori_loop(0, SKEWS_C[-1] + nc, slot, 0)
    half = width // 2
    for a in (1, 0):
        grad = dst[a, p.s].astype(F32)
        for r in range(ns - 1):
            grad_send(a, r).wait_recv()
            grad = grad + xr[a, r].astype(F32)
        grad = grad.astype(BF)
        dff_ref[2 * a] = grad[:, :half]
        dff_ref[2 * a + 1] = grad[:, half:]
    for k in range(1, nc):
        src = lax.rem(p.c + k, nc)
        landed = hid_ref.at[src]
        remote(landed, landed, hs.at[src], hr.at[src], p.zpeers[k - 1]).wait_recv()
        hid_send(src).wait_send()
    pltpu.make_async_copy(hsend.at[p.c], hid_ref.at[p.c], local.at[3]).wait()
    for a in range(2):
        for r in range(ns - 1):
            weight(a, r).wait_send()
            grad_send(a, r).wait_send()
    for k in range(nc - 1):
        og_send(k).wait_send()
    for i in range(3):
        for b in range(nc):
            sums[i].drain(b)
            shares[i].drain(b, b)


def attend_back_kernel(
    ga_ref, wf_ref, ctxf_ref, xf_ref, code_ref, e_ref, inv_ref, ctx_ref, q_ref, kv_ref,
    dw_ref, back_ref, qb_ref,
    dctx, kcat, dkey, dval, dqkv, back,
):
    h, b = pl.program_id(0), pl.program_id(1)
    heads = pl.num_programs(0)
    nblk, rows = code_ref.shape[0], code_ref.shape[2]
    width = xf_ref.shape[1]

    @pl.when((h == 0) & (b == 0))
    def _():
        out = wf_ref[3].reshape(width, 384)
        for i in range(3):
            dctx[i] = nn(ga_ref[...], out[:, i * 128 : (i + 1) * 128]).astype(BF)
        dw_ref[3] = tn(ga_ref[...], ctxf_ref[...]).astype(BF)
        back[...] = jnp.zeros_like(back)

    low_half = lax.broadcasted_iota(jnp.int32, (rows, 128), 1) < HEAD

    @pl.when(b == 0)
    def _():
        for j in range(nblk):
            at = slice(j * rows, (j + 1) * rows)
            entity = column(code_ref[j]) < 0.0
            kv = kv_ref[0, at].astype(F32)
            keep = jnp.where(low_half, kv, pltpu.roll(kv, HEAD, 1))
            kcat[at] = jnp.where(low_half == entity, 0.0, keep).astype(BF)
        dkey[...] = jnp.zeros_like(dkey)
        dval[...] = jnp.zeros_like(dval)

    at = pl.ds(pl.multiple_of(b * rows, rows), rows)
    grad_ctx = dctx[h, at].astype(F32).T * inv_ref[0, 0]
    row_dot = jnp.sum(grad_ctx * ctx_ref[...].astype(F32).T, axis=0, keepdims=True)
    grad_ctx = grad_ctx.astype(BF)
    weight = e_ref[0]
    grad = nn(kv_ref[0], grad_ctx)
    grad = (weight.astype(F32) * (grad - row_dot)).astype(BF)
    dval[...] += nt(weight, grad_ctx)
    dkey[...] += nn(grad, q_ref[0])
    grad_q = tn(kcat[...], grad).T * HEAD ** (-0.5)
    entity = column(code_ref[b]) < 0.0
    dqkv[at, 0:128] = jnp.where(entity, 0.0, grad_q).astype(BF)
    dqkv[at, 128:256] = jnp.where(entity, grad_q, 0.0).astype(BF)

    @pl.when(b == nblk - 1)
    def _():
        for j in range(nblk):
            part = slice(j * rows, (j + 1) * rows)
            entity = column(code_ref[j]) < 0.0
            grad_k = dkey[part]
            grad_k = jnp.where(entity, pltpu.roll(grad_k, HEAD, 1), grad_k)
            dqkv[part, 256:384] = jnp.where(low_half, grad_k, dval[part]).astype(BF)
        grads = dqkv[...]
        qb_ref[h] = total(grads.astype(F32))
        dw_ref[h] = tn(xf_ref[...], grads).astype(BF)
        back[...] += nt(grads, wf_ref[h].reshape(width, 384))

        @pl.when(h == heads - 1)
        def _():
            back_ref[...] = back[...].astype(BF)


def finish_kernel(
    ns, nc, back_ref, gfi_ref, hid_ref, dff_ref, dqo_ref, smc_ref, qb_ref,
    ing_ref, hidf_ref, dw_ref, sm_ref,
    m0, s0, y0, ig, zo, zr, zq, zsum, xr, smt, smz, smx,
    local, xs, xrs, z1s, z1r, z2s, z2r, z3s, z3r, z4s, z4r, gs, gr, hl, ss, sr, szs, szr, sxs, sxr,
    *tp_sems,
):
    p = Place(ns, nc)
    piece, width = gfi_ref.shape[1:]
    chunks = dw_ref.shape[0]
    first = dff_ref.shape[0]
    greet([p.mate, p.ymate] + p.zpeers + p.xpeers)

    def x_send(k, r):
        peer = p.xpeers[r]
        return remote(dqo_ref.at[k, peer["shard"]], xr.at[k, r], xs.at[k, r], xrs.at[k, r], peer)

    back_sum = TpReduce(p, back_ref, m0, s0, y0, [tp_sems[j] for j in range(4)])
    for b in range(nc):
        back_sum.send(b)
    for k in range(chunks - first):
        for r in range(ns - 1):
            x_send(k, r).start()
    copies = [
        pltpu.make_async_copy(dff_ref, zo.at[pl.ds(0, first)], local.at[0]),
        pltpu.make_async_copy(hid_ref, hidf_ref.at[:, p.t], local.at[1]),
    ]
    for copy in copies:
        copy.start()
    share_h = TpGather(p, hidf_ref, [tp_sems[4 + j].at[0] for j in range(6)])
    share_g = TpGather(p, ing_ref, [tp_sems[4 + j].at[1] for j in range(6)])

    outer = (p.c == 0) | (p.c == nc - 1)
    inner = (p.c > 0) & (p.c < nc - 1)
    inward = {"ctx": 1 + p.c // 3}
    outward = {"ctx": lax.rem(3 * (p.c + nc - 1), 6)}
    across = {"ctx": lax.rem(2 * nc - 1 - p.c, nc)}

    def to_inner(k):
        return remote(zo.at[k], zr.at[k], z1s.at[k], z1r.at[k], inward)

    def to_owner(k):
        return remote(zsum.at[k], zq.at[k], z2s.at[k], z2r.at[k], across)

    def to_other(k):
        return remote(dw_ref.at[k], dw_ref.at[k], z3s.at[k], z3r.at[k], across)

    def to_outer(k):
        return remote(dw_ref.at[k], dw_ref.at[k], z4s.at[k], z4r.at[k], outward)

    def owns(k):
        return lax.rem(k + p.c, 2) == 1

    def line_start(k):
        @pl.when(k == 0)
        def _():
            copies[0].wait()

        @pl.when(k >= first)
        def _():
            j = k - first
            grad = dqo_ref[j, p.s].astype(F32)
            for r in range(ns - 1):
                x_send(j, r).wait_recv()
                grad = grad + xr[j, r].astype(F32)
            zo[k] = grad.astype(BF)

        @pl.when(outer)
        def _():
            to_inner(k).start()

    def line_in(k):
        @pl.when(inner)
        def _():
            to_inner(k).wait_recv()

            @pl.when(jnp.logical_not(owns(k)))
            def _():
                zsum[k] = (zo[k].astype(F32) + zr[k].astype(F32)).astype(BF)
                to_owner(k).start()

    def line_out(k):
        @pl.when(inner)
        def _():
            @pl.when(owns(k))
            def _():
                to_owner(k).wait_recv()
                dw_ref[k] = (zo[k].astype(F32) + zr[k].astype(F32) + zq[k].astype(F32)).astype(BF)
                to_other(k).start()

            @pl.when(jnp.logical_not(owns(k)))
            def _():
                to_other(k).wait_recv()

            to_outer(k).start()

    at = p.c

    def small_tp(i, peer):
        return remote(smt.at[2 * i], smt.at[2 * i + 1], ss.at[i], sr.at[i], peer)

    shared = lax.broadcasted_iota(jnp.int32, smt.shape[1:], 0) < 6

    def small_fold(i):
        return smt[2 * i] + jnp.where(shared, smt[2 * i + 1], 0.0)

    def small_z(k):
        return remote(smz.at[at], smz.at[at], szs.at[k], szr.at[k], p.zpeers[k])

    def small_x(r):
        return remote(smx.at[p.s], smx.at[p.s], sxs.at[r], sxr.at[r], p.xpeers[r])

    def small_zero():
        smt[0] = jnp.zeros_like(smt[0])
        smt[0, :, 0:width] = smc_ref[...]
        for h in range(qb_ref.shape[0]):
            smt[0, 7:8, h * 384 : (h + 1) * 384] = qb_ref[h]
        small_tp(0, p.mate).start()

    def small_one():
        small_tp(0, p.mate).wait_recv()
        smt[2] = small_fold(0)
        small_tp(1, p.ymate).start()

    def small_two():
        small_tp(1, p.ymate).wait_recv()
        smz[at] = small_fold(1)
        for k in range(nc - 1):
            small_z(k).start()

    def small_three():
        for k in range(nc - 1):
            landed = smz.at[lax.rem(p.c + nc - 1 - k, nc)]
            remote(landed, landed, szs.at[k], szr.at[k], p.zpeers[k]).wait_recv()
        value = smz[0]
        for k in range(1, nc):
            value = value + smz[k]
        smx[p.s] = value
        for r in range(ns - 1):
            small_x(r).start()

    def small_four():
        for r in range(ns - 1):
            landed = smx.at[lax.rem(p.s + ns - 1 - r, ns)]
            remote(landed, landed, sxs.at[r], sxr.at[r], p.xpeers[r]).wait_recv()
        value = smx[0]
        for r in range(1, ns):
            value = value + smx[r]
        sm_ref[...] = value

    def grad_send(b):
        return remote(ig.at[b], ing_ref.at[p.c, p.t], gs.at[b], gr.at[p.c], {"ctx": b})

    def grad_own(b):
        ig[b] = (gfi_ref[b] + back_sum.result(b)).astype(BF)

        @pl.when(b != p.c)
        def _():
            grad_send(b).start()

        @pl.when(b == p.c)
        def _():
            pltpu.make_async_copy(ig.at[b], ing_ref.at[p.c, p.t], hl.at[0]).start()

    order = [lax.rem(p.c + k, nc) for k in range(nc)]

    def grad_share(k):
        q = lax.rem(p.c + k, nc)

        @pl.when(k > 0)
        def _():
            landed = ing_ref.at[q, p.t]
            remote(landed, landed, gs.at[q], gr.at[q], {"ctx": q}).wait_recv()
            share_g.send(q, k)

        @pl.when(k == 0)
        def _():
            pltpu.make_async_copy(ig.at[p.c], ing_ref.at[p.c, p.t], hl.at[0]).wait()
            share_g.send(q, k)

    for b in range(nc):
        share_h.send(b, b, hid_ref.at[b])
    small_zero()
    for k in range(first):
        line_start(k)
    for b in range(nc):
        back_sum.across(b)
    small_one()
    for b in range(nc):
        grad_own(b)
    small_two()
    for k in range(first):
        line_in(k)
    for b in range(nc):
        share_h.forward(b, b)
    for k in range(nc):
        grad_share(k)
    small_three()
    for k in range(first):
        line_out(k)
        line_start(k + first)
    for k in range(nc):
        share_g.forward(order[k], k)
    small_four()
    for k in range(first, chunks):
        line_in(k)
    for k in range(first, chunks):
        line_out(k)
    for b in range(nc):
        share_h.arrive(b, b)
        share_g.arrive(order[b], b)

    def line_end(k, carry):
        @pl.when(outer)
        def _():
            to_outer(k).wait_recv()
            to_inner(k).wait_send()

        @pl.when(inner)
        def _():
            @pl.when(owns(k))
            def _():
                to_other(k).wait_send()

            @pl.when(jnp.logical_not(owns(k)))
            def _():
                to_owner(k).wait_send()

            to_outer(k).wait_send()

        return carry

    lax.fori_loop(0, chunks, line_end, 0)
    copies[1].wait()
    for k in range(chunks - first):
        for r in range(ns - 1):
            x_send(k, r).wait_send()
    for b in range(nc):
        back_sum.drain(b)
        share_h.drain(b, b, hid_ref.at[b])
        share_g.drain(order[b], b)

        @pl.when(b != p.c)
        def _():
            grad_send(b).wait_send()

    small_tp(0, p.mate).wait_send()
    small_tp(1, p.ymate).wait_send()
    for k in range(nc - 1):
        small_z(k).wait_send()
    for r in range(ns - 1):
        small_x(r).wait_send()


def vmem(count):
    return [pl.BlockSpec(memory_space=pltpu.VMEM)] * count


def struct(shape, dtype):
    return jax.ShapeDtypeStruct(shape, dtype)


def params(collective_id=None):
    if collective_id is None:
        return pltpu.CompilerParams(
            vmem_limit_bytes=VMEM_LIMIT, dimension_semantics=("arbitrary", "arbitrary")
        )
    return pltpu.CompilerParams(
        vmem_limit_bytes=VMEM_LIMIT, collective_id=collective_id, has_side_effects=True
    )


TP_GATHER = 6
TP_REDUCE = 4


def per_device(
    hidden_in,
    token_type,
    segment,
    query_weight,
    key_value_weight,
    query_bias,
    value_bias,
    out_weight,
    out_bias,
    norm1_gain,
    norm1_bias,
    up_weight,
    up_bias,
    down_weight,
    down_bias,
    norm2_gain,
    norm2_bias,
    out_grad,
):
    ns, nc = lax.axis_size("shard"), lax.axis_size("ctx")
    seqs, local_len, width = hidden_in.shape
    part = query_weight.shape[2]
    heads = part // HEAD
    shard_rows = query_weight.shape[1]
    ff = up_weight.shape[1]
    piece = local_len // 4
    length = nc * local_len
    assert seqs == nc == 4 and heads == 3 and ff == width
    wide = ns - 1

    code = jnp.where(token_type == 0, segment, -segment).astype(F32).reshape(nc, 1, local_len)
    stacked = jnp.concatenate([query_weight, key_value_weight], axis=0)
    stacked = stacked.reshape(6, shard_rows, heads, HEAD).transpose(2, 1, 0, 3)
    stacked = stacked.reshape(heads, shard_rows, 6 * HEAD)
    out_t = out_weight.T.reshape(shard_rows, heads, 1, HEAD)
    out_t = jnp.pad(out_t, ((0, 0), (0, 0), (1, 0), (0, 0))).reshape(1, shard_rows, 2 * part)
    stacked = jnp.concatenate([stacked, out_t], axis=0)
    bias = jnp.concatenate([query_bias, jnp.zeros((1, part), F32), value_bias[None]], axis=0)
    bias = bias.reshape(6, heads, HEAD).transpose(1, 0, 2).reshape(heads, 1, 6 * HEAD)
    vectors = jnp.stack(
        [out_bias, norm1_gain, norm1_bias, up_bias, down_bias, norm2_gain, norm2_bias, norm2_bias]
    )
    down_t = down_weight.T

    xf, q, kv, code, wf = pl.pallas_call(
        functools.partial(project_kernel, ns, nc),
        out_shape=(
            struct((nc, 4, piece, width), BF),
            struct((heads, length, 128), BF),
            struct((heads, length, 128), BF),
            struct((nc, 1, local_len), F32),
            struct((heads + 1, ns, shard_rows, 384), BF),
        ),
        in_specs=vmem(4),
        out_specs=vmem(5),
        scratch_shapes=[DMA((3,))]
        + [DMA((nc - 1,))] * 4
        + [DMA((heads + 1, wide))] * 2
        + [DMA((nc,))] * TP_GATHER,
        compiler_params=params(0),
        name="project",
    )(hidden_in, code, stacked, bias)

    grid = (heads, nc)
    e_spec = pl.BlockSpec((1, length, local_len), lambda h, b: (h, 0, b))
    inv_spec = pl.BlockSpec((1, 1, 1, local_len), lambda h, b: (h, b, 0, 0))
    ctx_spec = pl.BlockSpec((local_len, 128), lambda h, b: (b, h))
    q_spec = pl.BlockSpec((1, local_len, 128), lambda h, b: (h, b, 0))
    kv_spec = pl.BlockSpec((1, length, 128), lambda h, b: (h, 0, 0))

    def whole(shape):
        return pl.BlockSpec(shape, lambda h, b: (0,) * len(shape))

    e, ctx, inv = pl.pallas_call(
        attend_kernel,
        grid=grid,
        out_shape=(
            struct((heads, length, length), BF),
            struct((length, heads * 128), BF),
            struct((heads, nc, 1, local_len), F32),
        ),
        in_specs=[q_spec, kv_spec, whole((nc, 1, local_len))],
        out_specs=(e_spec, ctx_spec, inv_spec),
        scratch_shapes=[
            pltpu.VMEM((length, 128), BF),
            pltpu.VMEM((128, length), BF),
            pltpu.VMEM((length, 128), F32),
        ],
        compiler_params=params(),
        name="attend",
    )(q, kv, code)

    full = pltpu.VMEM((nc, 4, piece, width), BF)
    own = pltpu.VMEM((nc, piece, width), BF)
    own32 = pltpu.VMEM((nc, piece, width), F32)
    reduce_bufs = [
        pltpu.VMEM((nc, 2, 2, piece, width), BF),
        pltpu.VMEM((nc, 2, piece, width), BF),
        own,
        own,
    ]
    rows_ff = pltpu.VMEM((nc, local_len, ff), BF)
    ga, hid, gfi, dff, small = pl.pallas_call(
        functools.partial(feed_kernel, ns, nc),
        out_shape=(
            struct((nc, 4, piece, width), BF),
            struct((nc, piece, width), BF),
            struct((nc, piece, width), F32),
            struct((4, shard_rows, width // 2), BF),
            struct((8, width), F32),
        ),
        in_specs=vmem(7),
        out_specs=vmem(5),
        scratch_shapes=[
            pltpu.VMEM((ns, shard_rows, ff), BF),
            pltpu.VMEM((ns, shard_rows, ff), BF),
            own,
            own,
        ]
        + reduce_bufs * 3
        + [
            full,
            full,
            rows_ff,
            pltpu.VMEM((nc, local_len, ff), F32),
            rows_ff,
            own32,
            own32,
            pltpu.VMEM((nc, piece, 1), F32),
            own32,
            pltpu.VMEM((2, ns, shard_rows, ff), BF),
            pltpu.VMEM((2, wide, shard_rows, ff), BF),
        ]
        + [DMA((4,))]
        + [DMA((2, wide))] * 2
        + [DMA((nc - 1,))] * 2
        + [DMA((nc,))] * 2
        + [DMA((2, wide))] * 2
        + [DMA((3, nc))] * (TP_REDUCE + TP_GATHER),
        compiler_params=params(1),
        name="feed",
    )(
        ctx.reshape(nc, local_len, heads * 128),
        wf[heads].reshape(width, 384),
        xf,
        out_grad,
        up_weight,
        down_t,
        vectors,
    )

    dqo, back, qb = pl.pallas_call(
        attend_back_kernel,
        grid=grid,
        out_shape=(
            struct((heads + 1, width, 384), BF),
            struct((length, width), BF),
            struct((heads, 1, 384), F32),
        ),
        in_specs=[
            whole((length, width)),
            whole((heads + 1, ns, shard_rows, 384)),
            whole((length, heads * 128)),
            whole((length, width)),
            whole((nc, 1, local_len)),
            e_spec,
            inv_spec,
            ctx_spec,
            q_spec,
            kv_spec,
        ],
        out_specs=(
            whole((heads + 1, width, 384)),
            whole((length, width)),
            whole((heads, 1, 384)),
        ),
        scratch_shapes=[
            pltpu.VMEM((heads, length, 128), BF),
            pltpu.VMEM((length, 128), BF),
            pltpu.VMEM((length, 128), F32),
            pltpu.VMEM((length, 128), F32),
            pltpu.VMEM((length, 384), BF),
            pltpu.VMEM((length, width), F32),
        ],
        compiler_params=params(),
        name="attend_back",
    )(
        ga.reshape(length, width),
        wf,
        ctx,
        xf.reshape(length, width),
        code,
        e,
        inv,
        ctx,
        q,
        kv,
    )

    chunks = 4 + heads + 1
    line = pltpu.VMEM((chunks, shard_rows, 384), BF)
    wide_small = 3 * 384
    ing, hid, dw, small = pl.pallas_call(
        functools.partial(finish_kernel, ns, nc),
        out_shape=(
            struct((nc, 4, piece, width), BF),
            struct((nc, 4, piece, width), BF),
            struct((chunks, shard_rows, 384), BF),
            struct((8, wide_small), F32),
        ),
        in_specs=vmem(7),
        out_specs=vmem(4),
        scratch_shapes=[
            pltpu.VMEM((nc, 2, piece, width), BF),
            own,
            own,
            own,
            line,
            line,
            line,
            line,
            pltpu.VMEM((heads + 1, wide, shard_rows, 384), BF),
            pltpu.VMEM((4, 8, wide_small), F32),
            pltpu.VMEM((nc, 8, wide_small), F32),
            pltpu.VMEM((ns, 8, wide_small), F32),
        ]
        + [DMA((2,))]
        + [DMA((heads + 1, wide))] * 2
        + [DMA((chunks,))] * 8
        + [DMA((nc,))] * 2
        + [DMA((1,))]
        + [DMA((2,))] * 2
        + [DMA((nc - 1,))] * 2
        + [DMA((wide,))] * 2
        + [DMA((nc,))] * TP_REDUCE
        + [DMA((2, nc))] * TP_GATHER,
        compiler_params=params(2),
        name="finish",
    )(
        back.reshape(nc, 2, 2, piece, width),
        gfi,
        hid,
        dff,
        dqo.reshape(heads + 1, ns, shard_rows, 384),
        small,
        qb,
    )

    hidden_out = hid.reshape(nc, local_len, width)
    in_grad = ing.reshape(nc, local_len, width).astype(F32)
    grads = dw.astype(F32)
    up_grad = jnp.concatenate([grads[0], grads[1]], axis=1)
    down_grad = jnp.concatenate([grads[2], grads[3]], axis=1).T
    split = grads[4:7].reshape(heads, shard_rows, 6, HEAD).transpose(2, 1, 0, 3)
    split = split.reshape(6, shard_rows, part)
    out_w = grads[7].reshape(shard_rows, heads, 2, HEAD)[:, :, 1].reshape(shard_rows, part).T
    vec = small[7].reshape(heads, 6, HEAD).transpose(1, 0, 2).reshape(6, part)
    return (
        hidden_out,
        in_grad,
        split[:4],
        split[4:],
        vec[:4],
        vec[5],
        out_w,
        small[4, :width],
        small[0, :width],
        small[1, :width],
        up_grad,
        small[6, :width],
        down_grad,
        small[5, :width],
        small[2, :width],
        small[3, :width],
    )


def solution(mesh):
    in_specs = (
        P("shard", "ctx", None),
        P("shard", "ctx"),
        P("shard", "ctx"),
        P(None, "shard", "tp"),
        P(None, "shard", "tp"),
        P(None, "tp"),
        P("tp"),
        P("tp", "shard"),
        P(),
        P(),
        P(),
        P("shard", "tp"),
        P("tp"),
        P("tp", "shard"),
        P(),
        P(),
        P(),
        P("shard", "ctx", None),
    )
    out_specs = (
        P("shard", "ctx", None),
        P("shard", "ctx", None),
        P(None, "shard", "tp"),
        P(None, "shard", "tp"),
        P(None, "tp"),
        P("tp"),
        P("tp", "shard"),
        P(),
        P(),
        P(),
        P("shard", "tp"),
        P("tp"),
        P("tp", "shard"),
        P(),
        P(),
        P(),
    )
    return jax.shard_map(
        per_device, mesh=mesh, in_specs=in_specs, out_specs=out_specs, check_vma=False
    )
```

time: 825 us -> 325 us (0.39)
  waiting for transfers between devices: 371 us -> 0 us
  Pallas kernels: 0 us -> 285 us
  matrix products: 212 us -> 0 us
  blocking collectives: 85 us -> 0 us
  other arithmetic: 64.1 us -> 5.63 us
  local copies, waits for them, and re-layouts: 66 us -> 32.6 us
  between operations: 15 us -> 0.79 us
    pallas_call x0 -> x5, Pallas kernels: none -> 285 us  [the longest x1 117 us: per_device(): pl.pallas_call(functools.partial(finish_kernel, ns, nc), out_shape=(struc...]
    dot_general x48 -> x0, matrix products: 212 us -> none  [the longest x3 23.9 us: attend_back(): jnp.einsum('sqk,sqc->skc', grad_entity, queries[1], preferred_element_typ...]
    psum x5 -> x0, waiting for transfers between devices: 201 us -> none  [the longest x1 77.6 us: per_device(): lax.psum(weight_grads[0].astype(jnp.bfloat16), 'ctx').astype(jnp.float32)]
    all_gather x4 -> x0, waiting for transfers between devices: 68.7 us -> none  [the longest x1 35.8 us: per_device(): keys_all = lax.all_gather(by_head(key_values), 'ctx', axis=3, tiled=True)]
    unnamed x19 -> x0, waiting for transfers between devices: 50.9 us -> none
    reduce_scatter x2 -> x0, waiting for transfers between devices: 50.6 us -> none  [the longest x1 28.4 us: per_device(): lax.psum_scatter(grad_kv_heads.astype(jnp.bfloat16), 'ctx', scatter_dimen...]
    all_gather x4 -> x0, blocking collectives: 43.7 us -> none  [the longest x1 13.6 us: per_device(): lax.all_gather(token_type, 'ctx', axis=1, tiled=True)]
    psum x1 -> x0, blocking collectives: 41.3 us -> none  [per_device(): lax.psum((jnp.sum(grad_first_own * first_hat_own, axis=0), jnp.sum(grad_f...]
  transfers between devices with their start and end apart: 15 -> 0, of which waited for: 12 -> 0; matrix products, arithmetic and copies ran while one was open for 14% -> 0% of each run, Pallas kernels for 0% -> 0%
where the time goes in v1:
time: 325 us; the launch traced here: 324 us
  Pallas kernels  285 us (88%)
  local copies, waits for them, and re-layouts  32.6 us (10%)
  other arithmetic  5.63 us (2%)
    pallas_call x1, Pallas kernels, per_device(): pl.pallas_call(functools.partial(finish_kernel, ns, nc), out_shape=(struc...  117 us
    pallas_call x1, Pallas kernels, per_device(): pl.pallas_call(functools.partial(feed_kernel, ns, nc), out_shape=(struct(...  89.9 us
    pallas_call x1, Pallas kernels, per_device(): pl.pallas_call(functools.partial(project_kernel, ns, nc), out_shape=(stru...  36.8 us
    pallas_call x1, Pallas kernels, per_device(): pl.pallas_call(attend_back_kernel, grid=grid, out_shape=(struct((heads +...  26.4 us
    pallas_call x1, Pallas kernels, per_device(): pl.pallas_call(attend_kernel, grid=grid, out_shape=(struct((heads, length...  14.6 us

profile of v1, /device:TPU:0, one launch (start us, length us, event | category | flops | bytes accessed | tf_op | source)
XLA Modules:
  0.0 324.0 jit_solution(14588736691700280867)
XLA Ops:
  0.6 0.0 copy-start.4
  0.7 0.0 copy-start.5
  0.7 0.0 copy-start.3
  0.7 0.1 pad.10.clone
  0.8 0.9 concatenate.23
  1.6 0.7 stack.25
  2.3 0.7 stack.26
  3.0 0.7 stack.27
  3.7 0.7 stack.28
  4.4 0.7 stack.29
  5.1 0.7 stack.30
  5.7 0.7 stack.31
  6.4 0.6 stack.32.vec_ref
  7.1 0.7 fusion
  7.8 0.6 reshape.86.code_ref
  8.4 0.8 concatenate.22
  9.2 0.1 maximum_bitcast_fusion.1
  9.2 0.7 reshape.91.bias_ref
  9.9 0.9 pad.4
  10.9 0.2 copy.53
  11.1 0.0 copy-done.4
  11.1 1.1 copy.55
  12.2 0.0 copy-done.5
  12.2 0.0 copy-done.3
  12.2 0.1 pad_maximum_fusion.2
  12.3 0.1 copy.51
  12.4 2.4 copy.52
  14.7 1.1 pad_maximum_fusion.w_ref
  15.9 36.8 %project.1 = (bf16[4,4,64,768]{3,2,1,0:T(8,128)(2,1)}, bf16[3,1024,128]{2,1,0:T(8,128)(2,1)}, bf16[3,1024,128]{2,1,0:T(8,128)(2,1)}, f32[4,1,256]{2,1,0:T(1,128)}, bf16[4,2,384,384]{3,2,1,0:T(8,128)(2,1)}) custom-call(bf16[4,256,768]{2,1,0:T(8,128)(2,1)} %x_ref.1, f32[4,1,256]{2,1,0:T(1,128)} %reshape.86.code_ref, ...), custom_call_target="tpu_custom_call" | custom-call | tf_op jit(solution)/shard_map/project/pallas_call | solution.py:912
  52.7 1.9 slice.70
  54.7 14.6 %attend.1 = (bf16[3,1024,1024]{2,1,0:T(8,128)(2,1)}, bf16[1024,384]{1,0:T(8,128)(2,1)}, f32[3,4,1,256]{3,2,1,0:T(1,128)}) custom-call(bf16[3,1024,128]{2,1,0:T(8,128)(2,1)} %get-tuple-element.36.q_ref, bf16[3,1024,128]{2,1,0:T(8,128)(2,1)} %get-tuple-element.37.kv_ref, f32[4,1,256]{2,1,0:T(1,128)} %get-tuple-element.38.code_ref), custom_call_target="tpu_custom_call" | custom-call | tf_op jit(solution)/shard_map/attend/pallas_call | solution.py:941
  69.2 89.9 %feed.1 = (bf16[4,4,64,768]{3,2,1,0:T(8,128)(2,1)}, bf16[4,64,768]{2,1,0:T(8,128)(2,1)}, f32[4,64,768]{2,1,0:T(8,128)}, bf16[4,384,384]{2,1,0:T(8,128)(2,1)}, f32[8,768]{1,0:T(8,128)}) custom-call(bf16[4,256,384]{2,1,0:T(8,128)(2,1)} %bitcast.44, bf16[768,384]{1,0:T(8,128)(2,1)} %bitcast.52, bf16[4,4,64,768]{3,2,1,0:T(8,128)(2,1)} %get-tuple-element.41.xf_ref, ...), custom_call_target="tpu_custom_call" | custom-call | tf_op jit(solution)/shard_map/feed/pallas_call | solution.py:970
  159.1 26.4 %attend_back.1 = (bf16[4,768,384]{2,1,0:T(8,128)(2,1)}, bf16[1024,768]{1,0:T(8,128)(2,1)}, f32[3,1,384]{2,1,0:T(1,128)}) custom-call(bf16[1024,768]{1,0:T(8,128)(2,1)} %bitcast.55, bf16[4,2,384,384]{3,2,1,0:T(8,128)(2,1)} %get-tuple-element.40.wf_ref, bf16[1024,384]{1,0:T(8,128)(2,1)} %get-tuple-element.39.ctxf_ref.ctx_ref, bf16[1024,768]{1,0:T(8,128)(2,1)} %bitcast.47, ...), custom_call_target="tpu_custom_call" | custom-call | tf_op jit(solution)/shard_map/attend_back/pallas_call | solution.py:1019
  185.5 117.3 %finish.1 = (bf16[4,4,64,768]{3,2,1,0:T(8,128)(2,1)}, bf16[4,4,64,768]{3,2,1,0:T(8,128)(2,1)}, bf16[8,384,384]{2,1,0:T(8,128)(2,1)}, f32[8,1152]{1,0:T(8,128)}) custom-call(bf16[4,2,2,64,768]{4,3,2,1,0:T(8,128)(2,1)} %bitcast.54, f32[4,64,768]{2,1,0:T(8,128)} %get-tuple-element.46.gfi_ref, bf16[4,64,768]{2,1,0:T(8,128)(2,1)} %get-tuple-element.47.hid_ref, ...), custom_call_target="tpu_custom_call" | custom-call | tf_op jit(solution)/shard_map/finish/pallas_call | solution.py:1070
  302.8 0.0 copy-start
  302.8 0.9 slice_reduce_fusion
  303.8 1.7 slice_reduce_fusion.1
  305.4 0.1 reshape_squeeze.13
  305.5 0.7 slice.78
  306.2 0.6 squeeze.36
  306.9 1.0 slice.98
  307.9 0.2 copy.60
  308.1 0.7 slice.99
  308.8 0.0 copy-done
  308.8 1.3 slice.93
  310.2 2.9 copy.56
  313.0 1.1 slice.95
  314.1 1.4 slice.94
  315.5 1.1 copy.57
  316.6 0.9 copy.58
  317.4 0.3 convert_element_type.17
  317.8 0.2 slice_bitcast_fusion.1
  317.9 1.3 pad_maximum_fusion.1
  319.2 0.0 copy-start.2
  319.2 1.4 copy.61
  320.6 0.2 copy-done.2
  320.8 0.0 copy-start.1
  320.8 2.0 bitcast_convert_fusion
  322.8 0.0 copy-done.1
  322.8 1.1 copy.65
  (4 shorter events, 0.0 us)
Async XLA Ops:
  0.6 10.4 %copy-start.4 = (bf16[768,384]{1,0:T(8,128)(2,1)S(1)}, bf16[768,384]{1,0:T(8,128)(2,1)}, u32[]{:S(2)}) copy-start(bf16[768,384]{1,0:T(8,128)(2,1)} %param.31) | copy-start | bytes 1769476
  0.7 11.5 %copy-start.5 = (bf16[2,384,192]{1,2,0:T(8,128)(2,1)S(1)}, bf16[2,384,192]{1,2,0:T(8,128)(2,1)}, u32[]{:S(2)}) copy-start(bf16[2,384,192]{1,2,0:T(8,128)(2,1)} %param.22) | copy-start | bytes 884740
  0.7 11.5 %copy-start.3 = (bf16[4,384,192]{1,2,0:T(8,128)(2,1)S(1)}, bf16[4,384,192]{1,2,0:T(8,128)(2,1)}, u32[]{:S(2)}) copy-start(bf16[4,384,192]{1,2,0:T(8,128)(2,1)} %param.21) | copy-start | bytes 1769476
  302.8 6.0 %copy-start = (bf16[8,384,384]{2,1,0:T(8,128)(2,1)S(1)}, bf16[8,384,384]{2,1,0:T(8,128)(2,1)}, u32[]{:S(2)}) copy-start(bf16[8,384,384]{2,1,0:T(8,128)(2,1)} %get-tuple-element.54) | copy-start | bytes 7077892
  319.2 1.6 copy-start.2
  320.8 2.0 copy-start.1

commit v2 on v1

--- a/solution.py
+++ b/solution.py
@@ -164,23 +164,17 @@
 
 
 def project_kernel(
-    ns, nc, x_ref, code_ref, w_ref, bias_ref,
-    xf_ref, q_ref, kv_ref, codef_ref, wf_ref,
-    local, zs, zr, ds, dr, ws, wr, *tp_sems,
+    ns, nc, x_ref, type_ref, seg_ref, qw_ref, kvw_ref, ow_ref, dn_ref, qb_ref, vb_ref,
+    xf_ref, q_ref, kv_ref, codef_ref, wf_ref, wo_ref, dnt_ref,
+    wst, code, bias, local, zs, zr, ds, dr, ws, wr, *tp_sems,
 ):
     p = Place(ns, nc)
     piece = x_ref.shape[1] // 4
+    heads = wst.shape[0] - 1
+    for j in range(nc):
+        label = seg_ref[j : j + 1]
+        code[j] = jnp.where(type_ref[j : j + 1] == 0, label, -label).astype(F32)
     greet([p.mate, p.ymate] + p.zpeers + p.xpeers)
-    heads = w_ref.shape[0] - 1
-
-    def weight(h, r):
-        return remote(
-            w_ref.at[h], wf_ref.at[h, p.s], ws.at[h, r], wr.at[h, r], p.xpeers[r]
-        )
-
-    for h in range(heads + 1):
-        for r in range(ns - 1):
-            weight(h, r).start()
     mine = pl.ds(p.t * piece, piece)
 
     def x_send(k):
@@ -191,22 +185,54 @@
 
     def code_send(k):
         peer = p.zpeers[k]
-        return remote(code_ref.at[peer["ctx"]], codef_ref.at[p.c], ds.at[k], dr.at[k], peer)
+        return remote(code.at[peer["ctx"]], codef_ref.at[p.c], ds.at[k], dr.at[k], peer)
+
+    def gathered(h, src):
+        return wf_ref.at[h, src] if h < heads else wo_ref.at[src]
+
+    def weight(h, r):
+        return remote(wst.at[h], gathered(h, p.s), ws.at[h, r], wr.at[h, r], p.xpeers[r])
+
+    def weight_landed(h):
+        for r in range(ns - 1):
+            landed = gathered(h, lax.rem(p.s + ns - 1 - r, ns))
+            remote(landed, landed, ws.at[h, r], wr.at[h, r], p.xpeers[r]).wait_recv()
 
     for k in range(nc - 1):
         x_send(k).start()
+    own = x_ref.at[p.c, mine]
+    gather = TpGather(p, xf_ref, tp_sems)
+    gather.send(p.c, 0, own)
+    for h in range(heads):
+        cols = slice(h * HEAD, (h + 1) * HEAD)
+        parts = [qw_ref[k, cols] for k in range(4)] + [kvw_ref[k, cols] for k in range(2)]
+        wst[h] = jnp.concatenate(parts, axis=0).T
+        for r in range(ns - 1):
+            weight(h, r).start()
+    turned = ow_ref[...].T
+    blank = jnp.zeros((turned.shape[0], HEAD), BF)
+    parts = []
+    for h in range(heads):
+        parts += [blank, turned[:, h * HEAD : (h + 1) * HEAD]]
+    wst[heads] = jnp.concatenate(parts, axis=1)
+    for r in range(ns - 1):
+        weight(heads, r).start()
     for k in range(nc - 1):
         code_send(k).start()
-    own = x_ref.at[p.c, mine]
     copies = [
         pltpu.make_async_copy(own, xf_ref.at[p.c, p.t], local.at[0]),
-        pltpu.make_async_copy(code_ref.at[p.c], codef_ref.at[p.c], local.at[1]),
-        pltpu.make_async_copy(w_ref, wf_ref.at[:, p.s], local.at[2]),
+        pltpu.make_async_copy(code.at[p.c], codef_ref.at[p.c], local.at[1]),
+        pltpu.make_async_copy(wst.at[pl.ds(0, heads)], wf_ref.at[:, p.s], local.at[2]),
+        pltpu.make_async_copy(wst.at[heads], wo_ref.at[p.s], local.at[3]),
     ]
     for copy in copies:
         copy.start()
-    gather = TpGather(p, xf_ref, tp_sems)
-    gather.send(p.c, 0, own)
+    vb = vb_ref[...].reshape(1, -1)
+    for h in range(heads):
+        cols = slice(h * HEAD, (h + 1) * HEAD)
+        parts = [qb_ref[k : k + 1, cols] for k in range(4)]
+        bias[h] = jnp.concatenate(parts + [jnp.zeros((1, HEAD), F32), vb[:, cols]], axis=1)
+    dnt_ref[...] = dn_ref[...].T
     blocks = [lax.rem(p.c + nc - k, nc) for k in range(nc)]
     for k in range(1, nc):
         landed = xf_ref.at[blocks[k], p.t]
@@ -224,13 +250,11 @@
     width = xf_ref.shape[-1]
     rows = 4 * piece
     for h in range(heads):
-        for r in range(ns - 1):
-            landed = wf_ref.at[h, lax.rem(p.s + ns - 1 - r, ns)]
-            remote(landed, landed, ws.at[h, r], wr.at[h, r], p.xpeers[r]).wait_recv()
+        weight_landed(h)
 
         def project(b, carry):
             x = xf_ref[b].reshape(rows, width)
-            out = nn(x, wf_ref[h].reshape(width, 384)) + bias_ref[h]
+            out = nn(x, wf_ref[h].reshape(width, 384)) + bias[h]
             entity = column(codef_ref[b]) < 0.0
             at = pl.ds(pl.multiple_of(b * rows, rows), rows)
             chosen = jnp.where(entity, out[:, 128:256], out[:, 0:128])
@@ -239,9 +263,7 @@
             return carry
 
         lax.fori_loop(0, nc, project, 0)
-    for r in range(ns - 1):
-        landed = wf_ref.at[heads, lax.rem(p.s + ns - 1 - r, ns)]
-        remote(landed, landed, ws.at[heads, r], wr.at[heads, r], p.xpeers[r]).wait_recv()
+    weight_landed(heads)
     for h in range(heads + 1):
         for r in range(ns - 1):
             weight(h, r).wait_send()
@@ -287,7 +309,7 @@
     inverse = 1.0 / jnp.maximum(jnp.sum(exponent, axis=0, keepdims=True), 1.0)
     exponent = exponent.astype(BF)
     e_ref[0] = exponent
-    inv_ref[0, 0] = inverse
+    inv_ref[0] = inverse
     ctx_ref[...] = (nn(vt[...], exponent) * inverse).T.astype(BF)
 
 
@@ -313,13 +335,16 @@
 
 
 def feed_kernel(
-    ns, nc, ctx_ref, wo_ref, xf_ref, og_ref, wu_ref, wd_ref, vec_ref,
-    ga_ref, hid_ref, gfi_ref, dff_ref, small_ref,
-    wuf, wdf, ogo, hsend,
-    t0, m0, s0, y0, t1, m1, s1, y1, t2, m2, s2, y2,
-    low, gf, active, slope, gup, fo, fh, fi, gs, dst, xr,
-    local, ws, wr, os, orr, hs, hr, xs, xrs, *tp_sems,
+    ns, nc, ctx_ref, wo_ref, xf_ref, og_ref, wu_ref, wd_ref, *rest,
 ):
+    vecs, rest = rest[:7], rest[7:]
+    (
+        ga_ref, hid_ref, gfi_ref, dff_ref, small_ref,
+        wuf, wdf, ogo, hsend,
+        t0, m0, s0, y0, t1, m1, s1, y1, t2, m2, s2, y2,
+        low, gf, active, slope, gup, fo, fh, fi, gs, dst, xr,
+        local, ws, wr, os, orr, hs, hr, xs, xrs, *tp_sems,
+    ) = rest
     p = Place(ns, nc)
     piece, width = xf_ref.shape[2:]
     rows = 4 * piece
@@ -359,7 +384,7 @@
         for i, buf in enumerate((low, gf, ga_ref))
     ]
     out_bias, gain1, bias1, up_bias, down_bias, gain2, bias2 = (
-        vec_ref[i : i + 1] for i in range(7)
+        ref[...].reshape(1, -1) for ref in vecs
     )
 
     def put(terms, b, values):
@@ -369,7 +394,7 @@
         small_ref[row : row + 1] += total(values)
 
     def out_project(b):
-        put(t0, b, nt(ctx_ref[b], wo_ref[...]))
+        put(t0, b, nt(ctx_ref[b], wo_ref[...].reshape(width, -1)))
         sums[0].send(b)
 
     def norm_one(b):
@@ -498,15 +523,15 @@
         return carry
 
     lax.fori_loop(0, SKEWS_C[-1] + nc, slot, 0)
-    half = width // 2
+    lanes = width // 128
     for a in (1, 0):
         grad = dst[a, p.s].astype(F32)
         for r in range(ns - 1):
             grad_send(a, r).wait_recv()
             grad = grad + xr[a, r].astype(F32)
         grad = grad.astype(BF)
-        dff_ref[2 * a] = grad[:, :half]
-        dff_ref[2 * a + 1] = grad[:, half:]
+        for j in range(lanes):
+            dff_ref[lanes * a + j] = grad[:, j * 128 : (j + 1) * 128]
     for k in range(1, nc):
         src = lax.rem(p.c + k, nc)
         landed = hid_ref.at[src]
@@ -525,98 +550,47 @@
             shares[i].drain(b, b)
 
 
-def attend_back_kernel(
-    ga_ref, wf_ref, ctxf_ref, xf_ref, code_ref, e_ref, inv_ref, ctx_ref, q_ref, kv_ref,
-    dw_ref, back_ref, qb_ref,
-    dctx, kcat, dkey, dval, dqkv, back,
-):
-    h, b = pl.program_id(0), pl.program_id(1)
-    heads = pl.num_programs(0)
-    nblk, rows = code_ref.shape[0], code_ref.shape[2]
-    width = xf_ref.shape[1]
-
-    @pl.when((h == 0) & (b == 0))
-    def _():
-        out = wf_ref[3].reshape(width, 384)
-        for i in range(3):
-            dctx[i] = nn(ga_ref[...], out[:, i * 128 : (i + 1) * 128]).astype(BF)
-        dw_ref[3] = tn(ga_ref[...], ctxf_ref[...]).astype(BF)
-        back[...] = jnp.zeros_like(back)
-
-    low_half = lax.broadcasted_iota(jnp.int32, (rows, 128), 1) < HEAD
-
-    @pl.when(b == 0)
-    def _():
-        for j in range(nblk):
-            at = slice(j * rows, (j + 1) * rows)
-            entity = column(code_ref[j]) < 0.0
-            kv = kv_ref[0, at].astype(F32)
-            keep = jnp.where(low_half, kv, pltpu.roll(kv, HEAD, 1))
-            kcat[at] = jnp.where(low_half == entity, 0.0, keep).astype(BF)
-        dkey[...] = jnp.zeros_like(dkey)
-        dval[...] = jnp.zeros_like(dval)
-
-    at = pl.ds(pl.multiple_of(b * rows, rows), rows)
-    grad_ctx = dctx[h, at].astype(F32).T * inv_ref[0, 0]
-    row_dot = jnp.sum(grad_ctx * ctx_ref[...].astype(F32).T, axis=0, keepdims=True)
-    grad_ctx = grad_ctx.astype(BF)
-    weight = e_ref[0]
-    grad = nn(kv_ref[0], grad_ctx)
-    grad = (weight.astype(F32) * (grad - row_dot)).astype(BF)
-    dval[...] += nt(weight, grad_ctx)
-    dkey[...] += nn(grad, q_ref[0])
-    grad_q = tn(kcat[...], grad).T * HEAD ** (-0.5)
-    entity = column(code_ref[b]) < 0.0
-    dqkv[at, 0:128] = jnp.where(entity, 0.0, grad_q).astype(BF)
-    dqkv[at, 128:256] = jnp.where(entity, grad_q, 0.0).astype(BF)
-
-    @pl.when(b == nblk - 1)
-    def _():
-        for j in range(nblk):
-            part = slice(j * rows, (j + 1) * rows)
-            entity = column(code_ref[j]) < 0.0
-            grad_k = dkey[part]
-            grad_k = jnp.where(entity, pltpu.roll(grad_k, HEAD, 1), grad_k)
-            dqkv[part, 256:384] = jnp.where(low_half, grad_k, dval[part]).astype(BF)
-        grads = dqkv[...]
-        qb_ref[h] = total(grads.astype(F32))
-        dw_ref[h] = tn(xf_ref[...], grads).astype(BF)
-        back[...] += nt(grads, wf_ref[h].reshape(width, 384))
-
-        @pl.when(h == heads - 1)
-        def _():
-            back_ref[...] = back[...].astype(BF)
-
-
-def finish_kernel(
-    ns, nc, back_ref, gfi_ref, hid_ref, dff_ref, dqo_ref, smc_ref, qb_ref,
+FF_CHUNKS = 12
+OUT_CHUNKS = 2
+HEAD_CHUNKS = 3
+OWN_LAG, PASS_LAG = 3, 6
+
+
+def back_kernel(
+    ns, nc, ga_ref, wf_ref, wo_ref, ctx_ref, xf_ref, code_ref, inv_ref, q_ref, kv_ref, gfi_ref, hid_ref,
+    dff_ref, smc_ref, e_ref,
     ing_ref, hidf_ref, dw_ref, sm_ref,
+    dctx, kcat, dkey, dval, dqkv, back, qb, ebuf, dqo, terms,
     m0, s0, y0, ig, zo, zr, zq, zsum, xr, smt, smz, smx,
-    local, xs, xrs, z1s, z1r, z2s, z2r, z3s, z3r, z4s, z4r, gs, gr, hl, ss, sr, szs, szr, sxs, sxr,
-    *tp_sems,
+    local, es, xs, xrs, z1s, z1r, z2s, z2r, z3s, z3r, z4s, z4r, gs, gr, hl,
+    ss, sr, szs, szr, sxs, sxr, *tp_sems,
 ):
     p = Place(ns, nc)
     piece, width = gfi_ref.shape[1:]
+    rows = 4 * piece
+    length = nc * rows
+    heads = q_ref.shape[0]
+    steps = heads * nc
     chunks = dw_ref.shape[0]
-    first = dff_ref.shape[0]
+
+    def fetch(i):
+        return pltpu.make_async_copy(e_ref.at[i], ebuf.at[lax.rem(i, 2)], es.at[lax.rem(i, 2)])
+
+    fetch(0).start()
     greet([p.mate, p.ymate] + p.zpeers + p.xpeers)
 
-    def x_send(k, r):
+
+    def x_send(lo, n, r):
         peer = p.xpeers[r]
-        return remote(dqo_ref.at[k, peer["shard"]], xr.at[k, r], xs.at[k, r], xrs.at[k, r], peer)
-
-    back_sum = TpReduce(p, back_ref, m0, s0, y0, [tp_sems[j] for j in range(4)])
-    for b in range(nc):
-        back_sum.send(b)
-    for k in range(chunks - first):
-        for r in range(ns - 1):
-            x_send(k, r).start()
-    copies = [
-        pltpu.make_async_copy(dff_ref, zo.at[pl.ds(0, first)], local.at[0]),
-        pltpu.make_async_copy(hid_ref, hidf_ref.at[:, p.t], local.at[1]),
-    ]
-    for copy in copies:
-        copy.start()
+        return remote(
+            dqo.at[pl.ds(lo, n), peer["shard"]],
+            xr.at[r, pl.ds(lo, n)],
+            xs.at[lo, r],
+            xrs.at[lo, r],
+            peer,
+        )
+
+    back_sum = TpReduce(p, terms, m0, s0, y0, [tp_sems[j] for j in range(4)])
     share_h = TpGather(p, hidf_ref, [tp_sems[4 + j].at[0] for j in range(6)])
     share_g = TpGather(p, ing_ref, [tp_sems[4 + j].at[1] for j in range(6)])
 
@@ -641,50 +615,72 @@
     def owns(k):
         return lax.rem(k + p.c, 2) == 1
 
-    def line_start(k):
-        @pl.when(k == 0)
-        def _():
-            copies[0].wait()
-
-        @pl.when(k >= first)
-        def _():
-            j = k - first
-            grad = dqo_ref[j, p.s].astype(F32)
-            for r in range(ns - 1):
-                x_send(j, r).wait_recv()
-                grad = grad + xr[j, r].astype(F32)
-            zo[k] = grad.astype(BF)
-
+    def line_start(lo, n):
+        for k in range(lo, lo + n):
+            if k >= FF_CHUNKS:
+                j = k - FF_CHUNKS
+                grad = dqo[j, p.s].astype(F32)
+                for r in range(ns - 1):
+                    if k == lo:
+                        x_send(j, n, r).wait_recv()
+                    grad = grad + xr[r, j].astype(F32)
+                zo[k] = grad.astype(BF)
+
+            @pl.when(outer)
+            def _(k=k):
+                to_inner(k).start()
+
+    def line_in(k):
+        to_inner(k).wait_recv()
+
+        @pl.when(jnp.logical_not(owns(k)))
+        def _():
+            zsum[k] = (zo[k].astype(F32) + zr[k].astype(F32)).astype(BF)
+            to_owner(k).start()
+
+    def line_own(k):
+        @pl.when(owns(k))
+        def _():
+            to_owner(k).wait_recv()
+            dw_ref[k] = (zo[k].astype(F32) + zr[k].astype(F32) + zq[k].astype(F32)).astype(BF)
+            to_other(k).start()
+            to_outer(k).start()
+
+    def line_pass(k):
+        @pl.when(jnp.logical_not(owns(k)))
+        def _():
+            to_other(k).wait_recv()
+            to_outer(k).start()
+
+    def line_to(lo, hi):
+        @pl.when(inner)
+        def _():
+            for k in range(lo, hi):
+                if k < chunks:
+                    line_in(k)
+                if 0 <= k - OWN_LAG < chunks:
+                    line_own(k - OWN_LAG)
+                if 0 <= k - PASS_LAG < chunks:
+                    line_pass(k - PASS_LAG)
+
+    def line_end(k):
         @pl.when(outer)
         def _():
-            to_inner(k).start()
-
-    def line_in(k):
+            to_outer(k).wait_recv()
+            to_inner(k).wait_send()
+
         @pl.when(inner)
         def _():
-            to_inner(k).wait_recv()
+            @pl.when(owns(k))
+            def _():
+                to_other(k).wait_send()
 
             @pl.when(jnp.logical_not(owns(k)))
             def _():
-                zsum[k] = (zo[k].astype(F32) + zr[k].astype(F32)).astype(BF)
-                to_owner(k).start()
-
-    def line_out(k):
-        @pl.when(inner)
-        def _():
-            @pl.when(owns(k))
-            def _():
-                to_owner(k).wait_recv()
-                dw_ref[k] = (zo[k].astype(F32) + zr[k].astype(F32) + zq[k].astype(F32)).astype(BF)
-                to_other(k).start()
-
-            @pl.when(jnp.logical_not(owns(k)))
-            def _():
-                to_other(k).wait_recv()
-
-            to_outer(k).start()
-
-    at = p.c
+                to_owner(k).wait_send()
+
+            to_outer(k).wait_send()
+
 
     def small_tp(i, peer):
         return remote(smt.at[2 * i], smt.at[2 * i + 1], ss.at[i], sr.at[i], peer)
@@ -695,7 +691,7 @@
         return smt[2 * i] + jnp.where(shared, smt[2 * i + 1], 0.0)
 
     def small_z(k):
-        return remote(smz.at[at], smz.at[at], szs.at[k], szr.at[k], p.zpeers[k])
+        return remote(smz.at[p.c], smz.at[p.c], szs.at[k], szr.at[k], p.zpeers[k])
 
     def small_x(r):
         return remote(smx.at[p.s], smx.at[p.s], sxs.at[r], sxr.at[r], p.xpeers[r])
@@ -703,8 +699,8 @@
     def small_zero():
         smt[0] = jnp.zeros_like(smt[0])
         smt[0, :, 0:width] = smc_ref[...]
-        for h in range(qb_ref.shape[0]):
-            smt[0, 7:8, h * 384 : (h + 1) * 384] = qb_ref[h]
+        for h in range(heads):
+            smt[0, 7:8, h * 384 : (h + 1) * 384] = qb[h]
         small_tp(0, p.mate).start()
 
     def small_one():
@@ -714,7 +710,7 @@
 
     def small_two():
         small_tp(1, p.ymate).wait_recv()
-        smz[at] = small_fold(1)
+        smz[p.c] = small_fold(1)
         for k in range(nc - 1):
             small_z(k).start()
 
@@ -738,6 +734,7 @@
             value = value + smx[r]
         sm_ref[...] = value
 
+
     def grad_send(b):
         return remote(ig.at[b], ing_ref.at[p.c, p.t], gs.at[b], gr.at[p.c], {"ctx": b})
 
@@ -755,83 +752,185 @@
     order = [lax.rem(p.c + k, nc) for k in range(nc)]
 
     def grad_share(k):
-        q = lax.rem(p.c + k, nc)
-
-        @pl.when(k > 0)
-        def _():
+        q = order[k]
+        if k > 0:
             landed = ing_ref.at[q, p.t]
             remote(landed, landed, gs.at[q], gr.at[q], {"ctx": q}).wait_recv()
-            share_g.send(q, k)
-
-        @pl.when(k == 0)
-        def _():
+        else:
             pltpu.make_async_copy(ig.at[p.c], ing_ref.at[p.c, p.t], hl.at[0]).wait()
-            share_g.send(q, k)
+        share_g.send(q, k)
+
 
     for b in range(nc):
         share_h.send(b, b, hid_ref.at[b])
-    small_zero()
-    for k in range(first):
-        line_start(k)
+    keep = pltpu.make_async_copy(hid_ref, hidf_ref.at[:, p.t], local.at[0])
+    keep.start()
+    zo[0:FF_CHUNKS] = dff_ref[...]
+    line_start(0, FF_CHUNKS)
+    grad_attn = ga_ref[...].reshape(length, width)
+    out = wo_ref[...].reshape(width, heads * 128)
+    for i in range(heads):
+        dctx[i] = nn(grad_attn, out[:, i * 128 : (i + 1) * 128]).astype(BF)
+
+    def put_grad(lo, n, value):
+        for j in range(n):
+            dqo[lo + j] = value[:, j * 128 : (j + 1) * 128].reshape(dqo.shape[1:])
+        for r in range(ns - 1):
+            x_send(lo, n, r).start()
+
+    value = tn(grad_attn, ctx_ref[...]).astype(BF)
+    value = [value[:, i * 128 + HEAD : (i + 1) * 128] for i in range(heads)]
+    put_grad(0, OUT_CHUNKS, jnp.concatenate(value + [jnp.zeros_like(value[0])], axis=1))
+    back[...] = jnp.zeros_like(back)
+    low_half = lax.broadcasted_iota(jnp.int32, (rows, 128), 1) < HEAD
+
+    def attend_step(i):
+        h, b = i // nc, lax.rem(i, nc)
+        fetch(i).wait()
+
+        @pl.when(i + 1 < steps)
+        def _():
+            fetch(i + 1).start()
+
+        @pl.when(b == 0)
+        def _():
+            for j in range(nc):
+                at = slice(j * rows, (j + 1) * rows)
+                entity = column(code_ref[j]) < 0.0
+                kv = kv_ref[h, at].astype(F32)
+                kept = jnp.where(low_half, kv, pltpu.roll(kv, HEAD, 1))
+                kcat[at] = jnp.where(low_half == entity, 0.0, kept).astype(BF)
+            dkey[...] = jnp.zeros_like(dkey)
+            dval[...] = jnp.zeros_like(dval)
+
+        at = pl.ds(pl.multiple_of(b * rows, rows), rows)
+        lanes = pl.ds(pl.multiple_of(h * 128, 128), 128)
+        grad_ctx = dctx[h, at].astype(F32).T * inv_ref[i]
+        row_dot = jnp.sum(grad_ctx * ctx_ref[at, lanes].astype(F32).T, axis=0, keepdims=True)
+        grad_ctx = grad_ctx.astype(BF)
+        weight = ebuf[lax.rem(i, 2)]
+        grad = nn(kv_ref[h], grad_ctx)
+        grad = (weight.astype(F32) * (grad - row_dot)).astype(BF)
+        dval[...] += nt(weight, grad_ctx)
+        dkey[...] += nn(grad, q_ref[h, at])
+        grad_q = tn(kcat[...], grad).T * HEAD ** (-0.5)
+        entity = column(code_ref[b]) < 0.0
+        dqkv[at, 0:128] = jnp.where(entity, 0.0, grad_q).astype(BF)
+        dqkv[at, 128:256] = jnp.where(entity, grad_q, 0.0).astype(BF)
+
+        @pl.when(b == nc - 1)
+        def _():
+            for j in range(nc):
+                part = slice(j * rows, (j + 1) * rows)
+                entity = column(code_ref[j]) < 0.0
+                grad_k = dkey[part]
+                grad_k = jnp.where(entity, pltpu.roll(grad_k, HEAD, 1), grad_k)
+                dqkv[part, 256:384] = jnp.where(low_half, grad_k, dval[part]).astype(BF)
+            w = wf_ref[h].reshape(width, 384)
+
+            @pl.when(h < heads - 1)
+            def _():
+                back[...] += nt(dqkv[...], w)
+
+            @pl.when(h == heads - 1)
+            def _():
+                for j in range(nc):
+                    part = slice(j * rows, (j + 1) * rows)
+                    value = back[part] + nt(dqkv[part], w)
+                    terms[j] = value.astype(BF).reshape(2, 2, piece, width)
+                    back_sum.send(j)
+
+            grads = dqkv[...]
+            value = tn(xf_ref[...].reshape(length, width), grads).astype(BF)
+            put_grad(OUT_CHUNKS + HEAD_CHUNKS * h, HEAD_CHUNKS, value)
+            qb[h] = total(grads.astype(F32))
+
+    groups = [(FF_CHUNKS, OUT_CHUNKS)]
+    groups += [
+        (FF_CHUNKS + OUT_CHUNKS + HEAD_CHUNKS * h, HEAD_CHUNKS) for h in range(heads)
+    ]
+    reached = [0]
+
+    def line(upto):
+        line_to(reached[0], upto)
+        reached[0] = upto
+
+    def forward_hidden():
+        for b in range(nc):
+            share_h.forward(b, b)
+
+    def hand(k):
+        share_g.forward(order[k], k)
+
+    events = {
+        0: lambda: line(1),
+        2: lambda: line(2),
+        3: lambda: line(3),
+        5: lambda: (line(4), forward_hidden(), line_start(*groups[0])),
+        7: lambda: line(5),
+        8: lambda: line(6),
+        9: lambda: line_start(*groups[1]),
+        10: lambda: line(7),
+        11: lambda: line(8),
+    }
+
+    def slot(i, carry):
+        attend_step(i)
+        for when, action in events.items():
+
+            @pl.when(i == when)
+            def _(action=action):
+                action()
+
+        return carry
+
+    lax.fori_loop(0, steps, slot, 0)
     for b in range(nc):
         back_sum.across(b)
+    small_zero()
+    line_start(*groups[2])
+    line(9)
+    grad_own(0)
+    line(10)
+    grad_own(1)
+    line(11)
+    grad_own(2)
     small_one()
-    for b in range(nc):
-        grad_own(b)
+    line(12)
+    grad_own(3)
+    line_start(*groups[3])
+    line(13)
     small_two()
-    for k in range(first):
-        line_in(k)
-    for b in range(nc):
-        share_h.forward(b, b)
-    for k in range(nc):
-        grad_share(k)
+    line(14)
+    grad_share(0)
+    grad_share(1)
+    line(15)
+    grad_share(2)
+    hand(0)
+    grad_share(3)
+    hand(1)
     small_three()
-    for k in range(first):
-        line_out(k)
-        line_start(k + first)
-    for k in range(nc):
-        share_g.forward(order[k], k)
+    line(16)
+    hand(2)
+    hand(3)
     small_four()
-    for k in range(first, chunks):
-        line_in(k)
-    for k in range(first, chunks):
-        line_out(k)
+    line(chunks + PASS_LAG)
     for b in range(nc):
         share_h.arrive(b, b)
         share_g.arrive(order[b], b)
-
-    def line_end(k, carry):
-        @pl.when(outer)
-        def _():
-            to_outer(k).wait_recv()
-            to_inner(k).wait_send()
-
-        @pl.when(inner)
-        def _():
-            @pl.when(owns(k))
-            def _():
-                to_other(k).wait_send()
-
-            @pl.when(jnp.logical_not(owns(k)))
-            def _():
-                to_owner(k).wait_send()
-
-            to_outer(k).wait_send()
-
-        return carry
-
-    lax.fori_loop(0, chunks, line_end, 0)
-    copies[1].wait()
-    for k in range(chunks - first):
+    for k in range(chunks):
+        line_end(k)
+    keep.wait()
+    for lo, n in groups:
         for r in range(ns - 1):
-            x_send(k, r).wait_send()
+            x_send(lo - FF_CHUNKS, n, r).wait_send()
     for b in range(nc):
         back_sum.drain(b)
         share_h.drain(b, b, hid_ref.at[b])
         share_g.drain(order[b], b)
 
         @pl.when(b != p.c)
-        def _():
+        def _(b=b):
             grad_send(b).wait_send()
 
     small_tp(0, p.mate).wait_send()
@@ -840,6 +939,47 @@
         small_z(k).wait_send()
     for r in range(ns - 1):
         small_x(r).wait_send()
+
+
+def deliver_kernel(
+    ing_ref, hid_ref, dw_ref, sm_ref,
+    hidden_ref, grad_ref, qw_ref, kvw_ref, qb_ref, vb_ref, ow_ref, uw_ref, dn_ref, *vec_refs,
+):
+    hidden_ref[...] = hid_ref[...]
+    grad_ref[...] = ing_ref[...].astype(F32)
+
+    @pl.when(pl.program_id(0) == 0)
+    def _():
+        def wide(lo, n):
+            return jnp.concatenate([dw_ref[lo + j].astype(F32) for j in range(n)], axis=1)
+
+        uw_ref[...] = wide(0, 6)
+        dn_ref[...] = wide(6, 6).T
+        heads = qb_ref.shape[1] // HEAD
+        ow_ref[...] = wide(FF_CHUNKS, OUT_CHUNKS)[:, : heads * HEAD].T
+        first = FF_CHUNKS + OUT_CHUNKS
+        grads = [wide(first + HEAD_CHUNKS * h, HEAD_CHUNKS).T for h in range(heads)]
+        small = sm_ref[...]
+        for k in range(6):
+            cols = slice(k * HEAD, (k + 1) * HEAD)
+            part = jnp.concatenate([grad[cols] for grad in grads], axis=0)
+            vec = jnp.concatenate(
+                [
+                    small[7:8, h * 384 + k * HEAD : h * 384 + (k + 1) * HEAD]
+                    for h in range(heads)
+                ],
+                axis=1,
+            )
+            if k < 4:
+                qw_ref[k] = part
+                qb_ref[k : k + 1] = vec
+            else:
+                kvw_ref[k - 4] = part
+            if k == 5:
+                vb_ref[...] = vec.reshape(-1)
+        width = uw_ref.shape[1]
+        for i, ref in enumerate(vec_refs):
+            ref[...] = small[i : i + 1, :width].reshape(-1)
 
 
 def vmem(count):
@@ -895,42 +1035,47 @@
     assert seqs == nc == 4 and heads == 3 and ff == width
     wide = ns - 1
 
-    code = jnp.where(token_type == 0, segment, -segment).astype(F32).reshape(nc, 1, local_len)
-    stacked = jnp.concatenate([query_weight, key_value_weight], axis=0)
-    stacked = stacked.reshape(6, shard_rows, heads, HEAD).transpose(2, 1, 0, 3)
-    stacked = stacked.reshape(heads, shard_rows, 6 * HEAD)
-    out_t = out_weight.T.reshape(shard_rows, heads, 1, HEAD)
-    out_t = jnp.pad(out_t, ((0, 0), (0, 0), (1, 0), (0, 0))).reshape(1, shard_rows, 2 * part)
-    stacked = jnp.concatenate([stacked, out_t], axis=0)
-    bias = jnp.concatenate([query_bias, jnp.zeros((1, part), F32), value_bias[None]], axis=0)
-    bias = bias.reshape(6, heads, HEAD).transpose(1, 0, 2).reshape(heads, 1, 6 * HEAD)
-    vectors = jnp.stack(
-        [out_bias, norm1_gain, norm1_bias, up_bias, down_bias, norm2_gain, norm2_bias, norm2_bias]
-    )
-    down_t = down_weight.T
-
-    xf, q, kv, code, wf = pl.pallas_call(
+    mixed = OUT_CHUNKS + HEAD_CHUNKS * heads
+    line = (FF_CHUNKS + mixed, shard_rows, 128)
+    xf, q, kv, code, wf, wo, down_t = pl.pallas_call(
         functools.partial(project_kernel, ns, nc),
         out_shape=(
             struct((nc, 4, piece, width), BF),
             struct((heads, length, 128), BF),
             struct((heads, length, 128), BF),
             struct((nc, 1, local_len), F32),
-            struct((heads + 1, ns, shard_rows, 384), BF),
+            struct((heads, ns, shard_rows, 384), BF),
+            struct((ns, shard_rows, 384), BF),
+            struct((shard_rows, ff), BF),
         ),
-        in_specs=vmem(4),
-        out_specs=vmem(5),
-        scratch_shapes=[DMA((3,))]
+        in_specs=vmem(9),
+        out_specs=vmem(7),
+        scratch_shapes=[
+            pltpu.VMEM((heads + 1, shard_rows, 384), BF),
+            pltpu.VMEM((nc, 1, local_len), F32),
+            pltpu.VMEM((heads, 1, 384), F32),
+            DMA((4,)),
+        ]
         + [DMA((nc - 1,))] * 4
         + [DMA((heads + 1, wide))] * 2
         + [DMA((nc,))] * TP_GATHER,
         compiler_params=params(0),
         name="project",
-    )(hidden_in, code, stacked, bias)
+    )(
+        hidden_in,
+        token_type,
+        segment,
+        query_weight.swapaxes(1, 2),
+        key_value_weight.swapaxes(1, 2),
+        out_weight,
+        down_weight,
+        query_bias,
+        value_bias,
+    )
 
     grid = (heads, nc)
-    e_spec = pl.BlockSpec((1, length, local_len), lambda h, b: (h, 0, b))
-    inv_spec = pl.BlockSpec((1, 1, 1, local_len), lambda h, b: (h, b, 0, 0))
+    e_spec = pl.BlockSpec((1, length, local_len), lambda h, b: (h * nc + b, 0, 0))
+    inv_spec = pl.BlockSpec((1, 1, local_len), lambda h, b: (h * nc + b, 0, 0))
     ctx_spec = pl.BlockSpec((local_len, 128), lambda h, b: (b, h))
     q_spec = pl.BlockSpec((1, local_len, 128), lambda h, b: (h, b, 0))
     kv_spec = pl.BlockSpec((1, length, 128), lambda h, b: (h, 0, 0))
@@ -942,9 +1087,9 @@
         attend_kernel,
         grid=grid,
         out_shape=(
-            struct((heads, length, length), BF),
+            struct((heads * nc, length, local_len), BF),
             struct((length, heads * 128), BF),
-            struct((heads, nc, 1, local_len), F32),
+            struct((heads * nc, 1, local_len), F32),
         ),
         in_specs=[q_spec, kv_spec, whole((nc, 1, local_len))],
         out_specs=(e_spec, ctx_spec, inv_spec),
@@ -973,10 +1118,10 @@
             struct((nc, 4, piece, width), BF),
             struct((nc, piece, width), BF),
             struct((nc, piece, width), F32),
-            struct((4, shard_rows, width // 2), BF),
+            struct((FF_CHUNKS, shard_rows, 128), BF),
             struct((8, width), F32),
         ),
-        in_specs=vmem(7),
+        in_specs=vmem(13),
         out_specs=vmem(5),
         scratch_shapes=[
             pltpu.VMEM((ns, shard_rows, ff), BF),
@@ -1008,39 +1153,32 @@
         name="feed",
     )(
         ctx.reshape(nc, local_len, heads * 128),
-        wf[heads].reshape(width, 384),
+        wo,
         xf,
         out_grad,
         up_weight,
         down_t,
-        vectors,
+        out_bias,
+        norm1_gain,
+        norm1_bias,
+        up_bias,
+        down_bias,
+        norm2_gain,
+        norm2_bias,
     )
 
-    dqo, back, qb = pl.pallas_call(
-        attend_back_kernel,
-        grid=grid,
+    chunks = pltpu.VMEM(line, BF)
+    wide_small = heads * 384
+    ing, hid, dw, small = pl.pallas_call(
+        functools.partial(back_kernel, ns, nc),
         out_shape=(
-            struct((heads + 1, width, 384), BF),
-            struct((length, width), BF),
-            struct((heads, 1, 384), F32),
+            struct((nc, 4, piece, width), BF),
+            struct((nc, 4, piece, width), BF),
+            struct(line, BF),
+            struct((8, wide_small), F32),
         ),
-        in_specs=[
-            whole((length, width)),
-            whole((heads + 1, ns, shard_rows, 384)),
-            whole((length, heads * 128)),
-            whole((length, width)),
-            whole((nc, 1, local_len)),
-            e_spec,
-            inv_spec,
-            ctx_spec,
-            q_spec,
-            kv_spec,
-        ],
-        out_specs=(
-            whole((heads + 1, width, 384)),
-            whole((length, width)),
-            whole((heads, 1, 384)),
-        ),
+        in_specs=vmem(13) + [pl.BlockSpec(memory_space=pl.ANY)],
+        out_specs=vmem(4),
         scratch_shapes=[
             pltpu.VMEM((heads, length, 128), BF),
             pltpu.VMEM((length, 128), BF),
@@ -1048,52 +1186,23 @@
             pltpu.VMEM((length, 128), F32),
             pltpu.VMEM((length, 384), BF),
             pltpu.VMEM((length, width), F32),
-        ],
-        compiler_params=params(),
-        name="attend_back",
-    )(
-        ga.reshape(length, width),
-        wf,
-        ctx,
-        xf.reshape(length, width),
-        code,
-        e,
-        inv,
-        ctx,
-        q,
-        kv,
-    )
-
-    chunks = 4 + heads + 1
-    line = pltpu.VMEM((chunks, shard_rows, 384), BF)
-    wide_small = 3 * 384
-    ing, hid, dw, small = pl.pallas_call(
-        functools.partial(finish_kernel, ns, nc),
-        out_shape=(
-            struct((nc, 4, piece, width), BF),
-            struct((nc, 4, piece, width), BF),
-            struct((chunks, shard_rows, 384), BF),
-            struct((8, wide_small), F32),
-        ),
-        in_specs=vmem(7),
-        out_specs=vmem(4),
-        scratch_shapes=[
-            pltpu.VMEM((nc, 2, piece, width), BF),
-            own,
-            own,
-            own,
-            line,
-            line,
-            line,
-            line,
-            pltpu.VMEM((heads + 1, wide, shard_rows, 384), BF),
+            pltpu.VMEM((heads, 1, 384), F32),
+            pltpu.VMEM((2, length, local_len), BF),
+            pltpu.VMEM((mixed, ns, shard_rows, 128), BF),
+        ]
+        + reduce_bufs
+        + [own]
+        + [chunks] * 4
+        + [
+            pltpu.VMEM((wide, mixed, shard_rows, 128), BF),
             pltpu.VMEM((4, 8, wide_small), F32),
             pltpu.VMEM((nc, 8, wide_small), F32),
             pltpu.VMEM((ns, 8, wide_small), F32),
+            DMA((1,)),
+            DMA((2,)),
         ]
-        + [DMA((2,))]
-        + [DMA((heads + 1, wide))] * 2
-        + [DMA((chunks,))] * 8
+        + [DMA((mixed, wide))] * 2
+        + [DMA((FF_CHUNKS + mixed,))] * 8
         + [DMA((nc,))] * 2
         + [DMA((1,))]
         + [DMA((2,))] * 2
@@ -1102,43 +1211,90 @@
         + [DMA((nc,))] * TP_REDUCE
         + [DMA((2, nc))] * TP_GATHER,
         compiler_params=params(2),
-        name="finish",
-    )(
-        back.reshape(nc, 2, 2, piece, width),
-        gfi,
-        hid,
-        dff,
-        dqo.reshape(heads + 1, ns, shard_rows, 384),
-        small,
+        name="back",
+    )(ga, wf, wo, ctx, xf, code, inv, q, kv, gfi, hid, dff, small, e)
+
+    def block(*shape):
+        return pl.BlockSpec(shape, lambda i: (i,) + (0,) * (len(shape) - 1))
+
+    def fixed(*shape):
+        return pl.BlockSpec(shape, lambda i: (0,) * len(shape))
+
+    def vector(size):
+        return pl.BlockSpec((size,), lambda i: (0,))
+
+    (
+        hidden_out,
+        in_grad,
+        qw,
+        kvw,
         qb,
-    )
-
-    hidden_out = hid.reshape(nc, local_len, width)
-    in_grad = ing.reshape(nc, local_len, width).astype(F32)
-    grads = dw.astype(F32)
-    up_grad = jnp.concatenate([grads[0], grads[1]], axis=1)
-    down_grad = jnp.concatenate([grads[2], grads[3]], axis=1).T
-    split = grads[4:7].reshape(heads, shard_rows, 6, HEAD).transpose(2, 1, 0, 3)
-    split = split.reshape(6, shard_rows, part)
-    out_w = grads[7].reshape(shard_rows, heads, 2, HEAD)[:, :, 1].reshape(shard_rows, part).T
-    vec = small[7].reshape(heads, 6, HEAD).transpose(1, 0, 2).reshape(6, part)
+        vb,
+        ow,
+        uw,
+        dn,
+        gain1,
+        bias1,
+        gain2,
+        bias2,
+        ob,
+        db,
+        ub,
+    ) = pl.pallas_call(
+        deliver_kernel,
+        grid=(nc,),
+        out_shape=(
+            struct((nc, local_len, width), BF),
+            struct((nc, local_len, width), F32),
+            struct((4, part, shard_rows), F32),
+            struct((2, part, shard_rows), F32),
+            struct((4, part), F32),
+            struct((part,), F32),
+            struct((part, shard_rows), F32),
+            struct((shard_rows, ff), F32),
+            struct((ff, shard_rows), F32),
+        )
+        + (struct((width,), F32),) * 7,
+        in_specs=[
+            block(1, local_len, width),
+            block(1, local_len, width),
+            fixed(*line),
+            fixed(8, wide_small),
+        ],
+        out_specs=[
+            block(1, local_len, width),
+            block(1, local_len, width),
+            fixed(4, part, shard_rows),
+            fixed(2, part, shard_rows),
+            fixed(4, part),
+            vector(part),
+            fixed(part, shard_rows),
+            fixed(shard_rows, ff),
+            fixed(ff, shard_rows),
+        ]
+        + [vector(width)] * 7,
+        compiler_params=pltpu.CompilerParams(
+            vmem_limit_bytes=VMEM_LIMIT, dimension_semantics=("arbitrary",)
+        ),
+        name="deliver",
+    )(ing.reshape(nc, local_len, width), hid.reshape(nc, local_len, width), dw, small)
     return (
         hidden_out,
         in_grad,
-        split[:4],
-        split[4:],
-        vec[:4],
-        vec[5],
-        out_w,
-        small[4, :width],
-        small[0, :width],
-        small[1, :width],
-        up_grad,
-        small[6, :width],
-        down_grad,
-        small[5, :width],
-        small[2, :width],
-        small[3, :width],
+        qw.swapaxes(1, 2),
+        kvw.swapaxes(1, 2),
+        qb,
+        vb,
+        ow,
+        ob,
+        gain1,
+        bias1,
+        uw,
+        ub,
+        dn,
+        db,
+        gain2,
+        bias2,
     )
 
 

time: 325 us -> 248 us (0.76)
  Pallas kernels: 285 us -> 247 us
  local copies, waits for them, and re-layouts: 32.6 us -> 0 us
  other arithmetic: 5.63 us -> 0 us
    pallas_call x3, Pallas kernels: 158 us -> 119 us  [the longest x1 97.1 us: per_device(): pl.pallas_call(functools.partial(back_kernel, ns, nc), out_shape=(struct(...]
    slice x15 -> x0, local copies, waits for them, and re-layouts: 15.8 us -> none  [the longest x2 4.2 us: per_device(): split = grads[4:7].reshape(heads, shard_rows, 6, HEAD).transpose(2, 1, 0, 3)]
    another operation x10 -> x0, local copies, waits for them, and re-layouts: 5.55 us -> none  [the longest x8 5.47 us: per_device(): jnp.stack([out_bias, norm1_gain, norm1_bias, up_bias, down_bias, norm2_ga...]
    unnamed x15 -> x0, local copies, waits for them, and re-layouts: 3.86 us -> none
    reshape x4 -> x0, local copies, waits for them, and re-layouts: 3.84 us -> none  [the longest x1 2.36 us: per_device(): stacked = stacked.reshape(heads, shard_rows, 6 * HEAD)]
where the time goes in v2:
time: 248 us; the launch traced here: 247 us
  Pallas kernels  247 us (100%)
    pallas_call x1, Pallas kernels, per_device(): pl.pallas_call(functools.partial(back_kernel, ns, nc), out_shape=(struct(...  97.1 us
    pallas_call x1, Pallas kernels, per_device(): pl.pallas_call(functools.partial(feed_kernel, ns, nc), out_shape=(struct(...  90.1 us
    pallas_call x1, Pallas kernels, per_device(): pl.pallas_call(functools.partial(project_kernel, ns, nc), out_shape=(stru...  37.4 us
    pallas_call x1, Pallas kernels, per_device(): pl.pallas_call(attend_kernel, grid=grid, out_shape=(struct((heads * nc, l...  14.6 us
    pallas_call x1, Pallas kernels, per_device(): pl.pallas_call(deliver_kernel, grid=(nc,), out_shape=(struct((nc, local_l...  7.45 us

profile of v2, /device:TPU:0, one launch (start us, length us, event | category | flops | bytes accessed | tf_op | source)
XLA Modules:
  0.0 247.4 jit_solution(3803469365657567844)
XLA Ops:
  0.6 37.4 %project.1 = (bf16[4,4,64,768]{3,2,1,0:T(8,128)(2,1)}, bf16[3,1024,128]{2,1,0:T(8,128)(2,1)}, bf16[3,1024,128]{2,1,0:T(8,128)(2,1)}, f32[4,1,256]{2,1,0:T(1,128)...) custom-call(bf16[4,256,768]{2,1,0:T(8,128)(2,1)} %x_ref.1, ...), custom_call_target="tpu_custom_call" | custom-call | tf_op jit(solution)/shard_map/project/pallas_call | solution.py:1040
  38.0 14.6 %attend.1 = (bf16[12,1024,256]{2,1,0:T(8,128)(2,1)}, bf16[1024,384]{1,0:T(8,128)(2,1)}, f32[12,1,256]{2,1,0:T(1,128)}) custom-call(bf16[3,1024,128]{2,1,0:T(8,128)(2,1)} %get-tuple-element.51.q_ref, bf16[3,1024,128]{2,1,0:T(8,128)(2,1)} %get-tuple-element.52.kv_ref, f32[4,1,256]{2,1,0:T(1,128)} %get-tuple-element.53.code_ref), custom_call_target="tpu_custom_call" | custom-call | tf_op jit(solution)/shard_map/attend/pallas_call | solution.py:1086
  52.7 90.1 %feed.1 = (bf16[4,4,64,768]{3,2,1,0:T(8,128)(2,1)}, bf16[4,64,768]{2,1,0:T(8,128)(2,1)}, f32[4,64,768]{2,1,0:T(8,128)}, bf16[12,384,128]{2,1,0:T(8,128)(2,1)}, f32[8,768]{1,0:T(8,128)}) custom-call(bf16[4,256,384]{2,1,0:T(8,128)(2,1)} %bitcast.7, bf16[2,384,384]{2,1,0:T(8,128)(2,1)} %get-tuple-element.55.wo_ref, ...), custom_call_target="tpu_custom_call" | custom-call | tf_op jit(solution)/shard_map/feed/pallas_call | solution.py:1115
  142.7 97.1 %back.1 = (bf16[4,4,64,768]{3,2,1,0:T(8,128)(2,1)}, bf16[4,4,64,768]{3,2,1,0:T(8,128)(2,1)}, bf16[23,384,128]{2,1,0:T(8,128)(2,1)}, f32[8,1152]{1,0:T(8,128)}) custom-call(bf16[4,4,64,768]{3,2,1,0:T(8,128)(2,1)} %get-tuple-element.58.ga_ref, bf16[3,2,384,384]{3,2,1,0:T(8,128)(2,1)} %get-tuple-element.59.wf_ref, ...), custom_call_target="tpu_custom_call" | custom-call | tf_op jit(solution)/shard_map/back/pallas_call | solution.py:1172
  239.8 7.4 %deliver.1 = (bf16[4,256,768]{2,1,0:T(8,128)(2,1)}, f32[4,256,768]{2,1,0:T(8,128)}, f32[4,192,384]{2,1,0:T(8,128)}, f32[2,192,384]{2,1,0:T(8,128)}, f32[4,192]{1...) custom-call(bf16[4,256,768]{2,1,0:T(8,128)(2,1)} %bitcast.8, ...), custom_call_target="tpu_custom_call" | custom-call | tf_op jit(solution)/shard_map/deliver/pallas_call | solution.py:1243

commit v3 on v2

--- a/solution.py
+++ b/solution.py
@@ -332,22 +332,42 @@
 
 
 SKEWS_C = (0, 1, 3, 4, 5, 6, 8, 9, 10, 11, 13, 14, 15)
-
-
-def feed_kernel(
+FF_CHUNKS = 12
+OUT_CHUNKS = 2
+HEAD_CHUNKS = 3
+OWN_LAG, PASS_LAG = 3, 6
+
+
+def layer_kernel(
     ns, nc, ctx_ref, wo_ref, xf_ref, og_ref, wu_ref, wd_ref, *rest,
 ):
     vecs, rest = rest[:7], rest[7:]
     (
-        ga_ref, hid_ref, gfi_ref, dff_ref, small_ref,
+        wf_ref, code_ref, inv_ref, q_ref, kv_ref, e_ref,
+        ing_ref, hidf_ref, dw_ref, sm_ref,
+        ga, hid, gfi, small,
         wuf, wdf, ogo, hsend,
         t0, m0, s0, y0, t1, m1, s1, y1, t2, m2, s2, y2,
-        low, gf, active, slope, gup, fo, fh, fi, gs, dst, xr,
-        local, ws, wr, os, orr, hs, hr, xs, xrs, *tp_sems,
+        low, gf, active, slope, gup, fo, fh, fi, gs,
+        dctx, kcat, dkey, dval, dqkv, qb, ebuf, dqo,
+        ig, zo, zr, zq, xr, smt, smz, smx,
+        local, ws, wr, os, orr, hs, hr,
+        es, xs, xrs, z1s, z1r, z2s, z2r, z3s, z3r, z4s, z4r, igs, igr,
+        ss, sr, szs, szr, sxs, sxr, *tp_sems,
     ) = rest
     p = Place(ns, nc)
     piece, width = xf_ref.shape[2:]
     rows = 4 * piece
+    length = nc * rows
+    heads = q_ref.shape[0]
+    steps = heads * nc
+    chunks = dw_ref.shape[0]
+    back = slope
+
+    def fetch(i):
+        return pltpu.make_async_copy(e_ref.at[i], ebuf.at[lax.rem(i, 2)], es.at[lax.rem(i, 2)])
+
+    fetch(0).start()
     greet([p.mate, p.ymate] + p.zpeers + p.xpeers)
     weights = ((wu_ref, wuf), (wd_ref, wdf))
 
@@ -373,28 +393,148 @@
     ]
     for copy in copies:
         copy.start()
-    small_ref[...] = jnp.zeros_like(small_ref)
+    small[...] = jnp.zeros_like(small)
 
     sums = [
         TpReduce(p, *bufs, [tp_sems[j].at[i] for j in range(4)])
-        for i, bufs in enumerate(((t0, m0, s0, y0), (t1, m1, s1, y1), (t2, m2, s2, y2)))
+        for i, bufs in enumerate(
+            ((t0, m0, s0, y0), (t1, m1, s1, y1), (t2, m2, s2, y2), (t0, m0, s0, y0))
+        )
     ]
     shares = [
         TpGather(p, buf, [tp_sems[4 + j].at[i] for j in range(6)])
-        for i, buf in enumerate((low, gf, ga_ref))
+        for i, buf in enumerate((low, gf, ga, hidf_ref, ing_ref))
     ]
+    back_sum, share_h, share_g = sums[3], shares[3], shares[4]
     out_bias, gain1, bias1, up_bias, down_bias, gain2, bias2 = (
         ref[...].reshape(1, -1) for ref in vecs
     )
 
+
+    def x_send(lo, n, r):
+        peer = p.xpeers[r]
+        return remote(
+            dqo.at[pl.ds(lo, n), peer["shard"]],
+            xr.at[r, pl.ds(lo, n)],
+            xs.at[lo, r],
+            xrs.at[lo, r],
+            peer,
+        )
+
+    outer = (p.c == 0) | (p.c == nc - 1)
+    inner = (p.c > 0) & (p.c < nc - 1)
+    inward = {"ctx": 1 + p.c // 3}
+    outward = {"ctx": lax.rem(3 * (p.c + nc - 1), 6)}
+    across = {"ctx": lax.rem(2 * nc - 1 - p.c, nc)}
+
+    def to_inner(k):
+        return remote(zo.at[k], zr.at[k], z1s.at[k], z1r.at[k], inward)
+
+    def to_owner(k):
+        return remote(zq.at[k], zq.at[k], z2s.at[k], z2r.at[k], across)
+
+    def to_other(k):
+        return remote(dw_ref.at[k], dw_ref.at[k], z3s.at[k], z3r.at[k], across)
+
+    def to_outer(k):
+        return remote(dw_ref.at[k], dw_ref.at[k], z4s.at[k], z4r.at[k], outward)
+
+    def owns(k):
+        return lax.rem(k + p.c, 2) == 1
+
+    def line_start(lo, n):
+        for r in range(ns - 1):
+            x_send(lo, n, r).wait_recv()
+        for k in range(lo, lo + n):
+            grad = dqo[k, p.s].astype(F32)
+            for r in range(ns - 1):
+                grad = grad + xr[r, k].astype(F32)
+            zo[k] = grad.astype(BF)
+
+            @pl.when(outer)
+            def _(k=k):
+                to_inner(k).start()
+
+    def line_in(k):
+        to_inner(k).wait_recv()
+
+        @pl.when(jnp.logical_not(owns(k)))
+        def _():
+            zq[k] = (zo[k].astype(F32) + zr[k].astype(F32)).astype(BF)
+            to_owner(k).start()
+
+    def line_own(k):
+        @pl.when(owns(k))
+        def _():
+            to_owner(k).wait_recv()
+            dw_ref[k] = (zo[k].astype(F32) + zr[k].astype(F32) + zq[k].astype(F32)).astype(BF)
+            to_other(k).start()
+            to_outer(k).start()
+
+    def line_pass(k):
+        @pl.when(jnp.logical_not(owns(k)))
+        def _():
+            to_other(k).wait_recv()
+            to_outer(k).start()
+
+    reached = [0]
+
+    def line(upto):
+        lo = reached[0]
+        reached[0] = upto
+
+        @pl.when(inner)
+        def _():
+            for k in range(lo, upto):
+                if k < chunks:
+                    line_in(k)
+                if 0 <= k - OWN_LAG < chunks:
+                    line_own(k - OWN_LAG)
+                if 0 <= k - PASS_LAG < chunks:
+                    line_pass(k - PASS_LAG)
+
+    def line_end(k):
+        @pl.when(outer)
+        def _():
+            to_outer(k).wait_recv()
+            to_inner(k).wait_send()
+
+        @pl.when(inner)
+        def _():
+            @pl.when(owns(k))
+            def _():
+                to_other(k).wait_send()
+
+            @pl.when(jnp.logical_not(owns(k)))
+            def _():
+                to_owner(k).wait_send()
+
+            to_outer(k).wait_send()
+
+    sizes = [HEAD_CHUNKS] * 4 + [OUT_CHUNKS] + [HEAD_CHUNKS] * heads
+    groups = [(sum(sizes[:g]), n) for g, n in enumerate(sizes)]
+
+    def start(g):
+        line_start(*groups[g])
+
+    def put_grad(lo, n, value):
+        for j in range(n):
+            dqo[lo + j] = value[:, j * 128 : (j + 1) * 128].reshape(dqo.shape[1:])
+        for r in range(ns - 1):
+            x_send(lo, n, r).start()
+
+
     def put(terms, b, values):
         terms[b] = values.astype(BF).reshape(2, 2, piece, width)
 
     def add_small(row, values):
-        small_ref[row : row + 1] += total(values)
+        small[row : row + 1] += total(values)
+
+    def block_rows(b):
+        return pl.ds(pl.multiple_of(b * rows, rows), rows)
 
     def out_project(b):
-        put(t0, b, nt(ctx_ref[b], wo_ref[...].reshape(width, -1)))
+        put(t0, b, nt(ctx_ref[block_rows(b)], wo_ref[...].reshape(width, -1)))
         sums[0].send(b)
 
     def norm_one(b):
@@ -427,7 +567,7 @@
         sums[1].send(b)
 
     def hid_send(b):
-        return remote(hsend.at[b], hid_ref.at[p.c], hs.at[b], hr.at[p.c], {"ctx": b})
+        return remote(hsend.at[b], hid.at[p.c], hs.at[b], hr.at[p.c], {"ctx": b})
 
     def norm_two(b):
         @pl.when(b == 0)
@@ -456,7 +596,7 @@
 
         @pl.when(b == p.c)
         def _():
-            pltpu.make_async_copy(hsend.at[b], hid_ref.at[p.c], local.at[3]).start()
+            pltpu.make_async_copy(hsend.at[b], hid.at[p.c], local.at[3]).start()
 
     def feed_back(b):
         shares[1].arrive(b, b)
@@ -472,9 +612,9 @@
         add_small(0, grad * fh[b])
         add_small(1, grad)
         grad = unspread(grad, fh[b], fi[b], gain1)
-        gfi_ref[b] = grad
+        gfi[b] = grad
         grad = grad.astype(BF)
-        ga_ref[b, p.t] = grad
+        ga[b, p.t] = grad
         add_small(4, grad.astype(F32))
         shares[2].send(b, b)
 
@@ -494,19 +634,31 @@
         lambda b: shares[2].arrive(b, b),
     )
 
-    def grad_send(a, r):
-        return remote(
-            dst.at[a, p.xpeers[r]["shard"]], xr.at[a, r], xs.at[a, r], xrs.at[a, r], p.xpeers[r]
-        )
-
-    def weight_grad(a):
-        left = (low, gf)[a][...].reshape(nc * rows, width)
-        right = (gup, active)[a][...].reshape(nc * rows, -1)
-        dst[a] = tn(left, right).astype(BF).reshape(dst.shape[1:])
-        for r in range(ns - 1):
-            grad_send(a, r).start()
-
-    def slot(step, carry):
+    half = HEAD_CHUNKS * 128
+
+    def weight_grad(g):
+        left = (gf, low)[g // 2][...].reshape(length, width)
+        right = (active, gup)[g // 2][:, :, half * (g % 2) : half * (g % 2 + 1)]
+        put_grad(*groups[g], tn(left, right.reshape(length, half)).astype(BF))
+
+    def run_at(step, events):
+        for when, action in events.items():
+
+            @pl.when(step == when)
+            def _(action=action):
+                action()
+
+    full = SKEWS_C[8] + nc - 1
+    feed_events = {
+        full: lambda: (weight_grad(0), weight_grad(1)),
+        full + 1: lambda: (weight_grad(2), weight_grad(3)),
+        full + 2: lambda: start(0),
+        full + 3: lambda: line(1),
+        full + 4: lambda: (start(1), line(3)),
+        full + 5: lambda: line(4),
+    }
+
+    def feed_slot(step, carry):
         for skew, stage in zip(SKEWS_C, stages):
             b = step - skew
 
@@ -514,172 +666,10 @@
             def _(stage=stage, b=b):
                 stage(b)
 
-        for a in range(2):
-
-            @pl.when(step == SKEWS_C[8] + nc - 1 + a)
-            def _(a=a):
-                weight_grad(1 - a)
-
+        run_at(step, feed_events)
         return carry
 
-    lax.fori_loop(0, SKEWS_C[-1] + nc, slot, 0)
-    lanes = width // 128
-    for a in (1, 0):
-        grad = dst[a, p.s].astype(F32)
-        for r in range(ns - 1):
-            grad_send(a, r).wait_recv()
-            grad = grad + xr[a, r].astype(F32)
-        grad = grad.astype(BF)
-        for j in range(lanes):
-            dff_ref[lanes * a + j] = grad[:, j * 128 : (j + 1) * 128]
-    for k in range(1, nc):
-        src = lax.rem(p.c + k, nc)
-        landed = hid_ref.at[src]
-        remote(landed, landed, hs.at[src], hr.at[src], p.zpeers[k - 1]).wait_recv()
-        hid_send(src).wait_send()
-    pltpu.make_async_copy(hsend.at[p.c], hid_ref.at[p.c], local.at[3]).wait()
-    for a in range(2):
-        for r in range(ns - 1):
-            weight(a, r).wait_send()
-            grad_send(a, r).wait_send()
-    for k in range(nc - 1):
-        og_send(k).wait_send()
-    for i in range(3):
-        for b in range(nc):
-            sums[i].drain(b)
-            shares[i].drain(b, b)
-
-
-FF_CHUNKS = 12
-OUT_CHUNKS = 2
-HEAD_CHUNKS = 3
-OWN_LAG, PASS_LAG = 3, 6
-
-
-def back_kernel(
-    ns, nc, ga_ref, wf_ref, wo_ref, ctx_ref, xf_ref, code_ref, inv_ref, q_ref, kv_ref, gfi_ref, hid_ref,
-    dff_ref, smc_ref, e_ref,
-    ing_ref, hidf_ref, dw_ref, sm_ref,
-    dctx, kcat, dkey, dval, dqkv, back, qb, ebuf, dqo, terms,
-    m0, s0, y0, ig, zo, zr, zq, zsum, xr, smt, smz, smx,
-    local, es, xs, xrs, z1s, z1r, z2s, z2r, z3s, z3r, z4s, z4r, gs, gr, hl,
-    ss, sr, szs, szr, sxs, sxr, *tp_sems,
-):
-    p = Place(ns, nc)
-    piece, width = gfi_ref.shape[1:]
-    rows = 4 * piece
-    length = nc * rows
-    heads = q_ref.shape[0]
-    steps = heads * nc
-    chunks = dw_ref.shape[0]
-
-    def fetch(i):
-        return pltpu.make_async_copy(e_ref.at[i], ebuf.at[lax.rem(i, 2)], es.at[lax.rem(i, 2)])
-
-    fetch(0).start()
-    greet([p.mate, p.ymate] + p.zpeers + p.xpeers)
-
-
-    def x_send(lo, n, r):
-        peer = p.xpeers[r]
-        return remote(
-            dqo.at[pl.ds(lo, n), peer["shard"]],
-            xr.at[r, pl.ds(lo, n)],
-            xs.at[lo, r],
-            xrs.at[lo, r],
-            peer,
-        )
-
-    back_sum = TpReduce(p, terms, m0, s0, y0, [tp_sems[j] for j in range(4)])
-    share_h = TpGather(p, hidf_ref, [tp_sems[4 + j].at[0] for j in range(6)])
-    share_g = TpGather(p, ing_ref, [tp_sems[4 + j].at[1] for j in range(6)])
-
-    outer = (p.c == 0) | (p.c == nc - 1)
-    inner = (p.c > 0) & (p.c < nc - 1)
-    inward = {"ctx": 1 + p.c // 3}
-    outward = {"ctx": lax.rem(3 * (p.c + nc - 1), 6)}
-    across = {"ctx": lax.rem(2 * nc - 1 - p.c, nc)}
-
-    def to_inner(k):
-        return remote(zo.at[k], zr.at[k], z1s.at[k], z1r.at[k], inward)
-
-    def to_owner(k):
-        return remote(zsum.at[k], zq.at[k], z2s.at[k], z2r.at[k], across)
-
-    def to_other(k):
-        return remote(dw_ref.at[k], dw_ref.at[k], z3s.at[k], z3r.at[k], across)
-
-    def to_outer(k):
-        return remote(dw_ref.at[k], dw_ref.at[k], z4s.at[k], z4r.at[k], outward)
-
-    def owns(k):
-        return lax.rem(k + p.c, 2) == 1
-
-    def line_start(lo, n):
-        for k in range(lo, lo + n):
-            if k >= FF_CHUNKS:
-                j = k - FF_CHUNKS
-                grad = dqo[j, p.s].astype(F32)
-                for r in range(ns - 1):
-                    if k == lo:
-                        x_send(j, n, r).wait_recv()
-                    grad = grad + xr[r, j].astype(F32)
-                zo[k] = grad.astype(BF)
-
-            @pl.when(outer)
-            def _(k=k):
-                to_inner(k).start()
-
-    def line_in(k):
-        to_inner(k).wait_recv()
-
-        @pl.when(jnp.logical_not(owns(k)))
-        def _():
-            zsum[k] = (zo[k].astype(F32) + zr[k].astype(F32)).astype(BF)
-            to_owner(k).start()
-
-    def line_own(k):
-        @pl.when(owns(k))
-        def _():
-            to_owner(k).wait_recv()
-            dw_ref[k] = (zo[k].astype(F32) + zr[k].astype(F32) + zq[k].astype(F32)).astype(BF)
-            to_other(k).start()
-            to_outer(k).start()
-
-    def line_pass(k):
-        @pl.when(jnp.logical_not(owns(k)))
-        def _():
-            to_other(k).wait_recv()
-            to_outer(k).start()
-
-    def line_to(lo, hi):
-        @pl.when(inner)
-        def _():
-            for k in range(lo, hi):
-                if k < chunks:
-                    line_in(k)
-                if 0 <= k - OWN_LAG < chunks:
-                    line_own(k - OWN_LAG)
-                if 0 <= k - PASS_LAG < chunks:
-                    line_pass(k - PASS_LAG)
-
-    def line_end(k):
-        @pl.when(outer)
-        def _():
-            to_outer(k).wait_recv()
-            to_inner(k).wait_send()
-
-        @pl.when(inner)
-        def _():
-            @pl.when(owns(k))
-            def _():
-                to_other(k).wait_send()
-
-            @pl.when(jnp.logical_not(owns(k)))
-            def _():
-                to_owner(k).wait_send()
-
-            to_outer(k).wait_send()
+    lax.fori_loop(0, SKEWS_C[-1] + nc, feed_slot, 0)
 
 
     def small_tp(i, peer):
@@ -698,7 +688,7 @@
 
     def small_zero():
         smt[0] = jnp.zeros_like(smt[0])
-        smt[0, :, 0:width] = smc_ref[...]
+        smt[0, :, 0:width] = small[...]
         for h in range(heads):
             smt[0, 7:8, h * 384 : (h + 1) * 384] = qb[h]
         small_tp(0, p.mate).start()
@@ -736,10 +726,10 @@
 
 
     def grad_send(b):
-        return remote(ig.at[b], ing_ref.at[p.c, p.t], gs.at[b], gr.at[p.c], {"ctx": b})
+        return remote(ig.at[b], ing_ref.at[p.c, p.t], igs.at[b], igr.at[p.c], {"ctx": b})
 
     def grad_own(b):
-        ig[b] = (gfi_ref[b] + back_sum.result(b)).astype(BF)
+        ig[b] = (gfi[b] + back_sum.result(b)).astype(BF)
 
         @pl.when(b != p.c)
         def _():
@@ -747,7 +737,7 @@
 
         @pl.when(b == p.c)
         def _():
-            pltpu.make_async_copy(ig.at[b], ing_ref.at[p.c, p.t], hl.at[0]).start()
+            pltpu.make_async_copy(ig.at[b], ing_ref.at[p.c, p.t], local.at[4]).start()
 
     order = [lax.rem(p.c + k, nc) for k in range(nc)]
 
@@ -755,32 +745,31 @@
         q = order[k]
         if k > 0:
             landed = ing_ref.at[q, p.t]
-            remote(landed, landed, gs.at[q], gr.at[q], {"ctx": q}).wait_recv()
+            remote(landed, landed, igs.at[q], igr.at[q], {"ctx": q}).wait_recv()
         else:
-            pltpu.make_async_copy(ig.at[p.c], ing_ref.at[p.c, p.t], hl.at[0]).wait()
+            pltpu.make_async_copy(ig.at[p.c], ing_ref.at[p.c, p.t], local.at[4]).wait()
         share_g.send(q, k)
 
 
+    for k in range(1, nc):
+        src = lax.rem(p.c + k, nc)
+        landed = hid.at[src]
+        remote(landed, landed, hs.at[src], hr.at[src], p.zpeers[k - 1]).wait_recv()
+        hid_send(src).wait_send()
+    pltpu.make_async_copy(hsend.at[p.c], hid.at[p.c], local.at[3]).wait()
     for b in range(nc):
-        share_h.send(b, b, hid_ref.at[b])
-    keep = pltpu.make_async_copy(hid_ref, hidf_ref.at[:, p.t], local.at[0])
+        share_h.send(b, b, hid.at[b])
+    keep = pltpu.make_async_copy(hid, hidf_ref.at[:, p.t], local.at[5])
     keep.start()
-    zo[0:FF_CHUNKS] = dff_ref[...]
-    line_start(0, FF_CHUNKS)
-    grad_attn = ga_ref[...].reshape(length, width)
+    for b in range(nc):
+        sums[0].drain(b)
+    grad_attn = ga[...].reshape(length, width)
     out = wo_ref[...].reshape(width, heads * 128)
     for i in range(heads):
         dctx[i] = nn(grad_attn, out[:, i * 128 : (i + 1) * 128]).astype(BF)
-
-    def put_grad(lo, n, value):
-        for j in range(n):
-            dqo[lo + j] = value[:, j * 128 : (j + 1) * 128].reshape(dqo.shape[1:])
-        for r in range(ns - 1):
-            x_send(lo, n, r).start()
-
     value = tn(grad_attn, ctx_ref[...]).astype(BF)
     value = [value[:, i * 128 + HEAD : (i + 1) * 128] for i in range(heads)]
-    put_grad(0, OUT_CHUNKS, jnp.concatenate(value + [jnp.zeros_like(value[0])], axis=1))
+    put_grad(*groups[4], jnp.concatenate(value + [jnp.zeros_like(value[0])], axis=1))
     back[...] = jnp.zeros_like(back)
     low_half = lax.broadcasted_iota(jnp.int32, (rows, 128), 1) < HEAD
 
@@ -803,7 +792,7 @@
             dkey[...] = jnp.zeros_like(dkey)
             dval[...] = jnp.zeros_like(dval)
 
-        at = pl.ds(pl.multiple_of(b * rows, rows), rows)
+        at = block_rows(b)
         lanes = pl.ds(pl.multiple_of(h * 128, 128), 128)
         grad_ctx = dctx[h, at].astype(F32).T * inv_ref[i]
         row_dot = jnp.sum(grad_ctx * ctx_ref[at, lanes].astype(F32).T, axis=0, keepdims=True)
@@ -830,30 +819,19 @@
 
             @pl.when(h < heads - 1)
             def _():
-                back[...] += nt(dqkv[...], w)
+                for j in range(nc):
+                    back[j] += nt(dqkv[j * rows : (j + 1) * rows], w)
 
             @pl.when(h == heads - 1)
             def _():
                 for j in range(nc):
-                    part = slice(j * rows, (j + 1) * rows)
-                    value = back[part] + nt(dqkv[part], w)
-                    terms[j] = value.astype(BF).reshape(2, 2, piece, width)
+                    put(t0, j, back[j] + nt(dqkv[j * rows : (j + 1) * rows], w))
                     back_sum.send(j)
 
             grads = dqkv[...]
             value = tn(xf_ref[...].reshape(length, width), grads).astype(BF)
-            put_grad(OUT_CHUNKS + HEAD_CHUNKS * h, HEAD_CHUNKS, value)
+            put_grad(FF_CHUNKS + OUT_CHUNKS + HEAD_CHUNKS * h, HEAD_CHUNKS, value)
             qb[h] = total(grads.astype(F32))
-
-    groups = [(FF_CHUNKS, OUT_CHUNKS)]
-    groups += [
-        (FF_CHUNKS + OUT_CHUNKS + HEAD_CHUNKS * h, HEAD_CHUNKS) for h in range(heads)
-    ]
-    reached = [0]
-
-    def line(upto):
-        line_to(reached[0], upto)
-        reached[0] = upto
 
     def forward_hidden():
         for b in range(nc):
@@ -862,55 +840,53 @@
     def hand(k):
         share_g.forward(order[k], k)
 
+    start(2)
+    line(5)
     events = {
-        0: lambda: line(1),
-        2: lambda: line(2),
-        3: lambda: line(3),
-        5: lambda: (line(4), forward_hidden(), line_start(*groups[0])),
-        7: lambda: line(5),
-        8: lambda: line(6),
-        9: lambda: line_start(*groups[1]),
-        10: lambda: line(7),
-        11: lambda: line(8),
+        0: lambda: line(6),
+        1: lambda: line(7),
+        3: lambda: (forward_hidden(), start(3), line(8)),
+        5: lambda: line(9),
+        6: lambda: line(10),
+        7: lambda: line(11),
+        8: lambda: line(12),
+        9: lambda: start(4),
+        10: lambda: line(13),
+        11: lambda: line(14),
     }
 
     def slot(i, carry):
         attend_step(i)
-        for when, action in events.items():
-
-            @pl.when(i == when)
-            def _(action=action):
-                action()
-
+        run_at(i, events)
         return carry
 
     lax.fori_loop(0, steps, slot, 0)
     for b in range(nc):
         back_sum.across(b)
     small_zero()
-    line_start(*groups[2])
-    line(9)
+    start(5)
+    line(15)
     grad_own(0)
-    line(10)
     grad_own(1)
-    line(11)
+    line(16)
     grad_own(2)
     small_one()
-    line(12)
+    line(17)
     grad_own(3)
-    line_start(*groups[3])
-    line(13)
+    start(6)
+    line(18)
     small_two()
-    line(14)
     grad_share(0)
     grad_share(1)
-    line(15)
+    line(19)
+    start(7)
     grad_share(2)
     hand(0)
+    line(20)
     grad_share(3)
     hand(1)
     small_three()
-    line(16)
+    line(21)
     hand(2)
     hand(3)
     small_four()
@@ -923,16 +899,24 @@
     keep.wait()
     for lo, n in groups:
         for r in range(ns - 1):
-            x_send(lo - FF_CHUNKS, n, r).wait_send()
+            x_send(lo, n, r).wait_send()
     for b in range(nc):
-        back_sum.drain(b)
-        share_h.drain(b, b, hid_ref.at[b])
+        for i in range(1, 4):
+            sums[i].drain(b)
+        for i in range(3):
+            shares[i].drain(b, b)
+        share_h.drain(b, b, hid.at[b])
         share_g.drain(order[b], b)
 
         @pl.when(b != p.c)
         def _(b=b):
             grad_send(b).wait_send()
 
+    for a in range(2):
+        for r in range(ns - 1):
+            weight(a, r).wait_send()
+    for k in range(nc - 1):
+        og_send(k).wait_send()
     small_tp(0, p.mate).wait_send()
     small_tp(1, p.ymate).wait_send()
     for k in range(nc - 1):
@@ -953,8 +937,8 @@
         def wide(lo, n):
             return jnp.concatenate([dw_ref[lo + j].astype(F32) for j in range(n)], axis=1)
 
-        uw_ref[...] = wide(0, 6)
-        dn_ref[...] = wide(6, 6).T
+        uw_ref[...] = wide(6, 6)
+        dn_ref[...] = wide(0, 6).T
         heads = qb_ref.shape[1] // HEAD
         ow_ref[...] = wide(FF_CHUNKS, OUT_CHUNKS)[:, : heads * HEAD].T
         first = FF_CHUNKS + OUT_CHUNKS
@@ -1112,18 +1096,25 @@
         own,
     ]
     rows_ff = pltpu.VMEM((nc, local_len, ff), BF)
-    ga, hid, gfi, dff, small = pl.pallas_call(
-        functools.partial(feed_kernel, ns, nc),
+    total_chunks = line[0]
+    chunks = pltpu.VMEM(line, BF)
+    wide_small = heads * 384
+    hbm = [pl.BlockSpec(memory_space=pl.ANY)]
+    ing, hid, dw, small = pl.pallas_call(
+        functools.partial(layer_kernel, ns, nc),
         out_shape=(
             struct((nc, 4, piece, width), BF),
-            struct((nc, piece, width), BF),
-            struct((nc, piece, width), F32),
-            struct((FF_CHUNKS, shard_rows, 128), BF),
-            struct((8, width), F32),
+            struct((nc, 4, piece, width), BF),
+            struct(line, BF),
+            struct((8, wide_small), F32),
         ),
-        in_specs=vmem(13),
-        out_specs=vmem(5),
+        in_specs=vmem(3) + hbm * 3 + vmem(12) + hbm,
+        out_specs=vmem(4),
         scratch_shapes=[
+            full,
+            own,
+            own32,
+            pltpu.VMEM((8, width), F32),
             pltpu.VMEM((ns, shard_rows, ff), BF),
             pltpu.VMEM((ns, shard_rows, ff), BF),
             own,
@@ -1140,19 +1131,40 @@
             own32,
             pltpu.VMEM((nc, piece, 1), F32),
             own32,
-            pltpu.VMEM((2, ns, shard_rows, ff), BF),
-            pltpu.VMEM((2, wide, shard_rows, ff), BF),
+            pltpu.VMEM((heads, length, 128), BF),
+            pltpu.VMEM((length, 128), BF),
+            pltpu.VMEM((length, 128), F32),
+            pltpu.VMEM((length, 128), F32),
+            pltpu.VMEM((length, 384), BF),
+            pltpu.VMEM((heads, 1, 384), F32),
+            pltpu.VMEM((2, length, local_len), BF),
+            pltpu.VMEM((total_chunks, ns, shard_rows, 128), BF),
+            own,
         ]
-        + [DMA((4,))]
+        + [chunks] * 3
+        + [
+            pltpu.VMEM((wide, total_chunks, shard_rows, 128), BF),
+            pltpu.VMEM((4, 8, wide_small), F32),
+            pltpu.VMEM((nc, 8, wide_small), F32),
+            pltpu.VMEM((ns, 8, wide_small), F32),
+            DMA((6,)),
+        ]
         + [DMA((2, wide))] * 2
         + [DMA((nc - 1,))] * 2
         + [DMA((nc,))] * 2
-        + [DMA((2, wide))] * 2
-        + [DMA((3, nc))] * (TP_REDUCE + TP_GATHER),
+        + [DMA((2,))]
+        + [DMA((total_chunks, wide))] * 2
+        + [DMA((total_chunks,))] * 8
+        + [DMA((nc,))] * 2
+        + [DMA((2,))] * 2
+        + [DMA((nc - 1,))] * 2
+        + [DMA((wide,))] * 2
+        + [DMA((4, nc))] * TP_REDUCE
+        + [DMA((5, nc))] * TP_GATHER,
         compiler_params=params(1),
-        name="feed",
+        name="layer",
     )(
-        ctx.reshape(nc, local_len, heads * 128),
+        ctx,
         wo,
         xf,
         out_grad,
@@ -1165,54 +1177,13 @@
         down_bias,
         norm2_gain,
         norm2_bias,
+        wf,
+        code,
+        inv,
+        q,
+        kv,
+        e,
     )
-
-    chunks = pltpu.VMEM(line, BF)
-    wide_small = heads * 384
-    ing, hid, dw, small = pl.pallas_call(
-        functools.partial(back_kernel, ns, nc),
-        out_shape=(
-            struct((nc, 4, piece, width), BF),
-            struct((nc, 4, piece, width), BF),
-            struct(line, BF),
-            struct((8, wide_small), F32),
-        ),
-        in_specs=vmem(13) + [pl.BlockSpec(memory_space=pl.ANY)],
-        out_specs=vmem(4),
-        scratch_shapes=[
-            pltpu.VMEM((heads, length, 128), BF),
-            pltpu.VMEM((length, 128), BF),
-            pltpu.VMEM((length, 128), F32),
-            pltpu.VMEM((length, 128), F32),
-            pltpu.VMEM((length, 384), BF),
-            pltpu.VMEM((length, width), F32),
-            pltpu.VMEM((heads, 1, 384), F32),
-            pltpu.VMEM((2, length, local_len), BF),
-            pltpu.VMEM((mixed, ns, shard_rows, 128), BF),
-        ]
-        + reduce_bufs
-        + [own]
-        + [chunks] * 4
-        + [
-            pltpu.VMEM((wide, mixed, shard_rows, 128), BF),
-            pltpu.VMEM((4, 8, wide_small), F32),
-            pltpu.VMEM((nc, 8, wide_small), F32),
-            pltpu.VMEM((ns, 8, wide_small), F32),
-            DMA((1,)),
-            DMA((2,)),
-        ]
-        + [DMA((mixed, wide))] * 2
-        + [DMA((FF_CHUNKS + mixed,))] * 8
-        + [DMA((nc,))] * 2
-        + [DMA((1,))]
-        + [DMA((2,))] * 2
-        + [DMA((nc - 1,))] * 2
-        + [DMA((wide,))] * 2
-        + [DMA((nc,))] * TP_REDUCE
-        + [DMA((2, nc))] * TP_GATHER,
-        compiler_params=params(2),
-        name="back",
-    )(ga, wf, wo, ctx, xf, code, inv, q, kv, gfi, hid, dff, small, e)
 
     def block(*shape):
         return pl.BlockSpec(shape, lambda i: (i,) + (0,) * (len(shape) - 1))

time: 248 us -> 215 us (0.87)
  Pallas kernels: 247 us -> 213 us
    pallas_call x2 -> x1, Pallas kernels: 187 us -> 154 us  [per_device(): pl.pallas_call(functools.partial(layer_kernel, ns, nc), out_shape=(struct...]
where the time goes in v3:
time: 215 us; the launch traced here: 214 us
  Pallas kernels  213 us (99%)
    pallas_call x1, Pallas kernels, per_device(): pl.pallas_call(functools.partial(layer_kernel, ns, nc), out_shape=(struct...  154 us
    pallas_call x1, Pallas kernels, per_device(): pl.pallas_call(functools.partial(project_kernel, ns, nc), out_shape=(stru...  37.3 us
    pallas_call x1, Pallas kernels, per_device(): pl.pallas_call(attend_kernel, grid=grid, out_shape=(struct((heads * nc, l...  14.6 us
    pallas_call x1, Pallas kernels, per_device(): pl.pallas_call(deliver_kernel, grid=(nc,), out_shape=(struct((nc, local_l...  7.45 us

profile of v3, /device:TPU:0, one launch (start us, length us, event | category | flops | bytes accessed | tf_op | source)
XLA Modules:
  0.0 214.0 jit_solution(838945670670785108)
XLA Ops:
  0.6 37.3 %project.1 = (bf16[4,4,64,768]{3,2,1,0:T(8,128)(2,1)}, bf16[3,1024,128]{2,1,0:T(8,128)(2,1)}, bf16[3,1024,128]{2,1,0:T(8,128)(2,1)}, f32[4,1,256]{2,1,0:T(1,128)...) custom-call(bf16[4,256,768]{2,1,0:T(8,128)(2,1)} %x_ref.1, ...), custom_call_target="tpu_custom_call" | custom-call | tf_op jit(solution)/shard_map/project/pallas_call | solution.py:1024
  38.0 14.6 %attend.1 = (bf16[12,1024,256]{2,1,0:T(8,128)(2,1)}, bf16[1024,384]{1,0:T(8,128)(2,1)}, f32[12,1,256]{2,1,0:T(1,128)}) custom-call(bf16[3,1024,128]{2,1,0:T(8,128)(2,1)} %get-tuple-element.46.q_ref.rest_10_, bf16[3,1024,128]{2,1,0:T(8,128)(2,1)} %get-tuple-element.47.kv_ref.rest_11_, f32[4,1,256]{2,1,0:T(1,128)} %get-tuple-element.48.code_ref.rest_8_), custom_call_target="tpu_custom_call" | custom-call | tf_op jit(solution)/shard_map/attend/pallas_call | solution.py:1070
  52.6 153.8 %layer.1 = (bf16[4,4,64,768]{3,2,1,0:T(8,128)(2,1)}, bf16[4,4,64,768]{3,2,1,0:T(8,128)(2,1)}, bf16[23,384,128]{2,1,0:T(8,128)(2,1)}, f32[8,1152]{1,0:T(8,128)}) custom-call(bf16[1024,384]{1,0:T(8,128)(2,1)} %get-tuple-element.49.ctx_ref, bf16[2,384,384]{2,1,0:T(8,128)(2,1)} %get-tuple-element.50.wo_ref, bf16[4,4,64,768]{3,2,1,0:T(8,128)(2,1)} %get-tuple-element.51.xf_ref, ...), custom_call_target="tpu_custom_call" | custom-call | tf_op jit(solution)/shard_map/layer/pallas_call | solution.py:1103
  206.4 7.4 %deliver.1 = (bf16[4,256,768]{2,1,0:T(8,128)(2,1)}, f32[4,256,768]{2,1,0:T(8,128)}, f32[4,192,384]{2,1,0:T(8,128)}, f32[2,192,384]{2,1,0:T(8,128)}, f32[4,192]{1...) custom-call(bf16[4,256,768]{2,1,0:T(8,128)(2,1)} %bitcast.6, ...), custom_call_target="tpu_custom_call" | custom-call | tf_op jit(solution)/shard_map/deliver/pallas_call | solution.py:1214

commit v4 on v3

--- a/solution.py
+++ b/solution.py
@@ -164,9 +164,10 @@
 
 
 def project_kernel(
-    ns, nc, x_ref, type_ref, seg_ref, qw_ref, kvw_ref, ow_ref, dn_ref, qb_ref, vb_ref,
-    xf_ref, q_ref, kv_ref, codef_ref, wf_ref, wo_ref, dnt_ref,
-    wst, code, bias, local, zs, zr, ds, dr, ws, wr, *tp_sems,
+    ns, nc, x_ref, type_ref, seg_ref, qw_ref, kvw_ref, ow_ref, dn_ref, qb_ref, vb_ref, wu_ref,
+    xf_ref, q_ref, kv_ref, codef_ref, wf_ref, wo_ref, dnt_ref, wuf_ref, ctx_ref, inv_ref, e_ref,
+    wst, code, bias, kcat, vt, segcol, ebuf,
+    local, zs, zr, ds, dr, ws, wr, us, ur, es, *tp_sems,
 ):
     p = Place(ns, nc)
     piece = x_ref.shape[1] // 4
@@ -188,7 +189,7 @@
         return remote(code.at[peer["ctx"]], codef_ref.at[p.c], ds.at[k], dr.at[k], peer)
 
     def gathered(h, src):
-        return wf_ref.at[h, src] if h < heads else wo_ref.at[src]
+        return wo_ref.at[src] if isinstance(h, int) and h == heads else wf_ref.at[h, src]
 
     def weight(h, r):
         return remote(wst.at[h], gathered(h, p.s), ws.at[h, r], wr.at[h, r], p.xpeers[r])
@@ -217,6 +218,12 @@
     wst[heads] = jnp.concatenate(parts, axis=1)
     for r in range(ns - 1):
         weight(heads, r).start()
+
+    def up_send(r):
+        return remote(wu_ref, wuf_ref.at[p.s], us.at[r], ur.at[r], p.xpeers[r])
+
+    for r in range(ns - 1):
+        up_send(r).start()
     for k in range(nc - 1):
         code_send(k).start()
     copies = [
@@ -224,6 +231,7 @@
         pltpu.make_async_copy(code.at[p.c], codef_ref.at[p.c], local.at[1]),
         pltpu.make_async_copy(wst.at[pl.ds(0, heads)], wf_ref.at[:, p.s], local.at[2]),
         pltpu.make_async_copy(wst.at[heads], wo_ref.at[p.s], local.at[3]),
+        pltpu.make_async_copy(wu_ref, wuf_ref.at[p.s], local.at[4]),
     ]
     for copy in copies:
         copy.start()
@@ -249,7 +257,17 @@
         copy.wait()
     width = xf_ref.shape[-1]
     rows = 4 * piece
-    for h in range(heads):
+    length = nc * rows
+    for j in range(nc):
+        col = jnp.abs(column(codef_ref[j]))
+        segcol[j * rows : (j + 1) * rows] = jnp.where(col == 0.0, -1.0, col)
+    low_half = lax.broadcasted_iota(jnp.int32, (rows, 128), 1) < HEAD
+
+    def e_out(i):
+        slot = lax.rem(i, 2)
+        return pltpu.make_async_copy(ebuf.at[slot], e_ref.at[i], es.at[slot])
+
+    def head_step(h, carry):
         weight_landed(h)
 
         def project(b, carry):
@@ -259,14 +277,56 @@
             at = pl.ds(pl.multiple_of(b * rows, rows), rows)
             chosen = jnp.where(entity, out[:, 128:256], out[:, 0:128])
             q_ref[h, at] = (chosen * HEAD ** (-0.5)).astype(BF)
-            kv_ref[h, at] = out[:, 256:384].astype(BF)
+            kv = out[:, 256:384].astype(BF)
+            kv_ref[h, at] = kv
+            kv = kv.astype(F32)
+            turned = pltpu.roll(kv, HEAD, 1)
+            keep = jnp.where(low_half, kv, turned)
+            kcat[at] = jnp.where(low_half == entity, 0.0, keep).astype(BF)
+            vt[:, at] = jnp.where(low_half, 0.0, kv).T.astype(BF)
             return carry
 
         lax.fori_loop(0, nc, project, 0)
+
+        def attend(b, carry):
+            i = h * nc + b
+            at = pl.ds(pl.multiple_of(b * rows, rows), rows)
+            scores = nt(kcat[...], q_ref[h, at])
+            segment = jnp.abs(codef_ref[b])
+            allowed = jnp.concatenate([segcol[...]] * (rows // 128), axis=1) == segment
+            scores = jnp.where(allowed, scores, MASKED)
+            top = jnp.max(scores, axis=0, keepdims=True)
+            top = jnp.where(top == MASKED, 0.0, top)
+            exponent = jnp.exp(scores - top)
+            inverse = 1.0 / jnp.maximum(jnp.sum(exponent, axis=0, keepdims=True), 1.0)
+            exponent = exponent.astype(BF)
+
+            @pl.when(i >= 2)
+            def _():
+                e_out(i - 2).wait()
+
+            ebuf[lax.rem(i, 2)] = exponent
+            e_out(i).start()
+            inv_ref[i] = inverse
+            lanes = pl.ds(pl.multiple_of(h * 128, 128), 128)
+            ctx_ref[at, lanes] = (nn(vt[...], exponent) * inverse).T.astype(BF)
+            return carry
+
+        lax.fori_loop(0, nc, attend, 0)
+        return carry
+
+    lax.fori_loop(0, heads, head_step, 0)
+    for i in range(heads * nc - 2, heads * nc):
+        e_out(i).wait()
+    for r in range(ns - 1):
+        landed = wuf_ref.at[lax.rem(p.s + ns - 1 - r, ns)]
+        remote(landed, landed, us.at[r], ur.at[r], p.xpeers[r]).wait_recv()
     weight_landed(heads)
     for h in range(heads + 1):
         for r in range(ns - 1):
             weight(h, r).wait_send()
+    for r in range(ns - 1):
+        up_send(r).wait_send()
     for k in range(nc - 1):
         x_send(k).wait_send()
         code_send(k).wait_send()
@@ -275,44 +335,6 @@
         gather.drain(blocks[k], k)
 
 
-def attend_kernel(q_ref, kv_ref, code_ref, e_ref, ctx_ref, inv_ref, kcat, vt, segcol):
-    h, b = pl.program_id(0), pl.program_id(1)
-    length = kv_ref.shape[1]
-    nblk, rows = code_ref.shape[0], code_ref.shape[2]
-
-    @pl.when((h == 0) & (b == 0))
-    def _():
-        for j in range(nblk):
-            col = jnp.abs(column(code_ref[j]))
-            segcol[j * rows : (j + 1) * rows] = jnp.where(col == 0.0, -1.0, col)
-
-    @pl.when(b == 0)
-    def _():
-        low_half = lax.broadcasted_iota(jnp.int32, (rows, 128), 1) < HEAD
-        for j in range(nblk):
-            at = slice(j * rows, (j + 1) * rows)
-            entity = column(code_ref[j]) < 0.0
-            kv = kv_ref[0, at].astype(F32)
-            turned = pltpu.roll(kv, HEAD, 1)
-            keep = jnp.where(low_half, kv, turned)
-            kcat[at] = jnp.where(low_half == entity, 0.0, keep).astype(BF)
-            vt[:, at] = jnp.where(low_half, 0.0, kv).T.astype(BF)
-
-    scores = nt(kcat[...], q_ref[0])
-    segment = jnp.abs(code_ref[b])
-    col = segcol[...]
-    allowed = jnp.concatenate([col] * (rows // 128), axis=1) == segment
-    scores = jnp.where(allowed, scores, MASKED)
-    top = jnp.max(scores, axis=0, keepdims=True)
-    top = jnp.where(top == MASKED, 0.0, top)
-    exponent = jnp.exp(scores - top)
-    inverse = 1.0 / jnp.maximum(jnp.sum(exponent, axis=0, keepdims=True), 1.0)
-    exponent = exponent.astype(BF)
-    e_ref[0] = exponent
-    inv_ref[0] = inverse
-    ctx_ref[...] = (nn(vt[...], exponent) * inverse).T.astype(BF)
-
-
 def spread(values):
     average = jnp.mean(values, axis=-1, keepdims=True)
     centred = values - average
@@ -335,18 +357,20 @@
 FF_CHUNKS = 12
 OUT_CHUNKS = 2
 HEAD_CHUNKS = 3
-OWN_LAG, PASS_LAG = 3, 6
+FIRST_SUM, CHUNK, HOP = -30.0, 2.1, 5.5
+STEP_ENDS = (-29.0, -25.0, -22.0, -20.0)
+BACK_START, BACK_STEP = -17.0, 1.42
 
 
 def layer_kernel(
-    ns, nc, ctx_ref, wo_ref, xf_ref, og_ref, wu_ref, wd_ref, *rest,
+    ns, nc, ctx_ref, wo_ref, xf_ref, wuf, og_ref, wd_ref, *rest,
 ):
     vecs, rest = rest[:7], rest[7:]
     (
         wf_ref, code_ref, inv_ref, q_ref, kv_ref, e_ref,
         ing_ref, hidf_ref, dw_ref, sm_ref,
         ga, hid, gfi, small,
-        wuf, wdf, ogo, hsend,
+        wdf, ogo, hsend,
         t0, m0, s0, y0, t1, m1, s1, y1, t2, m2, s2, y2,
         low, gf, active, slope, gup, fo, fh, fi, gs,
         dctx, kcat, dkey, dval, dqkv, qb, ebuf, dqo,
@@ -369,15 +393,12 @@
 
     fetch(0).start()
     greet([p.mate, p.ymate] + p.zpeers + p.xpeers)
-    weights = ((wu_ref, wuf), (wd_ref, wdf))
-
-    def weight(a, r):
-        src, dst = weights[a]
-        return remote(src, dst.at[p.s], ws.at[a, r], wr.at[a, r], p.xpeers[r])
-
-    for a in range(2):
-        for r in range(ns - 1):
-            weight(a, r).start()
+
+    def down_send(r):
+        return remote(wd_ref, wdf.at[p.s], ws.at[r], wr.at[r], p.xpeers[r])
+
+    for r in range(ns - 1):
+        down_send(r).start()
     mine = pl.ds(p.t * piece, piece)
 
     def og_send(k):
@@ -388,8 +409,7 @@
         og_send(k).start()
     copies = [
         pltpu.make_async_copy(og_ref.at[p.c, mine], ogo.at[p.c], local.at[0]),
-        pltpu.make_async_copy(wu_ref, wuf.at[p.s], local.at[1]),
-        pltpu.make_async_copy(wd_ref, wdf.at[p.s], local.at[2]),
+        pltpu.make_async_copy(wd_ref, wdf.at[p.s], local.at[1]),
     ]
     for copy in copies:
         copy.start()
@@ -411,15 +431,9 @@
     )
 
 
-    def x_send(lo, n, r):
+    def x_send(k, r):
         peer = p.xpeers[r]
-        return remote(
-            dqo.at[pl.ds(lo, n), peer["shard"]],
-            xr.at[r, pl.ds(lo, n)],
-            xs.at[lo, r],
-            xrs.at[lo, r],
-            peer,
-        )
+        return remote(dqo.at[k, peer["shard"]], xr.at[r, k], xs.at[k, r], xrs.at[k, r], peer)
 
     outer = (p.c == 0) | (p.c == nc - 1)
     inner = (p.c > 0) & (p.c < nc - 1)
@@ -442,29 +456,29 @@
     def owns(k):
         return lax.rem(k + p.c, 2) == 1
 
-    def line_start(lo, n):
+    def line_start(k):
+        grad = dqo[k, p.s].astype(F32)
         for r in range(ns - 1):
-            x_send(lo, n, r).wait_recv()
-        for k in range(lo, lo + n):
-            grad = dqo[k, p.s].astype(F32)
-            for r in range(ns - 1):
-                grad = grad + xr[r, k].astype(F32)
-            zo[k] = grad.astype(BF)
-
-            @pl.when(outer)
-            def _(k=k):
-                to_inner(k).start()
+            x_send(k, r).wait_recv()
+            grad = grad + xr[r, k].astype(F32)
+        zo[k] = grad.astype(BF)
+
+        @pl.when(outer)
+        def _():
+            to_inner(k).start()
 
     def line_in(k):
-        to_inner(k).wait_recv()
-
-        @pl.when(jnp.logical_not(owns(k)))
+        @pl.when(inner)
+        def _():
+            to_inner(k).wait_recv()
+
+        @pl.when(inner & jnp.logical_not(owns(k)))
         def _():
             zq[k] = (zo[k].astype(F32) + zr[k].astype(F32)).astype(BF)
             to_owner(k).start()
 
     def line_own(k):
-        @pl.when(owns(k))
+        @pl.when(inner & owns(k))
         def _():
             to_owner(k).wait_recv()
             dw_ref[k] = (zo[k].astype(F32) + zr[k].astype(F32) + zq[k].astype(F32)).astype(BF)
@@ -472,26 +486,23 @@
             to_outer(k).start()
 
     def line_pass(k):
-        @pl.when(jnp.logical_not(owns(k)))
+        @pl.when(inner & jnp.logical_not(owns(k)))
         def _():
             to_other(k).wait_recv()
             to_outer(k).start()
 
-    reached = [0]
-
-    def line(upto):
-        lo = reached[0]
-        reached[0] = upto
-
-        @pl.when(inner)
-        def _():
-            for k in range(lo, upto):
-                if k < chunks:
-                    line_in(k)
-                if 0 <= k - OWN_LAG < chunks:
-                    line_own(k - OWN_LAG)
-                if 0 <= k - PASS_LAG < chunks:
-                    line_pass(k - PASS_LAG)
+    plan = []
+    for k in range(chunks):
+        for hop, action in enumerate((line_start, line_in, line_own, line_pass)):
+            plan.append((FIRST_SUM + CHUNK * k + HOP * hop, functools.partial(action, k)))
+
+    def due(after, until):
+        stretch = [entry for entry in plan if after < entry[0] <= until]
+        return [action for _, action in sorted(stretch, key=lambda entry: entry[0])]
+
+    def run(actions):
+        for action in actions:
+            action()
 
     def line_end(k):
         @pl.when(outer)
@@ -514,14 +525,11 @@
     sizes = [HEAD_CHUNKS] * 4 + [OUT_CHUNKS] + [HEAD_CHUNKS] * heads
     groups = [(sum(sizes[:g]), n) for g, n in enumerate(sizes)]
 
-    def start(g):
-        line_start(*groups[g])
-
     def put_grad(lo, n, value):
         for j in range(n):
             dqo[lo + j] = value[:, j * 128 : (j + 1) * 128].reshape(dqo.shape[1:])
-        for r in range(ns - 1):
-            x_send(lo, n, r).start()
+            for r in range(ns - 1):
+                x_send(lo + j, r).start()
 
 
     def put(terms, b, values):
@@ -548,22 +556,21 @@
         shares[0].send(b, b)
 
     def feed_forward(b):
-        @pl.when(b == 0)
-        def _():
-            for a in range(2):
-                for r in range(ns - 1):
-                    landed = weights[a][1].at[lax.rem(p.s + ns - 1 - r, ns)]
-                    remote(landed, landed, ws.at[a, r], wr.at[a, r], p.xpeers[r]).wait_recv()
-            for copy in copies[1:]:
-                copy.wait()
-
         shares[0].arrive(b, b)
         up = nn(low[b].reshape(rows, width), wuf[...].reshape(width, -1)) + up_bias
         cdf = 0.5 * (1.0 + lax.erf(up * ROOT_HALF))
         act = (up * cdf).astype(BF)
         active[b] = act
         slope[b] = cdf + up * (jnp.exp(-0.5 * up * up) * INV_ROOT_TWO_PI)
-        put(t1, b, nt(act, wdf[...].reshape(width, -1)))
+
+        @pl.when(b == 0)
+        def _():
+            for r in range(ns - 1):
+                landed = wdf.at[lax.rem(p.s + ns - 1 - r, ns)]
+                remote(landed, landed, ws.at[r], wr.at[r], p.xpeers[r]).wait_recv()
+            copies[1].wait()
+
+        put(t1, b, nt(active[b], wdf[...].reshape(width, -1)))
         sums[1].send(b)
 
     def hid_send(b):
@@ -649,14 +656,12 @@
                 action()
 
     full = SKEWS_C[8] + nc - 1
+    ends = (-100.0,) + STEP_ENDS
     feed_events = {
-        full: lambda: (weight_grad(0), weight_grad(1)),
-        full + 1: lambda: (weight_grad(2), weight_grad(3)),
-        full + 2: lambda: start(0),
-        full + 3: lambda: line(1),
-        full + 4: lambda: (start(1), line(3)),
-        full + 5: lambda: line(4),
+        full + 2 + j: functools.partial(run, due(ends[j], ends[j + 1])) for j in range(4)
     }
+    feed_events[full] = lambda: (weight_grad(0), weight_grad(1))
+    feed_events[full + 1] = lambda: (weight_grad(2), weight_grad(3))
 
     def feed_slot(step, carry):
         for skew, stage in zip(SKEWS_C, stages):
@@ -840,20 +845,10 @@
     def hand(k):
         share_g.forward(order[k], k)
 
-    start(2)
-    line(5)
-    events = {
-        0: lambda: line(6),
-        1: lambda: line(7),
-        3: lambda: (forward_hidden(), start(3), line(8)),
-        5: lambda: line(9),
-        6: lambda: line(10),
-        7: lambda: line(11),
-        8: lambda: line(12),
-        9: lambda: start(4),
-        10: lambda: line(13),
-        11: lambda: line(14),
-    }
+    run(due(STEP_ENDS[-1], BACK_START))
+    ends = [BACK_START + BACK_STEP * i for i in range(steps + 1)]
+    events = {i: functools.partial(run, due(ends[i], ends[i + 1])) for i in range(steps)}
+    events[3] = lambda: (forward_hidden(), run(due(ends[3], ends[4])))
 
     def slot(i, carry):
         attend_step(i)
@@ -862,44 +857,24 @@
 
     lax.fori_loop(0, steps, slot, 0)
     for b in range(nc):
-        back_sum.across(b)
-    small_zero()
-    start(5)
-    line(15)
-    grad_own(0)
-    grad_own(1)
-    line(16)
-    grad_own(2)
-    small_one()
-    line(17)
-    grad_own(3)
-    start(6)
-    line(18)
-    small_two()
-    grad_share(0)
-    grad_share(1)
-    line(19)
-    start(7)
-    grad_share(2)
-    hand(0)
-    line(20)
-    grad_share(3)
-    hand(1)
-    small_three()
-    line(21)
-    hand(2)
-    hand(3)
-    small_four()
-    line(chunks + PASS_LAG)
+        plan += [
+            (2.0 + 0.5 * b, functools.partial(back_sum.across, b)),
+            (6.5 + 2.0 * b, functools.partial(grad_own, b)),
+            (13.0 + 1.0 * b, functools.partial(grad_share, b)),
+            (18.0 + 2.0 * b, functools.partial(hand, b)),
+        ]
+    plan += [(3.8, small_zero), (7.0, small_one), (14.5, small_two), (19.5, small_three)]
+    plan += [(25.0, small_four)]
+    run(due(ends[-1], 1000.0))
     for b in range(nc):
         share_h.arrive(b, b)
         share_g.arrive(order[b], b)
     for k in range(chunks):
         line_end(k)
     keep.wait()
-    for lo, n in groups:
+    for k in range(chunks):
         for r in range(ns - 1):
-            x_send(lo, n, r).wait_send()
+            x_send(k, r).wait_send()
     for b in range(nc):
         for i in range(1, 4):
             sums[i].drain(b)
@@ -912,9 +887,8 @@
         def _(b=b):
             grad_send(b).wait_send()
 
-    for a in range(2):
-        for r in range(ns - 1):
-            weight(a, r).wait_send()
+    for r in range(ns - 1):
+        down_send(r).wait_send()
     for k in range(nc - 1):
         og_send(k).wait_send()
     small_tp(0, p.mate).wait_send()
@@ -974,11 +948,7 @@
     return jax.ShapeDtypeStruct(shape, dtype)
 
 
-def params(collective_id=None):
-    if collective_id is None:
-        return pltpu.CompilerParams(
-            vmem_limit_bytes=VMEM_LIMIT, dimension_semantics=("arbitrary", "arbitrary")
-        )
+def params(collective_id):
     return pltpu.CompilerParams(
         vmem_limit_bytes=VMEM_LIMIT, collective_id=collective_id, has_side_effects=True
     )
@@ -1021,7 +991,8 @@
 
     mixed = OUT_CHUNKS + HEAD_CHUNKS * heads
     line = (FF_CHUNKS + mixed, shard_rows, 128)
-    xf, q, kv, code, wf, wo, down_t = pl.pallas_call(
+    hbm = [pl.BlockSpec(memory_space=pl.ANY)]
+    xf, q, kv, code, wf, wo, down_t, wuf, ctx, inv, e = pl.pallas_call(
         functools.partial(project_kernel, ns, nc),
         out_shape=(
             struct((nc, 4, piece, width), BF),
@@ -1031,17 +1002,27 @@
             struct((heads, ns, shard_rows, 384), BF),
             struct((ns, shard_rows, 384), BF),
             struct((shard_rows, ff), BF),
+            struct((ns, shard_rows, ff), BF),
+            struct((length, heads * 128), BF),
+            struct((heads * nc, 1, local_len), F32),
+            struct((heads * nc, length, local_len), BF),
         ),
-        in_specs=vmem(9),
-        out_specs=vmem(7),
+        in_specs=vmem(9) + hbm,
+        out_specs=vmem(10) + hbm,
         scratch_shapes=[
             pltpu.VMEM((heads + 1, shard_rows, 384), BF),
             pltpu.VMEM((nc, 1, local_len), F32),
             pltpu.VMEM((heads, 1, 384), F32),
-            DMA((4,)),
+            pltpu.VMEM((length, 128), BF),
+            pltpu.VMEM((128, length), BF),
+            pltpu.VMEM((length, 128), F32),
+            pltpu.VMEM((2, length, local_len), BF),
+            DMA((5,)),
         ]
         + [DMA((nc - 1,))] * 4
         + [DMA((heads + 1, wide))] * 2
+        + [DMA((wide,))] * 2
+        + [DMA((2,))]
         + [DMA((nc,))] * TP_GATHER,
         compiler_params=params(0),
         name="project",
@@ -1055,36 +1036,8 @@
         down_weight,
         query_bias,
         value_bias,
+        up_weight,
     )
-
-    grid = (heads, nc)
-    e_spec = pl.BlockSpec((1, length, local_len), lambda h, b: (h * nc + b, 0, 0))
-    inv_spec = pl.BlockSpec((1, 1, local_len), lambda h, b: (h * nc + b, 0, 0))
-    ctx_spec = pl.BlockSpec((local_len, 128), lambda h, b: (b, h))
-    q_spec = pl.BlockSpec((1, local_len, 128), lambda h, b: (h, b, 0))
-    kv_spec = pl.BlockSpec((1, length, 128), lambda h, b: (h, 0, 0))
-
-    def whole(shape):
-        return pl.BlockSpec(shape, lambda h, b: (0,) * len(shape))
-
-    e, ctx, inv = pl.pallas_call(
-        attend_kernel,
-        grid=grid,
-        out_shape=(
-            struct((heads * nc, length, local_len), BF),
-            struct((length, heads * 128), BF),
-            struct((heads * nc, 1, local_len), F32),
-        ),
-        in_specs=[q_spec, kv_spec, whole((nc, 1, local_len))],
-        out_specs=(e_spec, ctx_spec, inv_spec),
-        scratch_shapes=[
-            pltpu.VMEM((length, 128), BF),
-            pltpu.VMEM((128, length), BF),
-            pltpu.VMEM((length, 128), F32),
-        ],
-        compiler_params=params(),
-        name="attend",
-    )(q, kv, code)
 
     full = pltpu.VMEM((nc, 4, piece, width), BF)
     own = pltpu.VMEM((nc, piece, width), BF)
@@ -1099,7 +1052,6 @@
     total_chunks = line[0]
     chunks = pltpu.VMEM(line, BF)
     wide_small = heads * 384
-    hbm = [pl.BlockSpec(memory_space=pl.ANY)]
     ing, hid, dw, small = pl.pallas_call(
         functools.partial(layer_kernel, ns, nc),
         out_shape=(
@@ -1108,14 +1060,13 @@
             struct(line, BF),
             struct((8, wide_small), F32),
         ),
-        in_specs=vmem(3) + hbm * 3 + vmem(12) + hbm,
+        in_specs=vmem(4) + hbm * 2 + vmem(12) + hbm,
         out_specs=vmem(4),
         scratch_shapes=[
             full,
             own,
             own32,
             pltpu.VMEM((8, width), F32),
-            pltpu.VMEM((ns, shard_rows, ff), BF),
             pltpu.VMEM((ns, shard_rows, ff), BF),
             own,
             own,
@@ -1149,7 +1100,7 @@
             pltpu.VMEM((ns, 8, wide_small), F32),
             DMA((6,)),
         ]
-        + [DMA((2, wide))] * 2
+        + [DMA((wide,))] * 2
         + [DMA((nc - 1,))] * 2
         + [DMA((nc,))] * 2
         + [DMA((2,))]
@@ -1167,8 +1118,8 @@
         ctx,
         wo,
         xf,
+        wuf,
         out_grad,
-        up_weight,
         down_t,
         out_bias,
         norm1_gain,

time: 215 us -> 204 us (0.949)
  Pallas kernels: 213 us -> 202 us
    pallas_call x1 -> x0, Pallas kernels: 14.6 us -> none  [per_device(): pl.pallas_call(attend_kernel, grid=grid, out_shape=(struct((heads * nc, l...]
    pallas_call x1, Pallas kernels: 37.3 us -> 50.6 us  [per_device(): pl.pallas_call(functools.partial(project_kernel, ns, nc), out_shape=(stru...]
    pallas_call x1, Pallas kernels: 154 us -> 144 us  [per_device(): pl.pallas_call(functools.partial(layer_kernel, ns, nc), out_shape=(struct...]
where the time goes in v4:
time: 204 us; the launch traced here: 203 us
  Pallas kernels  202 us (99%)
    pallas_call x1, Pallas kernels, per_device(): pl.pallas_call(functools.partial(layer_kernel, ns, nc), out_shape=(struct...  144 us
    pallas_call x1, Pallas kernels, per_device(): pl.pallas_call(functools.partial(project_kernel, ns, nc), out_shape=(stru...  50.6 us
    pallas_call x1, Pallas kernels, per_device(): pl.pallas_call(deliver_kernel, grid=(nc,), out_shape=(struct((nc, local_l...  7.45 us

profile of v4, /device:TPU:0, one launch (start us, length us, event | category | flops | bytes accessed | tf_op | source)
XLA Modules:
  0.0 203.3 jit_solution(14093806633818650063)
XLA Ops:
  0.6 50.6 %project.1 = (bf16[4,4,64,768]{3,2,1,0:T(8,128)(2,1)}, bf16[3,1024,128]{2,1,0:T(8,128)(2,1)}, bf16[3,1024,128]{2,1,0:T(8,128)(2,1)}, f32[4,1,256]{2,1,0:T(1,128)...) custom-call(bf16[4,256,768]{2,1,0:T(8,128)(2,1)} %x_ref.1, ...), custom_call_target="tpu_custom_call" | custom-call | tf_op jit(solution)/shard_map/project/pallas_call | solution.py:995
  51.3 144.4 %layer.1 = (bf16[4,4,64,768]{3,2,1,0:T(8,128)(2,1)}, bf16[4,4,64,768]{3,2,1,0:T(8,128)(2,1)}, bf16[23,384,128]{2,1,0:T(8,128)(2,1)}, f32[8,1152]{1,0:T(8,128)}) custom-call(bf16[1024,384]{1,0:T(8,128)(2,1)} %get-tuple-element.47.ctx_ref, bf16[2,384,384]{2,1,0:T(8,128)(2,1)} %get-tuple-element.48.wo_ref, bf16[4,4,64,768]{3,2,1,0:T(8,128)(2,1)} %get-tuple-element.49.xf_ref, ...), custom_call_target="tpu_custom_call" | custom-call | tf_op jit(solution)/shard_map/layer/pallas_call | solution.py:1055
  195.7 7.4 %deliver.1 = (bf16[4,256,768]{2,1,0:T(8,128)(2,1)}, f32[4,256,768]{2,1,0:T(8,128)}, f32[4,192,384]{2,1,0:T(8,128)}, f32[2,192,384]{2,1,0:T(8,128)}, f32[4,192]{1...) custom-call(bf16[4,256,768]{2,1,0:T(8,128)(2,1)} %bitcast.6, ...), custom_call_target="tpu_custom_call" | custom-call | tf_op jit(solution)/shard_map/deliver/pallas_call | solution.py:1165

commit v5 on v4

--- a/solution.py
+++ b/solution.py
@@ -353,7 +353,7 @@
     return jnp.sum(values, axis=0, keepdims=True)
 
 
-SKEWS_C = (0, 1, 3, 4, 5, 6, 8, 9, 10, 11, 13, 14, 15)
+SKEWS_C = (0, 1, 2, 3, 4, 5, 6, 7, 8, 9, 11, 12, 13)
 FF_CHUNKS = 12
 OUT_CHUNKS = 2
 HEAD_CHUNKS = 3

time: 204 us -> 202 us (level)
    pallas_call x1, Pallas kernels: 144 us -> 142 us  [per_device(): pl.pallas_call(functools.partial(layer_kernel, ns, nc), out_shape=(struct...]
where the time goes in v5:
time: 202 us; the launch traced here: 201 us
  Pallas kernels  200 us (99%)
    pallas_call x1, Pallas kernels, per_device(): pl.pallas_call(functools.partial(layer_kernel, ns, nc), out_shape=(struct...  142 us
    pallas_call x1, Pallas kernels, per_device(): pl.pallas_call(functools.partial(project_kernel, ns, nc), out_shape=(stru...  50.6 us
    pallas_call x1, Pallas kernels, per_device(): pl.pallas_call(deliver_kernel, grid=(nc,), out_shape=(struct((nc, local_l...  7.45 us

profile of v5, /device:TPU:0, one launch (start us, length us, event | category | flops | bytes accessed | tf_op | source)
XLA Modules:
  0.0 201.1 jit_solution(14807226894863635633)
XLA Ops:
  0.6 50.6 %project.1 = (bf16[4,4,64,768]{3,2,1,0:T(8,128)(2,1)}, bf16[3,1024,128]{2,1,0:T(8,128)(2,1)}, bf16[3,1024,128]{2,1,0:T(8,128)(2,1)}, f32[4,1,256]{2,1,0:T(1,128)...) custom-call(bf16[4,256,768]{2,1,0:T(8,128)(2,1)} %x_ref.1, ...), custom_call_target="tpu_custom_call" | custom-call | tf_op jit(solution)/shard_map/project/pallas_call | solution.py:995
  51.3 142.2 %layer.1 = (bf16[4,4,64,768]{3,2,1,0:T(8,128)(2,1)}, bf16[4,4,64,768]{3,2,1,0:T(8,128)(2,1)}, bf16[23,384,128]{2,1,0:T(8,128)(2,1)}, f32[8,1152]{1,0:T(8,128)}) custom-call(bf16[1024,384]{1,0:T(8,128)(2,1)} %get-tuple-element.47.ctx_ref, bf16[2,384,384]{2,1,0:T(8,128)(2,1)} %get-tuple-element.48.wo_ref, bf16[4,4,64,768]{3,2,1,0:T(8,128)(2,1)} %get-tuple-element.49.xf_ref, ...), custom_call_target="tpu_custom_call" | custom-call | tf_op jit(solution)/shard_map/layer/pallas_call | solution.py:1055
  193.5 7.4 %deliver.1 = (bf16[4,256,768]{2,1,0:T(8,128)(2,1)}, f32[4,256,768]{2,1,0:T(8,128)}, f32[4,192,384]{2,1,0:T(8,128)}, f32[2,192,384]{2,1,0:T(8,128)}, f32[4,192]{1...) custom-call(bf16[4,256,768]{2,1,0:T(8,128)(2,1)} %bitcast.6, ...), custom_call_target="tpu_custom_call" | custom-call | tf_op jit(solution)/shard_map/deliver/pallas_call | solution.py:1165
